TPU v7x, 32 devices: a whole 2x2x4 slice. The times are simulated.
32 devices in a mesh: dp: 16 (over z, y, x), tensor: 2 (over core).
Axes of the slice: x: 2, y: 2, z: 4, core: 2. Of those that a mesh axis runs over, the one named last changes fastest.
Arguments:
- features: bfloat16 [4096, 8192], P('dp', 'tensor'), may hold values from -6 to 6
- gate_pre: bfloat16 [4096, 14336], P('dp', 'tensor'), may hold values from -6 to 6
- up_pre: bfloat16 [4096, 14336], P('dp', 'tensor'), may hold values from -6 to 6
- grad_hidden: bfloat16 [4096, 14336], P('dp', 'tensor'), may hold values from -0.4375 to 0.4375
- blocks: int32 [32, 3], P('tensor'), may hold values from 0 to 63, as said below
- owner: int32 [32], P('tensor'), may hold values from 0 to 15, as said below
- weights: float32 [96, 128, 128], P(('dp', 'tensor')), may hold values from -0.4375 to 0.4375
- moment1: float32 [96, 128, 128], P(('dp', 'tensor')), may hold values from -6 to 6
- moment2: float32 [96, 128, 128], P(('dp', 'tensor')), may hold values from 0.05 to 2
Outputs:
- new_weights: float32 [96, 128, 128], P(('dp', 'tensor'))
- new_moment1: float32 [96, 128, 128], P(('dp', 'tensor'))
- new_moment2: float32 [96, 128, 128], P(('dp', 'tensor'))
Inputs may be any that keep to these rules, and one draw needn't show every extreme that they name: Each row is (matrix, row block, column block): matrix 0 is the gate and 1 the up projection, row block below 64, column block below 56 and counted within the tensor index's own columns. The rows of one tensor index's list are distinct; columns hold unequal numbers of blocks. `owner`: in each tensor index's list no index of dp owns more than 3 blocks, and some index of dp owns exactly 3.
All inputs are finite; a program needn't handle non-finite values.
Results may differ from a plain program's by a relative error of at most 0.0028.
Values may be sent and summed in bfloat16 or wider, within the bound.
No kernel may reach another device: no remote copies, remote signals or barrier semaphores. Data moves between devices by JAX's collectives and lax.ppermute only.
A program may use at most 128 MiB of HBM per device.

v0:
```python
import jax
import jax.numpy as jnp
from jax import lax
from jax.sharding import PartitionSpec as P

beta_first = 0.9
beta_second = 0.999
learn_rate = 0.01
epsilon = 1e-08
bias_first = 1.0 - 0.9**10
bias_second = 1.0 - 0.999**10


def local(features, gate_pre, up_pre, grad_hidden, blocks, owner, weights, moment1, moment2):
    block_size = weights.shape[-1]
    capacity = weights.shape[0]
    replicas = lax.axis_size("dp")
    listed = owner.shape[0]
    gathered = lax.all_gather(features, "tensor", axis=1, tiled=True)
    tokens = gathered.shape[0]
    column_blocks = gate_pre.shape[1] // block_size
    gate_value = gate_pre.astype(jnp.float32)
    cotangent = grad_hidden.astype(jnp.float32)
    sigmoid_gate = jax.nn.sigmoid(gate_value)
    grad_up = (cotangent * (gate_value * sigmoid_gate)).astype(jnp.bfloat16)
    grad_gate = (
        cotangent
        * up_pre.astype(jnp.float32)
        * (sigmoid_gate * (1.0 + gate_value * (1.0 - sigmoid_gate)))
    ).astype(jnp.bfloat16)
    row_cells = gathered.reshape(tokens, -1, block_size)
    chosen_rows = jnp.take(row_cells, blocks[:, 1], axis=1)
    activations = jnp.concatenate(
        [
            grad_gate.reshape(tokens, column_blocks, block_size),
            grad_up.reshape(tokens, column_blocks, block_size),
        ],
        axis=1,
    )
    chosen_cols = jnp.take(activations, blocks[:, 0] * column_blocks + blocks[:, 2], axis=1)
    partial_value = jnp.einsum(
        "tbi,tbj->bij", chosen_rows, chosen_cols, preferred_element_type=jnp.float32
    )
    earlier = lax.broadcasted_iota(jnp.int32, (listed, listed), 1) < lax.broadcasted_iota(
        jnp.int32, (listed, listed), 0
    )
    slot_rank = jnp.sum(((owner[:, None] == owner[None, :]) & earlier).astype(jnp.int32), axis=1)
    owner_index = lax.axis_index("dp")
    target = owner * capacity + slot_rank
    outgoing = (
        jnp.zeros((replicas * capacity, block_size, block_size), jnp.float32)
        .at[target]
        .set(partial_value)
    )
    incoming = lax.all_to_all(
        outgoing.astype(jnp.bfloat16), "dp", split_axis=0, concat_axis=0, tiled=True
    ).astype(outgoing.dtype)
    block_grad = jnp.sum(incoming.reshape(replicas, capacity, block_size, block_size), axis=0)
    held_count = jnp.sum((owner == owner_index).astype(jnp.int32))
    is_valid = (jnp.arange(capacity, dtype=jnp.int32) < held_count)[:, None, None]
    first_new = beta_first * moment1 + (1.0 - beta_first) * block_grad
    second_new = beta_second * moment2 + (1.0 - beta_second) * block_grad * block_grad
    weight_new = weights - learn_rate * (first_new / bias_first) / (
        jnp.sqrt(second_new / bias_second) + epsilon
    )
    return (
        jnp.where(is_valid, weight_new, weights),
        jnp.where(is_valid, first_new, moment1),
        jnp.where(is_valid, second_new, moment2),
    )


def solution(mesh):
    placed = (
        P("dp", "tensor"),
        P("dp", "tensor"),
        P("dp", "tensor"),
        P("dp", "tensor"),
        P("tensor", None),
        P("tensor"),
        P(("dp", "tensor"), None, None),
        P(("dp", "tensor"), None, None),
        P(("dp", "tensor"), None, None),
    )
    return jax.shard_map(
        local,
        mesh=mesh,
        in_specs=placed,
        out_specs=(
            P(("dp", "tensor"), None, None),
            P(("dp", "tensor"), None, None),
            P(("dp", "tensor"), None, None),
        ),
        check_vma=False,
    )
```

profile of v0, /device:TPU:12, one launch (start us, length us, event | category | flops | bytes accessed | tf_op | source)
XLA Modules:
  0.0 128.7 jit_solution(11040340028689193413)
XLA Ops:
  7.2 0.0 all-gather.2.cloned.1.call-start
  7.2 4.1 %copy.22 = bf16[256,4096]{0,1:T(8,128)(2,1)} copy(bf16[256,4096]{1,0:T(8,128)(2,1)} %param.9) | data formatting | bytes 4194304 | tf_op args[0]
  11.3 0.0 all-gather.2.cloned.1.call-update
  11.3 5.9 %copy.24 = bf16[256,7168]{0,1:T(8,128)(2,1)} copy(bf16[256,7168]{1,0:T(8,128)(2,1)} %param.12) | data formatting | bytes 7340032 | tf_op args[3]
  17.2 6.0 %copy.25 = bf16[256,7168]{0,1:T(8,128)(2,1)} copy(bf16[256,7168]{1,0:T(8,128)(2,1)} %param.11) | data formatting | bytes 7340032 | tf_op args[2]
  23.3 6.2 %copy.26 = bf16[256,7168]{0,1:T(8,128)(2,1)} copy(bf16[256,7168]{1,0:T(8,128)(2,1)} %param.10) | data formatting | bytes 7340032 | tf_op args[1]
  29.5 8.4 %fusion.1 = (bf16[256,7168]{0,1:T(8,128)(2,1)}, bf16[256,7168]{0,1:T(8,128)(2,1)}) fusion(bf16[256,7168]{0,1:T(8,128)(2,1)} %copy.24, bf16[256,7168]{0,1:T(8,128)(2,1)} %copy.26, bf16[256,7168]{0,1:T(8,128)(2,1)} %copy.25), kind=kLoop, calls=%fused_computation.9 | loop fusion | flops 29360128 | bytes 18350080 | tf_op jit(solution)/shard_map/convert_element_type | solution.py:30
  37.9 5.9 %copy.27 = bf16[256,56,128]{2,0,1:T(8,128)(2,1)} copy(bf16[256,56,128]{0,2,1:T(8,128)(2,1)} %bitcast.19) | data formatting | bytes 7340032 | tf_op jit(solution)/shard_map/reshape | solution.py:35
  43.8 5.9 %copy.28 = bf16[256,56,128]{2,0,1:T(8,128)(2,1)} copy(bf16[256,56,128]{0,2,1:T(8,128)(2,1)} %bitcast.18) | data formatting | bytes 7340032 | tf_op jit(solution)/shard_map/reshape | solution.py:36
  49.8 0.0 copy-done.3
  49.8 0.0 copy-start.4
  49.8 6.7 %pad_maximum_fusion = bf16[256,112,128]{2,0,1:T(8,128)(2,1)} fusion(bf16[256,56,128]{2,0,1:T(8,128)(2,1)} %copy.28, bf16[256,56,128]{2,0,1:T(8,128)(2,1)} %copy.27), kind=kLoop, calls=%fused_computation.16 | loop fusion | flops 3670016 | bytes 14680064 | tf_op jit(solution)/shard_map/concatenate | solution.py:33
  56.6 3.8 %gather_fusion.1 = bf16[16,256,128]{2,1,0:T(8,128)(2,1)S(1)} fusion(bf16[256,112,128]{2,0,1:T(8,128)(2,1)} %pad_maximum_fusion, s32[1024]{0:T(1024)S(1)} %pad_clamp_fusion), kind=kCustom, calls=%fused_computation.1 | custom fusion | bytes 2097216 | tf_op jit(solution)/shard_map/jit(_take)/gather | solution.py:40
  60.4 0.0 copy-done.4
  60.4 0.2 convert_reduce_fusion.1
  60.6 0.6 fusion.20
  61.2 6.4 %copy.23 = bf16[256,64,128]{2,0,1:T(8,128)(2,1)} copy(bf16[256,64,128]{0,2,1:T(8,128)(2,1)} %bitcast.21) | data formatting | bytes 8388608 | tf_op jit(solution)/shard_map/reshape | solution.py:31
  67.6 2.9 %gather_fusion = bf16[16,256,128]{2,1,0:T(8,128)(2,1)S(1)} fusion(bf16[256,64,128]{2,0,1:T(8,128)(2,1)} %copy.23, s32[1024]{0:T(1024)S(1)} %pad_clamp_fusion.1), kind=kCustom, calls=%fused_computation | custom fusion | bytes 2097216 | tf_op jit(solution)/shard_map/jit(_take)/gather | solution.py:32
  70.6 1.5 %fusion.8 = f32[16,128,128]{2,1,0:T(8,128)} fusion(bf16[16,256,128]{2,1,0:T(8,128)(2,1)S(1)} %gather_fusion.1, bf16[16,256,128]{2,1,0:T(8,128)(2,1)S(1)} %gather_fusion, pred[16]{0:T(512)(128)(4,1)S(1)} %get-tuple-element.3, pred[16]{0:T(512)(128)(4,1)S(1)} %get-tuple-element.10), kind=kOutput, calls=%fused_computation.18 | convolution fusion | flops 135266304 | bytes 3145760 | tf_op jit(solution)/shard_map/tbi,tbj->bij/dot_general | solution.py:41
  72.1 0.4 broadcast_in_dim.42
  72.5 2.3 %scatter_fusion = f32[48,128,128]{2,1,0:T(8,128)S(1)} fusion(f32[48,128,128]{2,1,0:T(8,128)S(1)} %broadcast_in_dim.42, s32[16]{0:T(128)S(1)} %get-tuple-element.12, f32[16,128,128]{2,1,0:T(8,128)} %fusion.8), kind=kCustom, calls=%fused_computation.2 | custom fusion | bytes 3145792 | tf_op jit(solution)/shard_map/scatter | solution.py:53
  74.7 0.0 copy-start
  74.8 0.0 copy-start.1
  74.8 1.4 %convert_element_type.32 = bf16[48,128,128]{2,1,0:T(8,128)(2,1)} convert(f32[48,128,128]{2,1,0:T(8,128)S(1)} %scatter_fusion) | non-fusion elementwise | flops 786432 | bytes 4718592 | tf_op jit(solution)/shard_map/convert_element_type | solution.py:56
  76.2 7.1 %all-to-all-start = ((bf16[48,128,128]{2,1,0:T(8,128)(2,1)}), bf16[48,128,128]{2,1,0:T(8,128)(2,1)S(1)}, u32[]{:S(2)}, u32[]{:S(2)}) async-start(bf16[48,128,128]{2,1,0:T(8,128)(2,1)} %convert_element_type.32), calls=%async_computation | async-start | bytes 3145728 | tf_op jit(solution)/shard_map/all_to_all | solution.py:55
  83.3 0.6 iota_compare_fusion.1
  84.0 36.6 %all-to-all-done = bf16[48,128,128]{2,1,0:T(8,128)(2,1)S(1)} async-done(((bf16[48,128,128]{2,1,0:T(8,128)(2,1)}), bf16[48,128,128]{2,1,0:T(8,128)(2,1)S(1)}, u32[]{:S(2)}, u32[]{:S(2)}) %all-to-all-start) | async-done | bytes 1572896 | tf_op jit(solution)/shard_map/all_to_all | solution.py:55
  120.6 0.3 convert_reduce_fusion
  120.8 0.0 copy-done
  120.8 0.0 copy-done.1
  120.9 0.0 copy-done.2
  120.9 1.0 fusion.18
  (7 shorter events, 0.0 us)
Async XLA Ops:
  7.2 54.1 %all-gather.2.cloned.1.call-start = ((), (), s32[]{:S(2)}) async-start(), calls=%async_computation.1 | async-start | bytes 6291456 | tf_op jit(solution)/shard_map/all_gather | solution.py:19
  43.8 5.9 %copy-start.3 = (s32[16,3]{0,1:T(4,128)S(1)}, s32[16,3]{0,1:T(4,128)}, u32[]{:S(2)}) copy-start(s32[16,3]{0,1:T(4,128)} %param.13) | copy-start | bytes 580
  49.8 10.6 %copy-start.4 = (s32[16]{0:T(128)S(1)}, s32[16]{0:T(128)}, u32[]{:S(2)}) copy-start(s32[16]{0:T(128)} %param.14) | copy-start | bytes 196
  74.7 46.1 %copy-start = (f32[3,128,128]{2,1,0:T(8,128)S(1)}, f32[3,128,128]{2,1,0:T(8,128)}, u32[]{:S(2)}) copy-start(f32[3,128,128]{2,1,0:T(8,128)} %param.17) | copy-start | bytes 589828
  74.8 46.1 %copy-start.1 = (f32[3,128,128]{2,1,0:T(8,128)S(1)}, f32[3,128,128]{2,1,0:T(8,128)}, u32[]{:S(2)}) copy-start(f32[3,128,128]{2,1,0:T(8,128)} %param.15) | copy-start | bytes 589828
  76.2 44.7 %copy-start.2 = (f32[3,128,128]{2,1,0:T(8,128)S(1)}, f32[3,128,128]{2,1,0:T(8,128)}, u32[]{:S(2)}) copy-start(f32[3,128,128]{2,1,0:T(8,128)} %param.16) | copy-start | bytes 589828
  76.2 44.4 %all-to-all-start = ((bf16[48,128,128]{2,1,0:T(8,128)(2,1)}), bf16[48,128,128]{2,1,0:T(8,128)(2,1)S(1)}, u32[]{:S(2)}, u32[]{:S(2)}) async-start(bf16[48,128,128]{2,1,0:T(8,128)(2,1)} %convert_element_type.32), calls=%async_computation | async-start | bytes 3145728 | tf_op jit(solution)/shard_map/all_to_all | solution.py:55
Sparse Core Ops, SparseCore 0:
  11.4 15.0 all-gather.1
where the time goes:
time: 130 us; the launch traced here: 129 us
  local copies, waits for them, and re-layouts  49.9 us (38%)
  waiting for transfers between devices  36.6 us (28%)
  other arithmetic  19.4 us (15%)
  between operations  14.2 us (11%)
  starting transfers between devices  7.13 us (5%)
  matrix products  1.54 us (1%)
    all_to_all x1, waiting for transfers between devices, local(): lax.all_to_all(outgoing.astype(jnp.bfloat16), 'dp', split_axis=0, concat_...  36.6 us
    unnamed x14, local copies, waits for them, and re-layouts  22.2 us
    convert_element_type x1, other arithmetic, local(): grad_gate = (cotangent * up_pre.astype(jnp.float32) * (sigmoid_gate * (1....  8.45 us
    all_to_all x1, starting transfers between devices, local(): lax.all_to_all(outgoing.astype(jnp.bfloat16), 'dp', split_axis=0, concat_...  7.1 us
    concatenate x1, other arithmetic, local(): jnp.concatenate([grad_gate.reshape(tokens, column_blocks, block_size), gr...  6.74 us
    reshape x1, local copies, waits for them, and re-layouts, local(): row_cells = gathered.reshape(tokens, -1, block_size)  6.37 us
    reshape x1, local copies, waits for them, and re-layouts, local(): grad_up.reshape(tokens, column_blocks, block_size)  5.94 us
    reshape x1, local copies, waits for them, and re-layouts, local(): grad_gate.reshape(tokens, column_blocks, block_size)  5.93 us
  transfers between devices with their start and end apart: 2, of which 1 were waited for; matrix products, arithmetic and copies ran while one was open for 39% of the time, Pallas kernels for 0%

commit v1 on v0

v1 whole, which is shorter than its diff:
```python
import functools
import jax
import jax.numpy as jnp
from jax import lax
from jax.experimental import pallas as pl
from jax.experimental.pallas import tpu as pltpu
from jax.sharding import PartitionSpec as P

beta_first = 0.9
beta_second = 0.999
learn_rate = 0.01
epsilon = 1e-08
bias_first = 1.0 - 0.9**10
bias_second = 1.0 - 0.999**10

ANY = pl.BlockSpec(memory_space=pl.ANY)
SMEM = pl.BlockSpec(memory_space=pltpu.SMEM)
VMEM = pl.BlockSpec(memory_space=pltpu.VMEM)


def act_kernel(blk, own, gate, up, cot, act, place, gbuf, ubuf, cbuf, sems, seen, *, capacity):
    listed, tokens, size = act.shape

    def copies(k):
        cols = pl.ds(pl.multiple_of(blk[2, k] * size, size), size)
        return [
            pltpu.make_async_copy(src.at[:, cols], buf.at[k], sems.at[i, k])
            for i, (src, buf) in enumerate(((gate, gbuf), (up, ubuf), (cot, cbuf)))
        ]

    def begin(k, carry):
        for copy in copies(k):
            copy.start()
        return carry

    lax.fori_loop(0, listed, begin, 0)

    def clear(o, carry):
        seen[o] = 0
        return carry

    lax.fori_loop(0, seen.shape[0], clear, 0)

    def rank(k, carry):
        o = own[k]
        slot = seen[o]
        seen[o] = slot + 1
        place[k] = o * capacity + slot
        return carry

    lax.fori_loop(0, listed, rank, 0)
    place[listed] = seen[lax.axis_index("dp")]

    def compute(k, carry):
        for copy in copies(k):
            copy.wait()
        g = gbuf[k].astype(jnp.float32)
        c = cbuf[k].astype(jnp.float32)
        s = jax.nn.sigmoid(g)

        @pl.when(blk[0, k] == 0)
        def _():
            u = ubuf[k].astype(jnp.float32)
            act[k] = (c * u * (s * (1.0 + g * (1.0 - s)))).astype(act.dtype)

        @pl.when(blk[0, k] != 0)
        def _():
            act[k] = (c * (g * s)).astype(act.dtype)

        return carry

    lax.fori_loop(0, listed, compute, 0)


def product_kernel(blk, place, act, *rest, shards):
    feats = rest[:shards]
    out, fbuf, sems = rest[shards:]
    listed, tokens, size = act.shape
    per = feats[0].shape[1] // size
    mine = lax.axis_index("tensor")

    def begin(k, carry):
        r = blk[1, k]
        source = lax.rem(mine + shards - r // per, shards)
        cols = pl.ds(pl.multiple_of(lax.rem(r, per) * size, size), size)
        for j in range(shards):

            @pl.when(source == j)
            def _():
                pltpu.make_async_copy(feats[j].at[:, cols], fbuf.at[k], sems.at[k]).start()

        return carry

    lax.fori_loop(0, listed, begin, 0)

    def compute(k, carry):
        pltpu.make_async_copy(feats[0].at[:, pl.ds(0, size)], fbuf.at[k], sems.at[k]).wait()
        out[place[k]] = lax.dot_general(
            fbuf[k], act[k], (((0,), (0,)), ((), ())), preferred_element_type=jnp.float32
        ).astype(out.dtype)
        return carry

    lax.fori_loop(0, listed, compute, 0)


def local(features, gate_pre, up_pre, grad_hidden, blocks, owner, weights, moment1, moment2):
    size = weights.shape[-1]
    capacity = weights.shape[0]
    replicas = lax.axis_size("dp")
    shards = lax.axis_size("tensor")
    listed = owner.shape[0]
    tokens = features.shape[0]
    bf16, f32 = jnp.bfloat16, jnp.float32
    table = blocks.T

    feats = [features] + [
        lax.ppermute(features, "tensor", [(i, (i + j) % shards) for i in range(shards)])
        for j in range(1, shards)
    ]
    act, place = pl.pallas_call(
        functools.partial(act_kernel, capacity=capacity),
        out_shape=(
            jax.ShapeDtypeStruct((listed, tokens, size), bf16),
            jax.ShapeDtypeStruct((listed + 1,), jnp.int32),
        ),
        in_specs=[SMEM, SMEM, ANY, ANY, ANY],
        out_specs=(VMEM, SMEM),
        scratch_shapes=[pltpu.VMEM((listed, tokens, size), bf16)] * 3
        + [pltpu.SemaphoreType.DMA((3, listed)), pltpu.SMEM((replicas,), jnp.int32)],
        name="activations",
    )(table, owner, gate_pre, up_pre, grad_hidden)
    outgoing = pl.pallas_call(
        functools.partial(product_kernel, shards=shards),
        out_shape=jax.ShapeDtypeStruct((replicas * capacity, size, size), bf16),
        in_specs=[SMEM, SMEM, VMEM] + [ANY] * shards,
        out_specs=VMEM,
        scratch_shapes=[
            pltpu.VMEM((listed, tokens, size), bf16),
            pltpu.SemaphoreType.DMA((listed,)),
        ],
        name="products",
    )(table, place, act, *feats)
    incoming = lax.all_to_all(outgoing, "dp", split_axis=0, concat_axis=0, tiled=True)
    block_grad = jnp.sum(
        incoming.astype(f32).reshape(replicas, capacity, size, size), axis=0
    )
    is_valid = (jnp.arange(capacity, dtype=jnp.int32) < place[listed])[:, None, None]
    first_new = beta_first * moment1 + (1.0 - beta_first) * block_grad
    second_new = beta_second * moment2 + (1.0 - beta_second) * block_grad * block_grad
    weight_new = weights - learn_rate * (first_new / bias_first) / (
        jnp.sqrt(second_new / bias_second) + epsilon
    )
    return (
        jnp.where(is_valid, weight_new, weights),
        jnp.where(is_valid, first_new, moment1),
        jnp.where(is_valid, second_new, moment2),
    )


def solution(mesh):
    cells = P(("dp", "tensor"), None, None)
    split = P("dp", "tensor")
    return jax.shard_map(
        local,
        mesh=mesh,
        in_specs=(split, split, split, split, P("tensor", None), P("tensor"), cells, cells, cells),
        out_specs=(cells, cells, cells),
        check_vma=False,
    )
```

time: 130 us -> 59.7 us (0.46)
  local copies, waits for them, and re-layouts: 49.9 us -> 1.95 us
  other arithmetic: 19.4 us -> 1.9 us
  between operations: 14.2 us -> 0.74 us
  Pallas kernels: 0 us -> 11.3 us
  matrix products: 1.54 us -> 0 us
    unnamed x14 -> x10, local copies, waits for them, and re-layouts: 22.2 us -> 1.37 us
    reshape x3 -> x0, local copies, waits for them, and re-layouts: 18.2 us -> none  [the longest x1 6.37 us: local(): row_cells = gathered.reshape(tokens, -1, block_size)]
    pallas_call x0 -> x2, Pallas kernels: none -> 11.3 us  [the longest x1 6.62 us: local(): pl.pallas_call(functools.partial(product_kernel, shards=shards), out_shap...]
    convert_element_type x2 -> x0, other arithmetic: 9.87 us -> none  [the longest x1 8.45 us: local(): grad_gate = (cotangent * up_pre.astype(jnp.float32) * (sigmoid_gate * (1....]
    gather x2 -> x0, local copies, waits for them, and re-layouts: 6.76 us -> none  [the longest x1 3.83 us: local(): jnp.take(activations, blocks[:, 0] * column_blocks + blocks[:, 2], axis=1)]
    concatenate x1 -> x0, other arithmetic: 6.74 us -> none  [local(): jnp.concatenate([grad_gate.reshape(tokens, column_blocks, block_size), gr...]
    scatter x1 -> x0, local copies, waits for them, and re-layouts: 2.27 us -> none  [local(): outgoing = jnp.zeros((replicas * capacity, block_size, block_size), jnp.f...]
    dot_general x1 -> x0, matrix products: 1.54 us -> none  [local(): jnp.einsum('tbi,tbj->bij', chosen_rows, chosen_cols, preferred_element_ty...]
  transfers between devices with their start and end apart: 2 -> 2, of which waited for: 1 -> 1; matrix products, arithmetic and copies ran while one was open for 39% -> 2% of each run, Pallas kernels for 0% -> 8%
where the time goes in v1:
time: 59.7 us; the launch traced here: 59.4 us
  waiting for transfers between devices  36.2 us (61%)
  Pallas kernels  11.3 us (19%)
  starting transfers between devices  7.38 us (12%)
  local copies, waits for them, and re-layouts  1.95 us (3%)
  other arithmetic  1.9 us (3%)
  between operations  0.74 us (1%)
    all_to_all x1, waiting for transfers between devices, local(): lax.all_to_all(outgoing, 'dp', split_axis=0, concat_axis=0, tiled=True)  36.2 us
    all_to_all x1, starting transfers between devices, local(): lax.all_to_all(outgoing, 'dp', split_axis=0, concat_axis=0, tiled=True)  7.31 us
    pallas_call x1, Pallas kernels, local(): pl.pallas_call(functools.partial(product_kernel, shards=shards), out_shap...  6.62 us
    pallas_call x1, Pallas kernels, local(): pl.pallas_call(functools.partial(act_kernel, capacity=capacity), out_shap...  4.66 us
    unnamed x10, local copies, waits for them, and re-layouts  1.37 us
  transfers between devices with their start and end apart: 2, of which 1 were waited for; matrix products, arithmetic and copies ran while one was open for 2% of the time, Pallas kernels for 8%

profile of v1, /device:TPU:12, one launch (start us, length us, event | category | flops | bytes accessed | tf_op | source)
XLA Modules:
  0.0 59.4 jit_solution(16622195422019603239)
XLA Ops:
  0.6 0.1 collective-permute-start
  0.7 4.7 %activations.1 = (bf16[16,256,128]{2,1,0:T(8,128)(2,1)}, s32[17]{0:T(128)}) custom-call(s32[3,16]{1,0:T(4,128)} %bitcast.5, s32[16]{0:T(128)} %own.1, bf16[256,7168]{1,0:T(8,128)(2,1)} %gate.1, bf16[256,7168]{1,0:T(8,128)(2,1)} %up.1, bf16[256,7168]{1,0:T(8,128)(2,1)} %cot.1), custom_call_target="tpu_custom_call" | custom-call | tf_op jit(solution)/shard_map/activations/pallas_call | solution.py:120
  5.4 0.0 collective-permute-done.rest_1_
  5.4 0.0 copy-start
  5.4 1.3 %copy-done = bf16[256,4096]{1,0:T(8,128)(2,1)} copy-done((bf16[256,4096]{1,0:T(8,128)(2,1)}, bf16[256,4096]{1,0:T(8,128)(2,1)S(1)}, u32[]{:S(2)}) %copy-start) | copy-done | bytes 2097176
  6.7 6.6 %products.1 = bf16[48,128,128]{2,1,0:T(8,128)(2,1)} custom-call(s32[3,16]{1,0:T(4,128)} %bitcast.6, s32[17]{0:T(128)} %get-tuple-element.5.place, bf16[16,256,128]{2,1,0:T(8,128)(2,1)} %get-tuple-element.6.act, bf16[256,4096]{1,0:T(8,128)(2,1)} %rest_0_.1, bf16[256,4096]{1,0:T(8,128)(2,1)} %copy-done), custom_call_target="tpu_custom_call" | custom-call | tf_op jit(solution)/shard_map/products/pallas_call | solution.py:132
  13.4 0.0 copy-start.4
  13.4 0.0 copy-start.1
  13.4 0.0 copy-start.2
  13.4 0.0 copy-start.3
  13.4 7.3 %all-to-all-start = ((bf16[48,128,128]{2,1,0:T(8,128)(2,1)}), bf16[48,128,128]{2,1,0:T(8,128)(2,1)S(1)}, u32[]{:S(2)}, u32[]{:S(2)}) async-start(bf16[48,128,128]{2,1,0:T(8,128)(2,1)} %products.1), calls=%async_computation | async-start | bytes 3145728 | tf_op jit(solution)/shard_map/all_to_all | solution.py:143
  20.7 0.0 copy-done.4
  20.7 0.6 slice.3
  21.3 0.6 %iota_compare_fusion = pred[3]{0:T(512)(128)(4,1)S(1)} fusion(s32[]{:T(128)} %bitcast.1), kind=kLoop, calls=%fused_computation.7 | loop fusion | flops 3 | bytes 7 | tf_op jit(solution)/shard_map/lt | solution.py:147
  22.0 36.2 %all-to-all-done = bf16[48,128,128]{2,1,0:T(8,128)(2,1)S(1)} async-done(((bf16[48,128,128]{2,1,0:T(8,128)(2,1)}), bf16[48,128,128]{2,1,0:T(8,128)(2,1)S(1)}, u32[]{:S(2)}, u32[]{:S(2)}) %all-to-all-start) | async-done | bytes 1572896 | tf_op jit(solution)/shard_map/all_to_all | solution.py:143
  58.1 0.3 convert_reduce_fusion
  58.4 0.0 copy-done.1
  58.4 0.0 copy-done.2
  58.4 0.0 copy-done.3
  58.4 1.0 %fusion.2 = (f32[3,128,128]{2,1,0:T(8,128)}, f32[3,128,128]{2,1,0:T(8,128)}, f32[3,128,128]{2,1,0:T(8,128)}) fusion(f32[3,128,128]{2,1,0:T(8,128)S(1)} %copy-done.1, f32[3,128,128]{2,1,0:T(8,128)S(1)} %convert_reduce_fusion, pred[3]{0:T(512)(128)(4,1)S(1)} %iota_compare_fusion, f32[3,128,128]{2,1,0:T(8,128)S(1)} %copy-done.2, f32[3,128,128]{2,1,0:T(8,128)S(1)} %copy-done.3), kind=kLoop, calls=%fused_computation.6 | loop fusion | flops 737280 | bytes 1376259 | tf_op jit(solution)/shard_map/jit(_where)/select_n | solution.py:156
Async XLA Ops:
  0.6 4.8 %collective-permute-start = (bf16[256,4096]{1,0:T(8,128)(2,1)}, bf16[256,4096]{1,0:T(8,128)(2,1)S(1)}, u32[]{:S(2)}, u32[]{:S(2)}) collective-permute-start(bf16[256,4096]{1,0:T(8,128)(2,1)} %rest_0_.1), channel_id=1, source_target_pairs={{0,1},{1,0},{2,3},{3,2},{4,5},{5,4},{6,7},{7,6},{8,9},{9,8},{10,11... | collective-permute-start | bytes 6291464 | tf_op jit(solution)/shard_map/ppermute | solution.py:117
  5.4 1.3 %copy-start = (bf16[256,4096]{1,0:T(8,128)(2,1)}, bf16[256,4096]{1,0:T(8,128)(2,1)S(1)}, u32[]{:S(2)}) copy-start(bf16[256,4096]{1,0:T(8,128)(2,1)S(1)} %collective-permute-done.rest_1_) | copy-start | bytes 6291460
  13.4 7.4 %copy-start.4 = (s32[17]{0:T(128)S(1)}, s32[17]{0:T(128)}, u32[]{:S(2)}) copy-start(s32[17]{0:T(128)} %get-tuple-element.5.place) | copy-start | bytes 208
  13.4 45.0 %copy-start.1 = (f32[3,128,128]{2,1,0:T(8,128)S(1)}, f32[3,128,128]{2,1,0:T(8,128)}, u32[]{:S(2)}) copy-start(f32[3,128,128]{2,1,0:T(8,128)} %param.17) | copy-start | bytes 589828
  13.4 45.0 %copy-start.2 = (f32[3,128,128]{2,1,0:T(8,128)S(1)}, f32[3,128,128]{2,1,0:T(8,128)}, u32[]{:S(2)}) copy-start(f32[3,128,128]{2,1,0:T(8,128)} %param.15) | copy-start | bytes 589828
  13.4 45.0 %copy-start.3 = (f32[3,128,128]{2,1,0:T(8,128)S(1)}, f32[3,128,128]{2,1,0:T(8,128)}, u32[]{:S(2)}) copy-start(f32[3,128,128]{2,1,0:T(8,128)} %param.16) | copy-start | bytes 589828
  13.4 44.7 %all-to-all-start = ((bf16[48,128,128]{2,1,0:T(8,128)(2,1)}), bf16[48,128,128]{2,1,0:T(8,128)(2,1)S(1)}, u32[]{:S(2)}, u32[]{:S(2)}) async-start(bf16[48,128,128]{2,1,0:T(8,128)(2,1)} %products.1), calls=%async_computation | async-start | bytes 3145728 | tf_op jit(solution)/shard_map/all_to_all | solution.py:143

commit v2 on v1

v2 whole, which is shorter than its diff:
```python
import functools
import jax
import jax.numpy as jnp
from jax import lax
from jax.experimental import pallas as pl
from jax.experimental.pallas import tpu as pltpu
from jax.sharding import PartitionSpec as P

beta_first = 0.9
beta_second = 0.999
learn_rate = 0.01
epsilon = 1e-08
bias_first = 1.0 - 0.9**10
bias_second = 1.0 - 0.999**10

HBM = pl.BlockSpec(memory_space=pltpu.HBM)
SMEM = pl.BlockSpec(memory_space=pltpu.SMEM)
VMEM = pl.BlockSpec(memory_space=pltpu.VMEM)

COLUMNS = 4


def bin_slots(listed, replicas, capacity):
    crowd = min(listed, capacity * replicas // COLUMNS)
    return max(-(-listed // 3), -(-crowd // 2))


def route(own, place, seen, work, *, capacity, slots):
    listed = own.shape[0]
    replicas = seen.shape[0]
    me = lax.axis_index("dp")
    column = lax.rem(me, COLUMNS)
    my_bit = (lax.rem(column, 2), column // 2)
    COUNT, RANK, TAKE, AT_A, AT_B, LOAD = (i * COLUMNS for i in range(6))

    def clear_seen(o, carry):
        seen[o] = 0
        return carry

    lax.fori_loop(0, replicas, clear_seen, 0)
    for i in range(6 * COLUMNS):
        work[i] = 0

    def count(k, carry):
        q = lax.rem(own[k], COLUMNS)
        work[COUNT + q] = work[COUNT + q] + 1
        return carry

    lax.fori_loop(0, listed, count, 0)

    first, most = jnp.int32(0), work[COUNT]
    for q in range(1, COLUMNS):
        n = work[COUNT + q]
        first = jnp.where(n > most, q, first)
        most = jnp.maximum(n, most)
    for i in range(COLUMNS):
        q = jnp.bitwise_xor(first, i)
        bin_a = LOAD + lax.rem(q, 2)
        bin_b = LOAD + 2 + q // 2
        n, load_a, load_b = work[COUNT + q], work[bin_a], work[bin_b]
        take = jnp.clip(lax.shift_right_arithmetic(n + load_b - load_a, 1), 0, n)
        work[TAKE + q] = take
        work[AT_A + q] = load_a
        work[AT_B + q] = load_b
        work[bin_a] = load_a + take
        work[bin_b] = load_b + n - take

    def clear_place(j, carry):
        place[listed + j] = 0
        return carry

    lax.fori_loop(0, replicas // COLUMNS * capacity, clear_place, 0)

    def assign(k, carry):
        o = own[k]
        q = lax.rem(o, COLUMNS)
        r = work[RANK + q]
        work[RANK + q] = r + 1
        take = work[TAKE + q]
        in_a = r < take
        slot = jnp.where(in_a, work[AT_A + q] + r, work[AT_B + q] + r - take)
        bit = jnp.where(in_a, lax.rem(q, 2), q // 2)
        mine = jnp.where(in_a, my_bit[0], my_bit[1])
        keep = (bit == mine).astype(jnp.int32)
        place[k] = jnp.where(in_a, 0, 2 * slots) + keep * slots + slot
        s = seen[o]
        seen[o] = s + 1

        @pl.when(q == column)
        def _():
            place[listed + o // COLUMNS * capacity + s] = jnp.where(in_a, 0, slots) + slot

        return carry

    lax.fori_loop(0, listed, assign, 0)
    place[place.shape[0] - 1] = seen[me]


def act_kernel(blk, own, features, gate, up, cot, *rest, capacity, slots):
    states, rest = rest[:3], rest[3:]
    act, rows, place = rest[:3]
    held, (gbuf, ubuf, cbuf, sems, state_sems, seen, work) = rest[3:6], rest[6:]
    listed, tokens, size = act.shape
    per = features.shape[1] // size

    def row_copy(k):
        cols = pl.ds(pl.multiple_of(lax.rem(blk[1, k], per) * size, size), size)
        return pltpu.make_async_copy(features.at[:, cols], rows.at[k], sems.at[3, k])

    def copies(k):
        cols = pl.ds(pl.multiple_of(blk[2, k] * size, size), size)
        return [
            pltpu.make_async_copy(src.at[:, cols], buf.at[k], sems.at[i, k])
            for i, (src, buf) in enumerate(((gate, gbuf), (up, ubuf), (cot, cbuf)))
        ]

    def begin(k, carry):
        for copy in copies(k):
            copy.start()
        return carry

    def begin_rows(k, carry):
        row_copy(k).start()
        return carry

    lax.fori_loop(0, listed, begin, 0)
    lax.fori_loop(0, listed, begin_rows, 0)
    state_copies = [
        pltpu.make_async_copy(src, dst, state_sems.at[i])
        for i, (src, dst) in enumerate(zip(states, held))
    ]
    for copy in state_copies:
        copy.start()
    route(own, place, seen, work, capacity=capacity, slots=slots)

    def compute(k, carry):
        for copy in copies(k):
            copy.wait()
        gated = blk[0, k] == 0
        g = gbuf[k].astype(jnp.float32)
        c = cbuf[k].astype(jnp.float32)
        s = jax.nn.sigmoid(g)
        first = jnp.where(gated, c * ubuf[k].astype(jnp.float32), c)
        act[k] = (first * jnp.where(gated, s * (1.0 + g * (1.0 - s)), g * s)).astype(act.dtype)
        return carry

    lax.fori_loop(0, listed, compute, 0)

    def end_rows(k, carry):
        row_copy(k).wait()
        return carry

    lax.fori_loop(0, listed, end_rows, 0)
    for copy in state_copies:
        copy.wait()


def product_kernel(blk, place, act, rows, *rest, shards, slots):
    others = rest[: shards - 1]
    send_a, send_b, part = rest[shards - 1 :]
    listed, tokens, size = act.shape
    per = others[0].shape[1] // size
    mine = lax.axis_index("tensor")

    def compute(k, carry):
        r = blk[1, k]
        cols = pl.ds(pl.multiple_of(lax.rem(r, per) * size, size), size)
        source = lax.rem(mine + shards - r // per, shards)
        lhs = rows[k]
        for j in range(1, shards):
            lhs = jnp.where(source == j, others[j - 1][:, cols], lhs)
        part[place[k]] = lax.dot_general(
            lhs, act[k], (((0,), (0,)), ((), ())), preferred_element_type=jnp.float32
        )
        return carry

    lax.fori_loop(0, listed, compute, 0, unroll=4)
    send_a[...] = part[:slots].astype(send_a.dtype)
    send_b[...] = part[2 * slots : 3 * slots].astype(send_b.dtype)


def add_kernel(part, got, total, send, *, start):
    total[...] = part[start : start + total.shape[0]] + got[...].astype(total.dtype)
    send[...] = total[...].astype(send.dtype)


def plane_kernel(place, sum_a, sum_b, other_a, other_b, *outs, listed, capacity):
    kept, sends = outs[0], outs[1:]
    slots = sum_a.shape[0]
    plane = lax.axis_index("dp") // COLUMNS

    def total(z, s):
        j = place[listed + z * capacity + s]
        a = jnp.minimum(j, slots - 1)
        b = jnp.maximum(j - slots, 0)
        return jnp.where(
            j < slots,
            sum_a[a] + other_a[a].astype(jnp.float32),
            sum_b[b] + other_b[b].astype(jnp.float32),
        )

    if len(sends) == 1:
        sends = sends[0]

        def lay(j, carry):
            sends[j] = total(j // capacity, lax.rem(j, capacity)).astype(sends.dtype)
            return carry

        lax.fori_loop(0, sends.shape[0], lay, 0)
    else:
        for k, send in enumerate(sends):
            for s in range(capacity):
                send[s] = total(jnp.bitwise_xor(plane, k + 1), s).astype(send.dtype)
    for s in range(capacity):
        kept[s] = total(plane, s)


def update_kernel(place, kept, *rest, count):
    parts, rest = rest[:count], rest[count:]
    weights, moment1, moment2, *outs = rest
    outs, (bufs, sems) = outs[:3], outs[3:]
    held = place[place.shape[0] - 1]
    copies = []
    for s in range(kept.shape[0]):
        valid = s < held
        block_grad = kept[s]
        for part in parts:
            block_grad = block_grad + part[s].astype(jnp.float32)
        first_new = beta_first * moment1[s] + (1.0 - beta_first) * block_grad
        second_new = beta_second * moment2[s] + (1.0 - beta_second) * block_grad * block_grad
        weight_new = weights[s] - learn_rate * (first_new / bias_first) / (
            jnp.sqrt(second_new / bias_second) + epsilon
        )
        bufs[0, s] = jnp.where(valid, weight_new, weights[s])
        bufs[1, s] = jnp.where(valid, first_new, moment1[s])
        bufs[2, s] = jnp.where(valid, second_new, moment2[s])
        for i, out in enumerate(outs):
            copy = pltpu.make_async_copy(bufs.at[i, s], out.at[s], sems.at[i, s])
            copy.start()
            copies.append(copy)
    for copy in copies:
        copy.wait()


def local(features, gate_pre, up_pre, grad_hidden, blocks, owner, weights, moment1, moment2):
    size = weights.shape[-1]
    capacity = weights.shape[0]
    replicas = lax.axis_size("dp")
    shards = lax.axis_size("tensor")
    listed = owner.shape[0]
    tokens = features.shape[0]
    planes = replicas // COLUMNS
    slots = bin_slots(listed, replicas, capacity)
    bf16, f32 = jnp.bfloat16, jnp.float32
    table = blocks.T
    block = size * size
    column = tokens * size
    in_vmem = lambda n, dtype: pltpu.VMEM((n, size, size), dtype)
    swap = lambda v, bit: lax.ppermute(v, "dp", [(i, i ^ bit) for i in range(replicas)])
    stay = lambda v: pltpu.with_memory_space_constraint(v, pltpu.HBM)
    grant = lambda nbytes: pltpu.CompilerParams(vmem_limit_bytes=nbytes * 5 // 4 + (4 << 20))

    others = [
        lax.ppermute(features, "tensor", [(i, (i + j) % shards) for i in range(shards)])
        for j in range(1, shards)
    ]
    act, rows, place, *states = pl.pallas_call(
        functools.partial(act_kernel, capacity=capacity, slots=slots),
        out_shape=(
            pltpu.VMEM((listed, tokens, size), bf16),
            pltpu.VMEM((listed, tokens, size), bf16),
            jax.ShapeDtypeStruct((listed + planes * capacity + 1,), jnp.int32),
        )
        + (in_vmem(capacity, f32),) * 3,
        in_specs=[SMEM, SMEM] + [HBM] * 7,
        out_specs=(VMEM, VMEM, SMEM, VMEM, VMEM, VMEM),
        scratch_shapes=[pltpu.VMEM((listed, tokens, size), bf16)] * 3
        + [
            pltpu.SemaphoreType.DMA((4, listed)),
            pltpu.SemaphoreType.DMA((3,)),
            pltpu.SMEM((replicas,), jnp.int32),
            pltpu.SMEM((6 * COLUMNS,), jnp.int32),
        ],
        compiler_params=grant(5 * listed * column * 2 + 3 * capacity * block * 4),
        name="activations",
    )(table, owner, *map(stay, (features, gate_pre, up_pre, grad_hidden, weights, moment1, moment2)))
    send_a, send_b, part = pl.pallas_call(
        functools.partial(product_kernel, shards=shards, slots=slots),
        out_shape=(in_vmem(slots, bf16), in_vmem(slots, bf16), in_vmem(4 * slots, f32)),
        in_specs=[SMEM, SMEM] + [VMEM] * (shards + 1),
        out_specs=(VMEM, VMEM, VMEM),
        compiler_params=grant(
            2 * listed * column * 2 + (shards - 1) * features.size * 2 + 20 * slots * block
        ),
        name="products",
    )(table, place, act, rows, *others)

    def add(got, start):
        return pl.pallas_call(
            functools.partial(add_kernel, start=start),
            out_shape=(in_vmem(slots, f32), in_vmem(slots, bf16)),
            in_specs=[VMEM, VMEM],
            out_specs=(VMEM, VMEM),
            compiler_params=grant(24 * slots * block),
            name="sums",
        )(part, got)

    sum_a, send_a = add(swap(send_a, 1), slots)
    sum_b, send_b = add(swap(send_b, 2), 3 * slots)
    other_a = swap(send_a, 2)
    other_b = swap(send_b, 1)
    direct = planes <= 4 and planes & (planes - 1) == 0
    kept, *sends = pl.pallas_call(
        functools.partial(plane_kernel, listed=listed, capacity=capacity),
        out_shape=(in_vmem(capacity, f32),)
        + ((in_vmem(capacity, bf16),) * (planes - 1) if direct else (in_vmem(planes * capacity, bf16),)),
        in_specs=[SMEM, VMEM, VMEM, VMEM, VMEM],
        out_specs=(VMEM,) * (planes if direct else 2),
        compiler_params=grant((12 * slots + (4 + 2 * planes) * capacity) * block),
        name="planes",
    )(place, sum_a, sum_b, other_a, other_b)
    if direct:
        parts = [swap(send, (k + 1) * COLUMNS) for k, send in enumerate(sends)]
    else:
        groups = [[z * COLUMNS + c for z in range(planes)] for c in range(COLUMNS)]
        incoming = lax.all_to_all(
            sends[0], "dp", split_axis=0, concat_axis=0, tiled=True, axis_index_groups=groups
        )
        away = jnp.arange(planes) != lax.axis_index("dp") // COLUMNS
        incoming = incoming.astype(f32).reshape(planes, capacity, size, size)
        parts = [jnp.sum(jnp.where(away[:, None, None, None], incoming, 0.0), axis=0)]
    return pl.pallas_call(
        functools.partial(update_kernel, count=len(parts)),
        out_shape=(jax.ShapeDtypeStruct(weights.shape, f32),) * 3,
        in_specs=[SMEM] + [VMEM] * (4 + len(parts)),
        out_specs=(HBM, HBM, HBM),
        scratch_shapes=[
            pltpu.VMEM((3,) + weights.shape, f32),
            pltpu.SemaphoreType.DMA((3, capacity)),
        ],
        compiler_params=grant((28 + 4 * len(parts)) * capacity * block),
        name="update",
    )(place, kept, *parts, *states)


def solution(mesh):
    cells = P(("dp", "tensor"), None, None)
    split = P("dp", "tensor")
    return jax.shard_map(
        local,
        mesh=mesh,
        in_specs=(split, split, split, split, P("tensor", None), P("tensor"), cells, cells, cells),
        out_specs=(cells, cells, cells),
        check_vma=False,
    )
```

time: 59.7 us -> 38.2 us (0.64)
  the two profiles are of different devices: /device:TPU:12 before, /device:TPU:0 now
where the time goes in v2:
time: 38.2 us; the launch traced here: 38 us
  waiting for transfers between devices  14.8 us (39%)
  starting transfers between devices  12.4 us (32%)
  Pallas kernels  8.65 us (23%)
  local copies, waits for them, and re-layouts  1.34 us (4%)
  between operations  0.69 us (2%)
    ppermute x7, waiting for transfers between devices, local(): lax.ppermute(v, 'dp', [(i, i ^ bit) for i in range(replicas)])  14.8 us
    ppermute x7, starting transfers between devices, local(): lax.ppermute(v, 'dp', [(i, i ^ bit) for i in range(replicas)])  11.9 us
    pallas_call x1, Pallas kernels, local(): pl.pallas_call(functools.partial(act_kernel, capacity=capacity, slots=slo...  4.45 us
    pallas_call x1, Pallas kernels, local(): pl.pallas_call(functools.partial(product_kernel, shards=shards, slots=slo...  1.81 us
    pallas_call x1, Pallas kernels, local(): pl.pallas_call(functools.partial(update_kernel, count=len(parts)), out_sh...  1.51 us
    unnamed x6, local copies, waits for them, and re-layouts  1.34 us
  transfers between devices with their start and end apart: 8, of which 6 were waited for; matrix products, arithmetic and copies ran while one was open for 0% of the time, Pallas kernels for 12%

profile of v2, /device:TPU:0, one launch (start us, length us, event | category | flops | bytes accessed | tf_op | source)
XLA Modules:
  0.0 38.0 jit_solution(11547124833648006757)
XLA Ops:
  0.6 0.6 %collective-permute-start = (bf16[256,4096]{1,0:T(8,128)(2,1)}, bf16[256,4096]{1,0:T(8,128)(2,1)S(1)}, u32[]{:S(2)}, u32[]{:S(2)}) collective-permute-start(bf16[256,4096]{1,0:T(8,128)(2,1)} %features.1), channel_id=1, source_target_pairs={{0,1},{1,0},{2,3},{3,2},{4,5},{5,4},{6,7},{7,6},{8,9},{9,8},{10,11... | collective-permute-start | bytes 6291464 | tf_op jit(solution)/shard_map/ppermute | solution.py:264
  1.2 0.0 copy-start
  1.2 0.7 %copy-done = s32[16,3]{0,1:T(4,128)S(1)} copy-done((s32[16,3]{0,1:T(4,128)S(1)}, s32[16,3]{0,1:T(4,128)}, u32[]{:S(2)}) %copy-start) | copy-done | bytes 216
  1.9 0.0 copy-start.2
  1.9 0.7 %copy-done.2 = s32[16]{0:T(128)S(1)} copy-done((s32[16]{0:T(128)S(1)}, s32[16]{0:T(128)}, u32[]{:S(2)}) %copy-start.2) | copy-done | bytes 88
  2.5 0.0 copy-start.1
  2.5 4.4 %activations.1 = (bf16[16,256,128]{2,1,0:T(8,128)(2,1)S(1)}, bf16[16,256,128]{2,1,0:T(8,128)(2,1)S(1)}, s32[29]{0:T(128)S(1)}, f32[3,128,128]{2,1,0:T(8,128)S(1)...) custom-call(s32[3,16]{1,0:T(4,128)S(1)} %bitcast.1, s32[16]{0:T(128)S(1)} %copy-done.2, ...), custom_call_target="tpu_custom_call" | custom-call | tf_op jit(solution)/shard_map/activations/pallas_call | solution.py:267
  7.0 0.0 collective-permute-done.rest_0_
  7.0 0.0 copy-done.1
  7.0 1.8 %products.1 = (bf16[6,128,128]{2,1,0:T(8,128)(2,1)S(1)}, bf16[6,128,128]{2,1,0:T(8,128)(2,1)S(1)}, f32[24,128,128]{2,1,0:T(8,128)S(1)}) custom-call(s32[3,16]{1,0:T(4,128)S(1)} %bitcast.2, s32[29]{0:T(128)S(1)} %get-tuple-element.20.place, bf16[16,256,128]{2,1,0:T(8,128)(2,1)S(1)} %get-tuple-element.21.act, ...), custom_call_target="tpu_custom_call" | custom-call | tf_op jit(solution)/shard_map/products/pallas_call | solution.py:287
  8.8 2.6 %collective-permute-start.2 = (bf16[6,128,128]{2,1,0:T(8,128)(2,1)S(1)}, bf16[6,128,128]{2,1,0:T(8,128)(2,1)S(1)}, u32[]{:S(2)}, u32[]{:S(2)}) collective-permute-start(bf16[6,128,128]{2,1,0:T(8,128)(2,1)S(1)} %get-tuple-element.26), channel_id=1, source_target_pairs={{0,4},{2,6},{4,0},{6,2},{8,12},{10,14},{12,8},{14,10},{16,20},{18,... | collective-permute-start | bytes 589832 | tf_op jit(solution)/shard_map/ppermute | solution.py:259
  11.4 1.5 %collective-permute-start.1 = (bf16[6,128,128]{2,1,0:T(8,128)(2,1)S(1)}, bf16[6,128,128]{2,1,0:T(8,128)(2,1)S(1)}, u32[]{:S(2)}, u32[]{:S(2)}) collective-permute-start(bf16[6,128,128]{2,1,0:T(8,128)(2,1)S(1)} %get-tuple-element.24), channel_id=1, source_target_pairs={{0,2},{2,0},{4,6},{6,4},{8,10},{10,8},{12,14},{14,12},{16,18},{18,... | collective-permute-start | bytes 589832 | tf_op jit(solution)/shard_map/ppermute | solution.py:259
  12.9 4.0 %collective-permute-done.2.got = bf16[6,128,128]{2,1,0:T(8,128)(2,1)S(1)} collective-permute-done((bf16[6,128,128]{2,1,0:T(8,128)(2,1)S(1)}, bf16[6,128,128]{2,1,0:T(8,128)(2,1)S(1)}, u32[]{:S(2)}, u32[]{:S(2)}) %collective-permute-start.2) | collective-permute-done | bytes 196640 | tf_op jit(solution)/shard_map/ppermute | solution.py:259
  16.9 0.1 sums.3
  17.0 1.8 %collective-permute-start.4 = (bf16[6,128,128]{2,1,0:T(8,128)(2,1)S(1)}, bf16[6,128,128]{2,1,0:T(8,128)(2,1)S(1)}, u32[]{:S(2)}, u32[]{:S(2)}) collective-permute-start(bf16[6,128,128]{2,1,0:T(8,128)(2,1)S(1)} %get-tuple-element.29), channel_id=1, source_target_pairs={{0,2},{2,0},{4,6},{6,4},{8,10},{10,8},{12,14},{14,12},{16,18},{18,... | collective-permute-start | bytes 589832 | tf_op jit(solution)/shard_map/ppermute | solution.py:259
  18.7 0.0 collective-permute-done.1.got
  18.7 0.1 sums.2
  18.8 1.6 %collective-permute-start.3 = (bf16[6,128,128]{2,1,0:T(8,128)(2,1)S(1)}, bf16[6,128,128]{2,1,0:T(8,128)(2,1)S(1)}, u32[]{:S(2)}, u32[]{:S(2)}) collective-permute-start(bf16[6,128,128]{2,1,0:T(8,128)(2,1)S(1)} %get-tuple-element.28), channel_id=1, source_target_pairs={{0,4},{2,6},{4,0},{6,2},{8,12},{10,14},{12,8},{14,10},{16,20},{18,... | collective-permute-start | bytes 589832 | tf_op jit(solution)/shard_map/ppermute | solution.py:259
  20.4 3.3 %collective-permute-done.4.other_b = bf16[6,128,128]{2,1,0:T(8,128)(2,1)S(1)} collective-permute-done((bf16[6,128,128]{2,1,0:T(8,128)(2,1)S(1)}, bf16[6,128,128]{2,1,0:T(8,128)(2,1)S(1)}, u32[]{:S(2)}, u32[]{:S(2)}) %collective-permute-start.4) | collective-permute-done | bytes 196640 | tf_op jit(solution)/shard_map/ppermute | solution.py:259
  23.7 1.3 %collective-permute-done.3.other_a = bf16[6,128,128]{2,1,0:T(8,128)(2,1)S(1)} collective-permute-done((bf16[6,128,128]{2,1,0:T(8,128)(2,1)S(1)}, bf16[6,128,128]{2,1,0:T(8,128)(2,1)S(1)}, u32[]{:S(2)}, u32[]{:S(2)}) %collective-permute-start.3) | collective-permute-done | bytes 196640 | tf_op jit(solution)/shard_map/ppermute | solution.py:259
  24.9 0.7 %planes.1 = (f32[3,128,128]{2,1,0:T(8,128)S(1)}, bf16[3,128,128]{2,1,0:T(8,128)(2,1)S(1)}, bf16[3,128,128]{2,1,0:T(8,128)(2,1)S(1)}, bf16[3,128,128]{2,1,0:T(8,128)(2,1)S(1)}) custom-call(s32[29]{0:T(128)S(1)} %get-tuple-element.20.place, f32[6,128,128]{2,1,0:T(8,128)S(1)} %get-tuple-element.25.sum_a, f32[6,128,128]{2,1,0:T(8,128)S(1)} %get-tuple-element.27.sum_b, ...), custom_call_target="tpu_custom_call" | custom-call | tf_op jit(solution)/shard_map/planes/pallas_call | solution.py:313
  25.7 1.7 %collective-permute-start.5 = (bf16[3,128,128]{2,1,0:T(8,128)(2,1)S(1)}, bf16[3,128,128]{2,1,0:T(8,128)(2,1)S(1)}, u32[]{:S(2)}, u32[]{:S(2)}) collective-permute-start(bf16[3,128,128]{2,1,0:T(8,128)(2,1)S(1)} %get-tuple-element.31), channel_id=1, source_target_pairs={{0,8},{2,10},{4,12},{6,14},{8,0},{10,2},{12,4},{14,6},{16,24},{18,... | collective-permute-start | bytes 294920 | tf_op jit(solution)/shard_map/ppermute | solution.py:259
  27.3 2.6 %collective-permute-start.6 = (bf16[3,128,128]{2,1,0:T(8,128)(2,1)S(1)}, bf16[3,128,128]{2,1,0:T(8,128)(2,1)S(1)}, u32[]{:S(2)}, u32[]{:S(2)}) collective-permute-start(bf16[3,128,128]{2,1,0:T(8,128)(2,1)S(1)} %get-tuple-element.32), channel_id=1, source_target_pairs={{0,16},{2,18},{4,20},{6,22},{8,24},{10,26},{12,28},{14,30},{16,0},... | collective-permute-start | bytes 294920 | tf_op jit(solution)/shard_map/ppermute | solution.py:259
  29.9 0.2 collective-permute-start.7
  30.1 0.9 %collective-permute-done.5.rest_0_ = bf16[3,128,128]{2,1,0:T(8,128)(2,1)S(1)} collective-permute-done((bf16[3,128,128]{2,1,0:T(8,128)(2,1)S(1)}, bf16[3,128,128]{2,1,0:T(8,128)(2,1)S(1)}, u32[]{:S(2)}, u32[]{:S(2)}) %collective-permute-start.5) | collective-permute-done | bytes 98336 | tf_op jit(solution)/shard_map/ppermute | solution.py:259
  31.0 4.3 %collective-permute-done.6.rest_1_ = bf16[3,128,128]{2,1,0:T(8,128)(2,1)S(1)} collective-permute-done((bf16[3,128,128]{2,1,0:T(8,128)(2,1)S(1)}, bf16[3,128,128]{2,1,0:T(8,128)(2,1)S(1)}, u32[]{:S(2)}, u32[]{:S(2)}) %collective-permute-start.6) | collective-permute-done | bytes 98336 | tf_op jit(solution)/shard_map/ppermute | solution.py:259
  35.3 1.1 %collective-permute-done.7.rest_2_ = bf16[3,128,128]{2,1,0:T(8,128)(2,1)S(1)} collective-permute-done((bf16[3,128,128]{2,1,0:T(8,128)(2,1)S(1)}, bf16[3,128,128]{2,1,0:T(8,128)(2,1)S(1)}, u32[]{:S(2)}, u32[]{:S(2)}) %collective-permute-start.7) | collective-permute-done | bytes 98336 | tf_op jit(solution)/shard_map/ppermute | solution.py:259
  36.4 1.5 %update.1 = (f32[3,128,128]{2,1,0:T(8,128)}, f32[3,128,128]{2,1,0:T(8,128)}, f32[3,128,128]{2,1,0:T(8,128)}) custom-call(s32[29]{0:T(128)S(1)} %get-tuple-element.20.place, f32[3,128,128]{2,1,0:T(8,128)S(1)} %get-tuple-element.30.kept, bf16[3,128,128]{2,1,0:T(8,128)(2,1)S(1)} %collective-permute-done.5.rest_0_, ...), custom_call_target="tpu_custom_call" | custom-call | tf_op jit(solution)/shard_map/update/pallas_call | solution.py:332
Async XLA Ops:
  0.6 6.4 %collective-permute-start = (bf16[256,4096]{1,0:T(8,128)(2,1)}, bf16[256,4096]{1,0:T(8,128)(2,1)S(1)}, u32[]{:S(2)}, u32[]{:S(2)}) collective-permute-start(bf16[256,4096]{1,0:T(8,128)(2,1)} %features.1), channel_id=1, source_target_pairs={{0,1},{1,0},{2,3},{3,2},{4,5},{5,4},{6,7},{7,6},{8,9},{9,8},{10,11... | collective-permute-start | bytes 6291464 | tf_op jit(solution)/shard_map/ppermute | solution.py:264
  1.2 0.7 %copy-start = (s32[16,3]{0,1:T(4,128)S(1)}, s32[16,3]{0,1:T(4,128)}, u32[]{:S(2)}) copy-start(s32[16,3]{0,1:T(4,128)} %param.13) | copy-start | bytes 580
  1.9 0.7 %copy-start.2 = (s32[16]{0:T(128)S(1)}, s32[16]{0:T(128)}, u32[]{:S(2)}) copy-start(s32[16]{0:T(128)} %own.1) | copy-start | bytes 196
  2.5 4.5 %copy-start.1 = (s32[16,3]{0,1:T(4,128)S(1)}, s32[16,3]{0,1:T(4,128)}, u32[]{:S(2)}) copy-start(s32[16,3]{0,1:T(4,128)} %param.13) | copy-start | bytes 580
  8.8 8.1 %collective-permute-start.2 = (bf16[6,128,128]{2,1,0:T(8,128)(2,1)S(1)}, bf16[6,128,128]{2,1,0:T(8,128)(2,1)S(1)}, u32[]{:S(2)}, u32[]{:S(2)}) collective-permute-start(bf16[6,128,128]{2,1,0:T(8,128)(2,1)S(1)} %get-tuple-element.26), channel_id=1, source_target_pairs={{0,4},{2,6},{4,0},{6,2},{8,12},{10,14},{12,8},{14,10},{16,20},{18,... | collective-permute-start | bytes 589832 | tf_op jit(solution)/shard_map/ppermute | solution.py:259
  11.4 7.3 %collective-permute-start.1 = (bf16[6,128,128]{2,1,0:T(8,128)(2,1)S(1)}, bf16[6,128,128]{2,1,0:T(8,128)(2,1)S(1)}, u32[]{:S(2)}, u32[]{:S(2)}) collective-permute-start(bf16[6,128,128]{2,1,0:T(8,128)(2,1)S(1)} %get-tuple-element.24), channel_id=1, source_target_pairs={{0,2},{2,0},{4,6},{6,4},{8,10},{10,8},{12,14},{14,12},{16,18},{18,... | collective-permute-start | bytes 589832 | tf_op jit(solution)/shard_map/ppermute | solution.py:259
  17.0 6.7 %collective-permute-start.4 = (bf16[6,128,128]{2,1,0:T(8,128)(2,1)S(1)}, bf16[6,128,128]{2,1,0:T(8,128)(2,1)S(1)}, u32[]{:S(2)}, u32[]{:S(2)}) collective-permute-start(bf16[6,128,128]{2,1,0:T(8,128)(2,1)S(1)} %get-tuple-element.29), channel_id=1, source_target_pairs={{0,2},{2,0},{4,6},{6,4},{8,10},{10,8},{12,14},{14,12},{16,18},{18,... | collective-permute-start | bytes 589832 | tf_op jit(solution)/shard_map/ppermute | solution.py:259
  18.8 6.1 %collective-permute-start.3 = (bf16[6,128,128]{2,1,0:T(8,128)(2,1)S(1)}, bf16[6,128,128]{2,1,0:T(8,128)(2,1)S(1)}, u32[]{:S(2)}, u32[]{:S(2)}) collective-permute-start(bf16[6,128,128]{2,1,0:T(8,128)(2,1)S(1)} %get-tuple-element.28), channel_id=1, source_target_pairs={{0,4},{2,6},{4,0},{6,2},{8,12},{10,14},{12,8},{14,10},{16,20},{18,... | collective-permute-start | bytes 589832 | tf_op jit(solution)/shard_map/ppermute | solution.py:259
  25.7 5.3 %collective-permute-start.5 = (bf16[3,128,128]{2,1,0:T(8,128)(2,1)S(1)}, bf16[3,128,128]{2,1,0:T(8,128)(2,1)S(1)}, u32[]{:S(2)}, u32[]{:S(2)}) collective-permute-start(bf16[3,128,128]{2,1,0:T(8,128)(2,1)S(1)} %get-tuple-element.31), channel_id=1, source_target_pairs={{0,8},{2,10},{4,12},{6,14},{8,0},{10,2},{12,4},{14,6},{16,24},{18,... | collective-permute-start | bytes 294920 | tf_op jit(solution)/shard_map/ppermute | solution.py:259
  27.3 8.0 %collective-permute-start.6 = (bf16[3,128,128]{2,1,0:T(8,128)(2,1)S(1)}, bf16[3,128,128]{2,1,0:T(8,128)(2,1)S(1)}, u32[]{:S(2)}, u32[]{:S(2)}) collective-permute-start(bf16[3,128,128]{2,1,0:T(8,128)(2,1)S(1)} %get-tuple-element.32), channel_id=1, source_target_pairs={{0,16},{2,18},{4,20},{6,22},{8,24},{10,26},{12,28},{14,30},{16,0},... | collective-permute-start | bytes 294920 | tf_op jit(solution)/shard_map/ppermute | solution.py:259
  29.9 6.5 %collective-permute-start.7 = (bf16[3,128,128]{2,1,0:T(8,128)(2,1)S(1)}, bf16[3,128,128]{2,1,0:T(8,128)(2,1)S(1)}, u32[]{:S(2)}, u32[]{:S(2)}) collective-permute-start(bf16[3,128,128]{2,1,0:T(8,128)(2,1)S(1)} %get-tuple-element.33), channel_id=1, source_target_pairs={{0,24},{2,26},{4,28},{6,30},{8,16},{10,18},{12,20},{14,22},{16,8},... | collective-permute-start | bytes 294920 | tf_op jit(solution)/shard_map/ppermute | solution.py:259

commit v3 on v2

--- a/solution.py
+++ b/solution.py
@@ -25,7 +25,7 @@
     return max(-(-listed // 3), -(-crowd // 2))
 
 
-def route(own, place, seen, work, *, capacity, slots):
+def route(blk, own, place, seen, work, *, capacity, slots):
     listed = own.shape[0]
     replicas = seen.shape[0]
     me = lax.axis_index("dp")
@@ -66,7 +66,7 @@
         work[bin_b] = load_b + n - take
 
     def clear_place(j, carry):
-        place[listed + j] = 0
+        place[2 * listed + j] = 0
         return carry
 
     lax.fori_loop(0, replicas // COLUMNS * capacity, clear_place, 0)
@@ -83,12 +83,13 @@
         mine = jnp.where(in_a, my_bit[0], my_bit[1])
         keep = (bit == mine).astype(jnp.int32)
         place[k] = jnp.where(in_a, 0, 2 * slots) + keep * slots + slot
+        place[listed + k] = blk[1, k]
         s = seen[o]
         seen[o] = s + 1
 
         @pl.when(q == column)
         def _():
-            place[listed + o // COLUMNS * capacity + s] = jnp.where(in_a, 0, slots) + slot
+            place[2 * listed + o // COLUMNS * capacity + s] = jnp.where(in_a, 0, slots) + slot
 
         return carry
 
@@ -96,12 +97,13 @@
     place[place.shape[0] - 1] = seen[me]
 
 
-def act_kernel(blk, own, features, gate, up, cot, *rest, capacity, slots):
+def act_kernel(blk_hbm, own_hbm, features, gate, up, cot, *rest, capacity, slots):
     states, rest = rest[:3], rest[3:]
     act, rows, place = rest[:3]
-    held, (gbuf, ubuf, cbuf, sems, state_sems, seen, work) = rest[3:6], rest[6:]
+    held, (gbuf, ubuf, cbuf, blk, own, sems, state_sems, seen, work) = rest[3:6], rest[6:]
     listed, tokens, size = act.shape
     per = features.shape[1] // size
+    mine = lax.axis_index("tensor")
 
     def row_copy(k):
         cols = pl.ds(pl.multiple_of(lax.rem(blk[1, k], per) * size, size), size)
@@ -115,28 +117,41 @@
         ]
 
     def begin(k, carry):
-        for copy in copies(k):
-            copy.start()
+        gated = blk[0, k] == 0
+        first, second, third = copies(k)
+        first.start()
+        third.start()
+        pl.when(gated)(second.start)
         return carry
 
     def begin_rows(k, carry):
-        row_copy(k).start()
-        return carry
-
-    lax.fori_loop(0, listed, begin, 0)
-    lax.fori_loop(0, listed, begin_rows, 0)
+        pl.when(blk[1, k] // per == mine)(row_copy(k).start)
+        return carry
+
+    tables = [
+        pltpu.make_async_copy(blk_hbm, blk, state_sems.at[3]),
+        pltpu.make_async_copy(own_hbm, own, state_sems.at[4]),
+    ]
+    for copy in tables:
+        copy.start()
+    tables[0].wait()
+    lax.fori_loop(0, listed, begin, 0, unroll=2)
+    lax.fori_loop(0, listed, begin_rows, 0, unroll=2)
     state_copies = [
         pltpu.make_async_copy(src, dst, state_sems.at[i])
         for i, (src, dst) in enumerate(zip(states, held))
     ]
     for copy in state_copies:
         copy.start()
-    route(own, place, seen, work, capacity=capacity, slots=slots)
+    tables[1].wait()
+    route(blk, own, place, seen, work, capacity=capacity, slots=slots)
 
     def compute(k, carry):
-        for copy in copies(k):
-            copy.wait()
         gated = blk[0, k] == 0
+        first, second, third = copies(k)
+        first.wait()
+        third.wait()
+        pl.when(gated)(second.wait)
         g = gbuf[k].astype(jnp.float32)
         c = cbuf[k].astype(jnp.float32)
         s = jax.nn.sigmoid(g)
@@ -144,10 +159,10 @@
         act[k] = (first * jnp.where(gated, s * (1.0 + g * (1.0 - s)), g * s)).astype(act.dtype)
         return carry
 
-    lax.fori_loop(0, listed, compute, 0)
+    lax.fori_loop(0, listed, compute, 0, unroll=2)
 
     def end_rows(k, carry):
-        row_copy(k).wait()
+        pl.when(blk[1, k] // per == mine)(row_copy(k).wait)
         return carry
 
     lax.fori_loop(0, listed, end_rows, 0)
@@ -155,7 +170,7 @@
         copy.wait()
 
 
-def product_kernel(blk, place, act, rows, *rest, shards, slots):
+def product_kernel(place, act, rows, *rest, shards, slots):
     others = rest[: shards - 1]
     send_a, send_b, part = rest[shards - 1 :]
     listed, tokens, size = act.shape
@@ -163,7 +178,7 @@
     mine = lax.axis_index("tensor")
 
     def compute(k, carry):
-        r = blk[1, k]
+        r = place[listed + k]
         cols = pl.ds(pl.multiple_of(lax.rem(r, per) * size, size), size)
         source = lax.rem(mine + shards - r // per, shards)
         lhs = rows[k]
@@ -174,7 +189,7 @@
         )
         return carry
 
-    lax.fori_loop(0, listed, compute, 0, unroll=4)
+    lax.fori_loop(0, listed, compute, 0, unroll=16)
     send_a[...] = part[:slots].astype(send_a.dtype)
     send_b[...] = part[2 * slots : 3 * slots].astype(send_b.dtype)
 
@@ -190,7 +205,7 @@
     plane = lax.axis_index("dp") // COLUMNS
 
     def total(z, s):
-        j = place[listed + z * capacity + s]
+        j = place[2 * listed + z * capacity + s]
         a = jnp.minimum(j, slots - 1)
         b = jnp.maximum(j - slots, 0)
         return jnp.where(
@@ -252,7 +267,6 @@
     planes = replicas // COLUMNS
     slots = bin_slots(listed, replicas, capacity)
     bf16, f32 = jnp.bfloat16, jnp.float32
-    table = blocks.T
     block = size * size
     column = tokens * size
     in_vmem = lambda n, dtype: pltpu.VMEM((n, size, size), dtype)
@@ -269,31 +283,33 @@
         out_shape=(
             pltpu.VMEM((listed, tokens, size), bf16),
             pltpu.VMEM((listed, tokens, size), bf16),
-            jax.ShapeDtypeStruct((listed + planes * capacity + 1,), jnp.int32),
+            pltpu.SMEM((2 * listed + planes * capacity + 1,), jnp.int32),
         )
         + (in_vmem(capacity, f32),) * 3,
-        in_specs=[SMEM, SMEM] + [HBM] * 7,
+        in_specs=[HBM] * 9,
         out_specs=(VMEM, VMEM, SMEM, VMEM, VMEM, VMEM),
         scratch_shapes=[pltpu.VMEM((listed, tokens, size), bf16)] * 3
         + [
+            pltpu.SMEM((3, listed), jnp.int32),
+            pltpu.SMEM((listed,), jnp.int32),
             pltpu.SemaphoreType.DMA((4, listed)),
-            pltpu.SemaphoreType.DMA((3,)),
+            pltpu.SemaphoreType.DMA((5,)),
             pltpu.SMEM((replicas,), jnp.int32),
             pltpu.SMEM((6 * COLUMNS,), jnp.int32),
         ],
         compiler_params=grant(5 * listed * column * 2 + 3 * capacity * block * 4),
         name="activations",
-    )(table, owner, *map(stay, (features, gate_pre, up_pre, grad_hidden, weights, moment1, moment2)))
+    )(*map(stay, (blocks.T, owner, features, gate_pre, up_pre, grad_hidden, weights, moment1, moment2)))
     send_a, send_b, part = pl.pallas_call(
         functools.partial(product_kernel, shards=shards, slots=slots),
         out_shape=(in_vmem(slots, bf16), in_vmem(slots, bf16), in_vmem(4 * slots, f32)),
-        in_specs=[SMEM, SMEM] + [VMEM] * (shards + 1),
+        in_specs=[SMEM] + [VMEM] * (shards + 1),
         out_specs=(VMEM, VMEM, VMEM),
         compiler_params=grant(
             2 * listed * column * 2 + (shards - 1) * features.size * 2 + 20 * slots * block
         ),
         name="products",
-    )(table, place, act, rows, *others)
+    )(place, act, rows, *others)
 
     def add(got, start):
         return pl.pallas_call(

time: 38.2 us -> 33.9 us (0.89)
  Pallas kernels: 8.65 us -> 5.83 us
  local copies, waits for them, and re-layouts: 1.34 us -> 0 us
  waiting for transfers between devices: 14.8 us -> 14.3 us
  starting transfers between devices: 12.4 us -> 12.8 us
    unnamed x6 -> x0, local copies, waits for them, and re-layouts: 1.34 us -> none
    pallas_call x1, Pallas kernels: 1.81 us -> 0.62 us  [local(): pl.pallas_call(functools.partial(product_kernel, shards=shards, slots=slo...]
    pallas_call x1, Pallas kernels: 0.75 us -> 0.14 us  [local(): pl.pallas_call(functools.partial(plane_kernel, listed=listed, capacity=ca...]
    pallas_call x1, Pallas kernels: 1.51 us -> 0.96 us  [local(): pl.pallas_call(functools.partial(update_kernel, count=len(parts)), out_sh...]
    ppermute x7, waiting for transfers between devices: 14.8 us -> 14.3 us  [local(): lax.ppermute(v, 'dp', [(i, i ^ bit) for i in range(replicas)])]
    pallas_call x1, Pallas kernels: 4.45 us -> 3.98 us  [local(): pl.pallas_call(functools.partial(act_kernel, capacity=capacity, slots=slo...]
where the time goes in v3:
time: 33.9 us; the launch traced here: 33.6 us
  waiting for transfers between devices  14.3 us (42%)
  starting transfers between devices  12.8 us (38%)
  Pallas kernels  5.83 us (17%)
  between operations  0.67 us (2%)
    ppermute x7, waiting for transfers between devices, local(): lax.ppermute(v, 'dp', [(i, i ^ bit) for i in range(replicas)])  14.3 us
    ppermute x7, starting transfers between devices, local(): lax.ppermute(v, 'dp', [(i, i ^ bit) for i in range(replicas)])  12.2 us
    pallas_call x1, Pallas kernels, local(): pl.pallas_call(functools.partial(act_kernel, capacity=capacity, slots=slo...  3.98 us
    pallas_call x1, Pallas kernels, local(): pl.pallas_call(functools.partial(update_kernel, count=len(parts)), out_sh...  0.96 us
  transfers between devices with their start and end apart: 8, of which 6 were waited for; matrix products, arithmetic and copies ran while one was open for 0% of the time, Pallas kernels for 12%

profile of v3, /device:TPU:0, one launch (start us, length us, event | category | flops | bytes accessed | tf_op | source)
XLA Modules:
  0.0 33.6 jit_solution(8692719292085739245)
XLA Ops:
  0.6 0.6 %collective-permute-start = (bf16[256,4096]{1,0:T(8,128)(2,1)}, bf16[256,4096]{1,0:T(8,128)(2,1)S(1)}, u32[]{:S(2)}, u32[]{:S(2)}) collective-permute-start(bf16[256,4096]{1,0:T(8,128)(2,1)} %features.1), channel_id=1, source_target_pairs={{0,1},{1,0},{2,3},{3,2},{4,5},{5,4},{6,7},{7,6},{8,9},{9,8},{10,11... | collective-permute-start | bytes 6291464 | tf_op jit(solution)/shard_map/ppermute | solution.py:278
  1.2 4.0 %activations.1 = (bf16[16,256,128]{2,1,0:T(8,128)(2,1)S(1)}, bf16[16,256,128]{2,1,0:T(8,128)(2,1)S(1)}, s32[45]{0:T(128)S(4)}, f32[3,128,128]{2,1,0:T(8,128)S(1)...) custom-call(s32[3,16]{1,0:T(4,128)} %bitcast.1, s32[16]{0:T(128)} %own_hbm.1, bf16[256,4096]{1,0:T(8,128)(2,1)} %features.1, ...), custom_call_target="tpu_custom_call" | custom-call | tf_op jit(solution)/shard_map/activations/pallas_call | solution.py:281
  5.2 0.0 collective-permute-done.rest_0_
  5.2 0.6 %products.1 = (bf16[6,128,128]{2,1,0:T(8,128)(2,1)S(1)}, bf16[6,128,128]{2,1,0:T(8,128)(2,1)S(1)}, f32[24,128,128]{2,1,0:T(8,128)S(1)}) custom-call(s32[45]{0:T(128)S(4)} %get-tuple-element.20.place, bf16[16,256,128]{2,1,0:T(8,128)(2,1)S(1)} %get-tuple-element.21.act, bf16[16,256,128]{2,1,0:T(8,128)(2,1)S(1)} %get-tuple-element.22.rows, ...), custom_call_target="tpu_custom_call" | custom-call | tf_op jit(solution)/shard_map/products/pallas_call | solution.py:303
  5.8 2.9 %collective-permute-start.2 = (bf16[6,128,128]{2,1,0:T(8,128)(2,1)S(1)}, bf16[6,128,128]{2,1,0:T(8,128)(2,1)S(1)}, u32[]{:S(2)}, u32[]{:S(2)}) collective-permute-start(bf16[6,128,128]{2,1,0:T(8,128)(2,1)S(1)} %get-tuple-element.26), channel_id=1, source_target_pairs={{0,4},{2,6},{4,0},{6,2},{8,12},{10,14},{12,8},{14,10},{16,20},{18,... | collective-permute-start | bytes 589832 | tf_op jit(solution)/shard_map/ppermute | solution.py:273
  8.8 1.5 %collective-permute-start.1 = (bf16[6,128,128]{2,1,0:T(8,128)(2,1)S(1)}, bf16[6,128,128]{2,1,0:T(8,128)(2,1)S(1)}, u32[]{:S(2)}, u32[]{:S(2)}) collective-permute-start(bf16[6,128,128]{2,1,0:T(8,128)(2,1)S(1)} %get-tuple-element.24), channel_id=1, source_target_pairs={{0,2},{2,0},{4,6},{6,4},{8,10},{10,8},{12,14},{14,12},{16,18},{18,... | collective-permute-start | bytes 589832 | tf_op jit(solution)/shard_map/ppermute | solution.py:273
  10.2 3.7 %collective-permute-done.2.got = bf16[6,128,128]{2,1,0:T(8,128)(2,1)S(1)} collective-permute-done((bf16[6,128,128]{2,1,0:T(8,128)(2,1)S(1)}, bf16[6,128,128]{2,1,0:T(8,128)(2,1)S(1)}, u32[]{:S(2)}, u32[]{:S(2)}) %collective-permute-start.2) | collective-permute-done | bytes 196640 | tf_op jit(solution)/shard_map/ppermute | solution.py:273
  14.0 0.1 sums.3
  14.0 1.8 %collective-permute-start.4 = (bf16[6,128,128]{2,1,0:T(8,128)(2,1)S(1)}, bf16[6,128,128]{2,1,0:T(8,128)(2,1)S(1)}, u32[]{:S(2)}, u32[]{:S(2)}) collective-permute-start(bf16[6,128,128]{2,1,0:T(8,128)(2,1)S(1)} %get-tuple-element.29), channel_id=1, source_target_pairs={{0,2},{2,0},{4,6},{6,4},{8,10},{10,8},{12,14},{14,12},{16,18},{18,... | collective-permute-start | bytes 589832 | tf_op jit(solution)/shard_map/ppermute | solution.py:273
  15.8 0.0 collective-permute-done.1.got
  15.8 0.1 sums.2
  15.9 1.6 %collective-permute-start.3 = (bf16[6,128,128]{2,1,0:T(8,128)(2,1)S(1)}, bf16[6,128,128]{2,1,0:T(8,128)(2,1)S(1)}, u32[]{:S(2)}, u32[]{:S(2)}) collective-permute-start(bf16[6,128,128]{2,1,0:T(8,128)(2,1)S(1)} %get-tuple-element.28), channel_id=1, source_target_pairs={{0,4},{2,6},{4,0},{6,2},{8,12},{10,14},{12,8},{14,10},{16,20},{18,... | collective-permute-start | bytes 589832 | tf_op jit(solution)/shard_map/ppermute | solution.py:273
  17.5 3.0 %collective-permute-done.4.other_b = bf16[6,128,128]{2,1,0:T(8,128)(2,1)S(1)} collective-permute-done((bf16[6,128,128]{2,1,0:T(8,128)(2,1)S(1)}, bf16[6,128,128]{2,1,0:T(8,128)(2,1)S(1)}, u32[]{:S(2)}, u32[]{:S(2)}) %collective-permute-start.4) | collective-permute-done | bytes 196640 | tf_op jit(solution)/shard_map/ppermute | solution.py:273
  20.5 1.3 %collective-permute-done.3.other_a = bf16[6,128,128]{2,1,0:T(8,128)(2,1)S(1)} collective-permute-done((bf16[6,128,128]{2,1,0:T(8,128)(2,1)S(1)}, bf16[6,128,128]{2,1,0:T(8,128)(2,1)S(1)}, u32[]{:S(2)}, u32[]{:S(2)}) %collective-permute-start.3) | collective-permute-done | bytes 196640 | tf_op jit(solution)/shard_map/ppermute | solution.py:273
  21.8 0.1 planes.1
  21.9 1.6 %collective-permute-start.5 = (bf16[3,128,128]{2,1,0:T(8,128)(2,1)S(1)}, bf16[3,128,128]{2,1,0:T(8,128)(2,1)S(1)}, u32[]{:S(2)}, u32[]{:S(2)}) collective-permute-start(bf16[3,128,128]{2,1,0:T(8,128)(2,1)S(1)} %get-tuple-element.31), channel_id=1, source_target_pairs={{0,8},{2,10},{4,12},{6,14},{8,0},{10,2},{12,4},{14,6},{16,24},{18,... | collective-permute-start | bytes 294920 | tf_op jit(solution)/shard_map/ppermute | solution.py:273
  23.5 2.6 %collective-permute-start.6 = (bf16[3,128,128]{2,1,0:T(8,128)(2,1)S(1)}, bf16[3,128,128]{2,1,0:T(8,128)(2,1)S(1)}, u32[]{:S(2)}, u32[]{:S(2)}) collective-permute-start(bf16[3,128,128]{2,1,0:T(8,128)(2,1)S(1)} %get-tuple-element.32), channel_id=1, source_target_pairs={{0,16},{2,18},{4,20},{6,22},{8,24},{10,26},{12,28},{14,30},{16,0},... | collective-permute-start | bytes 294920 | tf_op jit(solution)/shard_map/ppermute | solution.py:273
  26.1 0.2 collective-permute-start.7
  26.4 0.6 %collective-permute-done.5.rest_0_ = bf16[3,128,128]{2,1,0:T(8,128)(2,1)S(1)} collective-permute-done((bf16[3,128,128]{2,1,0:T(8,128)(2,1)S(1)}, bf16[3,128,128]{2,1,0:T(8,128)(2,1)S(1)}, u32[]{:S(2)}, u32[]{:S(2)}) %collective-permute-start.5) | collective-permute-done | bytes 98336 | tf_op jit(solution)/shard_map/ppermute | solution.py:273
  26.9 4.3 %collective-permute-done.6.rest_1_ = bf16[3,128,128]{2,1,0:T(8,128)(2,1)S(1)} collective-permute-done((bf16[3,128,128]{2,1,0:T(8,128)(2,1)S(1)}, bf16[3,128,128]{2,1,0:T(8,128)(2,1)S(1)}, u32[]{:S(2)}, u32[]{:S(2)}) %collective-permute-start.6) | collective-permute-done | bytes 98336 | tf_op jit(solution)/shard_map/ppermute | solution.py:273
  31.2 1.4 %collective-permute-done.7.rest_2_ = bf16[3,128,128]{2,1,0:T(8,128)(2,1)S(1)} collective-permute-done((bf16[3,128,128]{2,1,0:T(8,128)(2,1)S(1)}, bf16[3,128,128]{2,1,0:T(8,128)(2,1)S(1)}, u32[]{:S(2)}, u32[]{:S(2)}) %collective-permute-start.7) | collective-permute-done | bytes 98336 | tf_op jit(solution)/shard_map/ppermute | solution.py:273
  32.6 1.0 %update.1 = (f32[3,128,128]{2,1,0:T(8,128)}, f32[3,128,128]{2,1,0:T(8,128)}, f32[3,128,128]{2,1,0:T(8,128)}) custom-call(s32[45]{0:T(128)S(4)} %get-tuple-element.20.place, f32[3,128,128]{2,1,0:T(8,128)S(1)} %get-tuple-element.30.kept, bf16[3,128,128]{2,1,0:T(8,128)(2,1)S(1)} %collective-permute-done.5.rest_0_, ...), custom_call_target="tpu_custom_call" | custom-call | tf_op jit(solution)/shard_map/update/pallas_call | solution.py:348
Async XLA Ops:
  0.6 4.6 %collective-permute-start = (bf16[256,4096]{1,0:T(8,128)(2,1)}, bf16[256,4096]{1,0:T(8,128)(2,1)S(1)}, u32[]{:S(2)}, u32[]{:S(2)}) collective-permute-start(bf16[256,4096]{1,0:T(8,128)(2,1)} %features.1), channel_id=1, source_target_pairs={{0,1},{1,0},{2,3},{3,2},{4,5},{5,4},{6,7},{7,6},{8,9},{9,8},{10,11... | collective-permute-start | bytes 6291464 | tf_op jit(solution)/shard_map/ppermute | solution.py:278
  5.8 8.1 %collective-permute-start.2 = (bf16[6,128,128]{2,1,0:T(8,128)(2,1)S(1)}, bf16[6,128,128]{2,1,0:T(8,128)(2,1)S(1)}, u32[]{:S(2)}, u32[]{:S(2)}) collective-permute-start(bf16[6,128,128]{2,1,0:T(8,128)(2,1)S(1)} %get-tuple-element.26), channel_id=1, source_target_pairs={{0,4},{2,6},{4,0},{6,2},{8,12},{10,14},{12,8},{14,10},{16,20},{18,... | collective-permute-start | bytes 589832 | tf_op jit(solution)/shard_map/ppermute | solution.py:273
  8.8 7.1 %collective-permute-start.1 = (bf16[6,128,128]{2,1,0:T(8,128)(2,1)S(1)}, bf16[6,128,128]{2,1,0:T(8,128)(2,1)S(1)}, u32[]{:S(2)}, u32[]{:S(2)}) collective-permute-start(bf16[6,128,128]{2,1,0:T(8,128)(2,1)S(1)} %get-tuple-element.24), channel_id=1, source_target_pairs={{0,2},{2,0},{4,6},{6,4},{8,10},{10,8},{12,14},{14,12},{16,18},{18,... | collective-permute-start | bytes 589832 | tf_op jit(solution)/shard_map/ppermute | solution.py:273
  14.0 6.4 %collective-permute-start.4 = (bf16[6,128,128]{2,1,0:T(8,128)(2,1)S(1)}, bf16[6,128,128]{2,1,0:T(8,128)(2,1)S(1)}, u32[]{:S(2)}, u32[]{:S(2)}) collective-permute-start(bf16[6,128,128]{2,1,0:T(8,128)(2,1)S(1)} %get-tuple-element.29), channel_id=1, source_target_pairs={{0,2},{2,0},{4,6},{6,4},{8,10},{10,8},{12,14},{14,12},{16,18},{18,... | collective-permute-start | bytes 589832 | tf_op jit(solution)/shard_map/ppermute | solution.py:273
  15.9 5.9 %collective-permute-start.3 = (bf16[6,128,128]{2,1,0:T(8,128)(2,1)S(1)}, bf16[6,128,128]{2,1,0:T(8,128)(2,1)S(1)}, u32[]{:S(2)}, u32[]{:S(2)}) collective-permute-start(bf16[6,128,128]{2,1,0:T(8,128)(2,1)S(1)} %get-tuple-element.28), channel_id=1, source_target_pairs={{0,4},{2,6},{4,0},{6,2},{8,12},{10,14},{12,8},{14,10},{16,20},{18,... | collective-permute-start | bytes 589832 | tf_op jit(solution)/shard_map/ppermute | solution.py:273
  21.9 5.0 %collective-permute-start.5 = (bf16[3,128,128]{2,1,0:T(8,128)(2,1)S(1)}, bf16[3,128,128]{2,1,0:T(8,128)(2,1)S(1)}, u32[]{:S(2)}, u32[]{:S(2)}) collective-permute-start(bf16[3,128,128]{2,1,0:T(8,128)(2,1)S(1)} %get-tuple-element.31), channel_id=1, source_target_pairs={{0,8},{2,10},{4,12},{6,14},{8,0},{10,2},{12,4},{14,6},{16,24},{18,... | collective-permute-start | bytes 294920 | tf_op jit(solution)/shard_map/ppermute | solution.py:273
  23.5 7.7 %collective-permute-start.6 = (bf16[3,128,128]{2,1,0:T(8,128)(2,1)S(1)}, bf16[3,128,128]{2,1,0:T(8,128)(2,1)S(1)}, u32[]{:S(2)}, u32[]{:S(2)}) collective-permute-start(bf16[3,128,128]{2,1,0:T(8,128)(2,1)S(1)} %get-tuple-element.32), channel_id=1, source_target_pairs={{0,16},{2,18},{4,20},{6,22},{8,24},{10,26},{12,28},{14,30},{16,0},... | collective-permute-start | bytes 294920 | tf_op jit(solution)/shard_map/ppermute | solution.py:273
  26.1 6.5 %collective-permute-start.7 = (bf16[3,128,128]{2,1,0:T(8,128)(2,1)S(1)}, bf16[3,128,128]{2,1,0:T(8,128)(2,1)S(1)}, u32[]{:S(2)}, u32[]{:S(2)}) collective-permute-start(bf16[3,128,128]{2,1,0:T(8,128)(2,1)S(1)} %get-tuple-element.33), channel_id=1, source_target_pairs={{0,24},{2,26},{4,28},{6,30},{8,16},{10,18},{12,20},{14,22},{16,8},... | collective-permute-start | bytes 294920 | tf_op jit(solution)/shard_map/ppermute | solution.py:273

commit v4 on v3

--- a/solution.py
+++ b/solution.py
@@ -20,12 +20,13 @@
 COLUMNS = 4
 
 
-def bin_slots(listed, replicas, capacity):
+def bin_sizes(listed, replicas, capacity):
     crowd = min(listed, capacity * replicas // COLUMNS)
-    return max(-(-listed // 3), -(-crowd // 2))
-
-
-def route(blk, own, place, seen, work, *, capacity, slots):
+    level, most = -(-listed // COLUMNS), max(-(-listed // 3), -(-crowd // 2))
+    return sorted({min(level, most), min(level + max(listed // 16, 1), most), most})
+
+
+def route(blk, own, place, flag, seen, work, *, capacity, sizes):
     listed = own.shape[0]
     replicas = seen.shape[0]
     me = lax.axis_index("dp")
@@ -48,22 +49,44 @@
 
     lax.fori_loop(0, listed, count, 0)
 
-    first, most = jnp.int32(0), work[COUNT]
-    for q in range(1, COLUMNS):
-        n = work[COUNT + q]
-        first = jnp.where(n > most, q, first)
-        most = jnp.maximum(n, most)
-    for i in range(COLUMNS):
-        q = jnp.bitwise_xor(first, i)
-        bin_a = LOAD + lax.rem(q, 2)
-        bin_b = LOAD + 2 + q // 2
-        n, load_a, load_b = work[COUNT + q], work[bin_a], work[bin_b]
-        take = jnp.clip(lax.shift_right_arithmetic(n + load_b - load_a, 1), 0, n)
-        work[TAKE + q] = take
-        work[AT_A + q] = load_a
-        work[AT_B + q] = load_b
-        work[bin_a] = load_a + take
-        work[bin_b] = load_b + n - take
+    n = [work[COUNT + q] for q in range(COLUMNS)]
+
+    def shares(size, a0):
+        a2 = jnp.minimum(n[2], size - a0)
+        a1 = n[1] - jnp.minimum(n[1], size - (n[0] - a0))
+        a3 = jnp.minimum(n[3], size - a1)
+        return a0, a1, a2, a3
+
+    def search(size):
+        low = jnp.maximum(n[0] - size, 0)
+        high = jnp.minimum(n[0], size)
+
+        def attempt(i, best):
+            a = shares(size, low + i)
+            ok = (low + i <= high) & (a[1] <= size) & (n[2] - a[2] + n[3] - a[3] <= size)
+            return jnp.where(ok, low + i, best)
+
+        return lax.fori_loop(0, size + 1, attempt, jnp.int32(-1))
+
+    flag[0] = len(sizes) - 1
+    work[LOAD + 1] = sizes[-1]
+    work[LOAD] = search(sizes[-1])
+    for i in reversed(range(len(sizes) - 1)):
+        best = search(sizes[i])
+
+        @pl.when(best >= 0)
+        def _():
+            flag[0] = i
+            work[LOAD + 1] = sizes[i]
+            work[LOAD] = best
+
+    slots = work[LOAD + 1]
+    a = shares(slots, work[LOAD])
+    for q in range(COLUMNS):
+        work[TAKE + q] = a[q]
+    for q, (at_a, at_b) in enumerate(((0, 0), (0, n[0] - a[0]), (a[0], 0), (a[1], n[2] - a[2]))):
+        work[AT_A + q] = at_a
+        work[AT_B + q] = at_b
 
     def clear_place(j, carry):
         place[2 * listed + j] = 0
@@ -97,11 +120,11 @@
     place[place.shape[0] - 1] = seen[me]
 
 
-def act_kernel(blk_hbm, own_hbm, features, gate, up, cot, *rest, capacity, slots):
+def act_kernel(blk_hbm, own_hbm, features, gate, up, cot, *rest, capacity, sizes):
     states, rest = rest[:3], rest[3:]
-    act, rows, place = rest[:3]
-    held, (gbuf, ubuf, cbuf, blk, own, sems, state_sems, seen, work) = rest[3:6], rest[6:]
-    listed, tokens, size = act.shape
+    act, rows, place, flag = rest[:4]
+    held, (gbuf, ubuf, cbuf, blk, own, sems, state_sems, seen, work) = rest[4:7], rest[7:]
+    listed, _, size = act.shape
     per = features.shape[1] // size
     mine = lax.axis_index("tensor")
 
@@ -144,7 +167,7 @@
     for copy in state_copies:
         copy.start()
     tables[1].wait()
-    route(blk, own, place, seen, work, capacity=capacity, slots=slots)
+    route(blk, own, place, flag, seen, work, capacity=capacity, sizes=sizes)
 
     def compute(k, carry):
         gated = blk[0, k] == 0
@@ -173,7 +196,7 @@
 def product_kernel(place, act, rows, *rest, shards, slots):
     others = rest[: shards - 1]
     send_a, send_b, part = rest[shards - 1 :]
-    listed, tokens, size = act.shape
+    listed, _, size = act.shape
     per = others[0].shape[1] // size
     mine = lax.axis_index("tensor")
 
@@ -265,7 +288,7 @@
     listed = owner.shape[0]
     tokens = features.shape[0]
     planes = replicas // COLUMNS
-    slots = bin_slots(listed, replicas, capacity)
+    sizes = bin_sizes(listed, replicas, capacity)
     bf16, f32 = jnp.bfloat16, jnp.float32
     block = size * size
     column = tokens * size
@@ -278,16 +301,17 @@
         lax.ppermute(features, "tensor", [(i, (i + j) % shards) for i in range(shards)])
         for j in range(1, shards)
     ]
-    act, rows, place, *states = pl.pallas_call(
-        functools.partial(act_kernel, capacity=capacity, slots=slots),
+    act, rows, place, flag, *states = pl.pallas_call(
+        functools.partial(act_kernel, capacity=capacity, sizes=sizes),
         out_shape=(
             pltpu.VMEM((listed, tokens, size), bf16),
             pltpu.VMEM((listed, tokens, size), bf16),
             pltpu.SMEM((2 * listed + planes * capacity + 1,), jnp.int32),
+            pltpu.SMEM((1,), jnp.int32),
         )
         + (in_vmem(capacity, f32),) * 3,
         in_specs=[HBM] * 9,
-        out_specs=(VMEM, VMEM, SMEM, VMEM, VMEM, VMEM),
+        out_specs=(VMEM, VMEM, SMEM, SMEM, VMEM, VMEM, VMEM),
         scratch_shapes=[pltpu.VMEM((listed, tokens, size), bf16)] * 3
         + [
             pltpu.SMEM((3, listed), jnp.int32),
@@ -300,43 +324,49 @@
         compiler_params=grant(5 * listed * column * 2 + 3 * capacity * block * 4),
         name="activations",
     )(*map(stay, (blocks.T, owner, features, gate_pre, up_pre, grad_hidden, weights, moment1, moment2)))
-    send_a, send_b, part = pl.pallas_call(
-        functools.partial(product_kernel, shards=shards, slots=slots),
-        out_shape=(in_vmem(slots, bf16), in_vmem(slots, bf16), in_vmem(4 * slots, f32)),
-        in_specs=[SMEM] + [VMEM] * (shards + 1),
-        out_specs=(VMEM, VMEM, VMEM),
-        compiler_params=grant(
-            2 * listed * column * 2 + (shards - 1) * features.size * 2 + 20 * slots * block
-        ),
-        name="products",
-    )(place, act, rows, *others)
-
-    def add(got, start):
+    direct = planes <= 4 and planes & (planes - 1) == 0
+
+    def plane_sums(slots):
+        send_a, send_b, part = pl.pallas_call(
+            functools.partial(product_kernel, shards=shards, slots=slots),
+            out_shape=(in_vmem(slots, bf16), in_vmem(slots, bf16), in_vmem(4 * slots, f32)),
+            in_specs=[SMEM] + [VMEM] * (shards + 1),
+            out_specs=(VMEM, VMEM, VMEM),
+            compiler_params=grant(
+                2 * listed * column * 2 + (shards - 1) * features.size * 2 + 20 * slots * block
+            ),
+            name="products",
+        )(place, act, rows, *others)
+
+        def add(got, start):
+            return pl.pallas_call(
+                functools.partial(add_kernel, start=start),
+                out_shape=(in_vmem(slots, f32), in_vmem(slots, bf16)),
+                in_specs=[VMEM, VMEM],
+                out_specs=(VMEM, VMEM),
+                compiler_params=grant(24 * slots * block),
+                name="sums",
+            )(part, got)
+
+        sum_a, send_a = add(swap(send_a, 1), slots)
+        sum_b, send_b = add(swap(send_b, 2), 3 * slots)
+        other_a = swap(send_a, 2)
+        other_b = swap(send_b, 1)
         return pl.pallas_call(
-            functools.partial(add_kernel, start=start),
-            out_shape=(in_vmem(slots, f32), in_vmem(slots, bf16)),
-            in_specs=[VMEM, VMEM],
-            out_specs=(VMEM, VMEM),
-            compiler_params=grant(24 * slots * block),
-            name="sums",
-        )(part, got)
-
-    sum_a, send_a = add(swap(send_a, 1), slots)
-    sum_b, send_b = add(swap(send_b, 2), 3 * slots)
-    other_a = swap(send_a, 2)
-    other_b = swap(send_b, 1)
-    direct = planes <= 4 and planes & (planes - 1) == 0
-    kept, *sends = pl.pallas_call(
-        functools.partial(plane_kernel, listed=listed, capacity=capacity),
-        out_shape=(in_vmem(capacity, f32),)
-        + ((in_vmem(capacity, bf16),) * (planes - 1) if direct else (in_vmem(planes * capacity, bf16),)),
-        in_specs=[SMEM, VMEM, VMEM, VMEM, VMEM],
-        out_specs=(VMEM,) * (planes if direct else 2),
-        compiler_params=grant((12 * slots + (4 + 2 * planes) * capacity) * block),
-        name="planes",
-    )(place, sum_a, sum_b, other_a, other_b)
+            functools.partial(plane_kernel, listed=listed, capacity=capacity),
+            out_shape=(in_vmem(capacity, f32),)
+            + ((in_vmem(capacity, bf16),) * (planes - 1) if direct else (in_vmem(planes * capacity, bf16),)),
+            in_specs=[SMEM, VMEM, VMEM, VMEM, VMEM],
+            out_specs=(VMEM,) * (planes if direct else 2),
+            compiler_params=grant((12 * slots + (4 + 2 * planes) * capacity) * block),
+            name="planes",
+        )(place, sum_a, sum_b, other_a, other_b)
+
+    kept, *sends = lax.switch(flag[0], [functools.partial(plane_sums, n) for n in sizes])
     if direct:
-        parts = [swap(send, (k + 1) * COLUMNS) for k, send in enumerate(sends)]
+        parts = []
+        for k, send in enumerate(sends):
+            parts.append(swap(send, (k + 1) * COLUMNS))
     else:
         groups = [[z * COLUMNS + c for z in range(planes)] for c in range(COLUMNS)]
         incoming = lax.all_to_all(

time: 33.9 us -> 31.7 us (0.935)
  waiting for transfers between devices: 14.3 us -> 12.3 us
    ppermute x7, waiting for transfers between devices: 14.3 us -> 12.3 us  [local(): lax.ppermute(v, 'dp', [(i, i ^ bit) for i in range(replicas)])]
  transfers between devices with their start and end apart: 8 -> 8, of which waited for: 6 -> 6; matrix products, arithmetic and copies ran while one was open for 0% -> 0% of each run, Pallas kernels for 12% -> 13%
where the time goes in v4:
time: 31.7 us; the launch traced here: 31.5 us
  starting transfers between devices  12.6 us (40%)
  waiting for transfers between devices  12.3 us (39%)
  Pallas kernels  5.95 us (19%)
  between operations  0.67 us (2%)
    ppermute x7, waiting for transfers between devices, local(): lax.ppermute(v, 'dp', [(i, i ^ bit) for i in range(replicas)])  12.3 us
    ppermute x7, starting transfers between devices, local(): lax.ppermute(v, 'dp', [(i, i ^ bit) for i in range(replicas)])  12 us
    pallas_call x1, Pallas kernels, local(): pl.pallas_call(functools.partial(act_kernel, capacity=capacity, sizes=siz...  4.17 us
    pallas_call x1, Pallas kernels, local(): pl.pallas_call(functools.partial(update_kernel, count=len(parts)), out_sh...  0.96 us
  transfers between devices with their start and end apart: 8, of which 6 were waited for; matrix products, arithmetic and copies ran while one was open for 0% of the time, Pallas kernels for 13%

profile of v4, /device:TPU:0, one launch (start us, length us, event | category | flops | bytes accessed | tf_op | source)
XLA Modules:
  0.0 31.5 jit_solution(5905717454239991471)
XLA Ops:
  0.6 0.6 %collective-permute-start.12 = (bf16[256,4096]{1,0:T(8,128)(2,1)}, bf16[256,4096]{1,0:T(8,128)(2,1)S(1)}, u32[]{:S(2)}, u32[]{:S(2)}) collective-permute-start(bf16[256,4096]{1,0:T(8,128)(2,1)} %features.1), channel_id=1, source_target_pairs={{0,1},{1,0},{2,3},{3,2},{4,5},{5,4},{6,7},{7,6},{8,9},{9,8},{10,11... | collective-permute-start | bytes 6291464 | tf_op jit(solution)/shard_map/ppermute | solution.py:301
  1.2 4.2 %activations.1 = (bf16[16,256,128]{2,1,0:T(8,128)(2,1)S(1)}, bf16[16,256,128]{2,1,0:T(8,128)(2,1)S(1)}, s32[45]{0:T(128)S(4)}, s32[1]{0:T(128)S(4)}, f32[3,128,1...) custom-call(s32[3,16]{1,0:T(4,128)} %bitcast.2, s32[16]{0:T(128)} %own_hbm.1, ...), custom_call_target="tpu_custom_call" | custom-call | tf_op jit(solution)/shard_map/activations/pallas_call | solution.py:304
  5.4 0.0 collective-permute-done.12
  5.4 14.4 %conditional.1 = ((f32[3,128,128]{2,1,0:T(8,128)S(1)}, bf16[3,128,128]{2,1,0:T(8,128)(2,1)S(1)}, bf16[3,128,128]{2,1,0:T(8,128)(2,1)S(1)}, bf16[3,128,128]{2,1,0:T(8,128)(2,1)S(1)})) conditional(s32[]{:T(128)} %bitcast.1, (s32[45]{0:T(128)S(4)}, bf16[16,256,128]{2,1,0:T(8,128)(2,1)S(1)}, bf16[16,256,128]{2,1,0:T(8,128)(2,1)S(1)}, ...), branch_computations={%region_0.0_spmd, %region_1.0_spmd, %region_2.0_spmd} | conditional | bytes 11534532 | solution.py:365
  5.4 0.6 %products.3 = (bf16[4,128,128]{2,1,0:T(8,128)(2,1)S(1)}, bf16[4,128,128]{2,1,0:T(8,128)(2,1)S(1)}, f32[16,128,128]{2,1,0:T(8,128)S(1)}) custom-call(s32[45]{0:T(128)S(4)} %get-tuple-element.24.place, bf16[16,256,128]{2,1,0:T(8,128)(2,1)S(1)} %get-tuple-element.25.act, bf16[16,256,128]{2,1,0:T(8,128)(2,1)S(1)} %get-tuple-element.26.rows, ...), custom_call_target="tpu_custom_call" | custom-call | tf_op jit(solution)/shard_map/cond/branch_0_fun/products/pallas_call | solution.py:330
  6.0 2.7 %collective-permute-start.1 = (bf16[4,128,128]{2,1,0:T(8,128)(2,1)S(1)}, bf16[4,128,128]{2,1,0:T(8,128)(2,1)S(1)}, u32[]{:S(2)}, u32[]{:S(2)}) collective-permute-start(bf16[4,128,128]{2,1,0:T(8,128)(2,1)S(1)} %get-tuple-element.31), channel_id=1, source_target_pairs={{0,4},{2,6},{4,0},{6,2},{8,12},{10,14},{12,8},{14,10},{16,20},{18,... | collective-permute-start | bytes 393224 | tf_op jit(solution)/shard_map/cond/branch_0_fun/ppermute | solution.py:296
  8.7 1.5 %collective-permute-start = (bf16[4,128,128]{2,1,0:T(8,128)(2,1)S(1)}, bf16[4,128,128]{2,1,0:T(8,128)(2,1)S(1)}, u32[]{:S(2)}, u32[]{:S(2)}) collective-permute-start(bf16[4,128,128]{2,1,0:T(8,128)(2,1)S(1)} %get-tuple-element.29), channel_id=1, source_target_pairs={{0,2},{2,0},{4,6},{6,4},{8,10},{10,8},{12,14},{14,12},{16,18},{18,... | collective-permute-start | bytes 393224 | tf_op jit(solution)/shard_map/cond/branch_0_fun/ppermute | solution.py:296
  10.2 2.5 %collective-permute-done.1.got = bf16[4,128,128]{2,1,0:T(8,128)(2,1)S(1)} collective-permute-done((bf16[4,128,128]{2,1,0:T(8,128)(2,1)S(1)}, bf16[4,128,128]{2,1,0:T(8,128)(2,1)S(1)}, u32[]{:S(2)}, u32[]{:S(2)}) %collective-permute-start.1) | collective-permute-done | bytes 131104 | tf_op jit(solution)/shard_map/cond/branch_0_fun/ppermute | solution.py:296
  12.8 1.8 %collective-permute-start.3 = (bf16[4,128,128]{2,1,0:T(8,128)(2,1)S(1)}, bf16[4,128,128]{2,1,0:T(8,128)(2,1)S(1)}, u32[]{:S(2)}, u32[]{:S(2)}) collective-permute-start(bf16[4,128,128]{2,1,0:T(8,128)(2,1)S(1)} %get-tuple-element.34), channel_id=1, source_target_pairs={{0,2},{2,0},{4,6},{6,4},{8,10},{10,8},{12,14},{14,12},{16,18},{18,... | collective-permute-start | bytes 393224 | tf_op jit(solution)/shard_map/cond/branch_0_fun/ppermute | solution.py:296
  14.6 0.0 collective-permute-done.got
  14.6 1.6 %collective-permute-start.2 = (bf16[4,128,128]{2,1,0:T(8,128)(2,1)S(1)}, bf16[4,128,128]{2,1,0:T(8,128)(2,1)S(1)}, u32[]{:S(2)}, u32[]{:S(2)}) collective-permute-start(bf16[4,128,128]{2,1,0:T(8,128)(2,1)S(1)} %get-tuple-element.33), channel_id=1, source_target_pairs={{0,4},{2,6},{4,0},{6,2},{8,12},{10,14},{12,8},{14,10},{16,20},{18,... | collective-permute-start | bytes 393224 | tf_op jit(solution)/shard_map/cond/branch_0_fun/ppermute | solution.py:296
  16.2 1.8 %collective-permute-done.3.other_b = bf16[4,128,128]{2,1,0:T(8,128)(2,1)S(1)} collective-permute-done((bf16[4,128,128]{2,1,0:T(8,128)(2,1)S(1)}, bf16[4,128,128]{2,1,0:T(8,128)(2,1)S(1)}, u32[]{:S(2)}, u32[]{:S(2)}) %collective-permute-start.3) | collective-permute-done | bytes 131104 | tf_op jit(solution)/shard_map/cond/branch_0_fun/ppermute | solution.py:296
  18.0 1.6 %collective-permute-done.2.other_a = bf16[4,128,128]{2,1,0:T(8,128)(2,1)S(1)} collective-permute-done((bf16[4,128,128]{2,1,0:T(8,128)(2,1)S(1)}, bf16[4,128,128]{2,1,0:T(8,128)(2,1)S(1)}, u32[]{:S(2)}, u32[]{:S(2)}) %collective-permute-start.2) | collective-permute-done | bytes 131104 | tf_op jit(solution)/shard_map/cond/branch_0_fun/ppermute | solution.py:296
  19.6 0.1 planes.3
  19.8 1.6 %collective-permute-start.13 = (bf16[3,128,128]{2,1,0:T(8,128)(2,1)S(1)}, bf16[3,128,128]{2,1,0:T(8,128)(2,1)S(1)}, u32[]{:S(2)}, u32[]{:S(2)}) collective-permute-start(bf16[3,128,128]{2,1,0:T(8,128)(2,1)S(1)} %get-tuple-element.76), channel_id=1, source_target_pairs={{0,8},{2,10},{4,12},{6,14},{8,0},{10,2},{12,4},{14,6},{16,24},{18,... | collective-permute-start | bytes 294920 | tf_op jit(solution)/shard_map/ppermute | solution.py:296
  21.4 2.6 %collective-permute-start.14 = (bf16[3,128,128]{2,1,0:T(8,128)(2,1)S(1)}, bf16[3,128,128]{2,1,0:T(8,128)(2,1)S(1)}, u32[]{:S(2)}, u32[]{:S(2)}) collective-permute-start(bf16[3,128,128]{2,1,0:T(8,128)(2,1)S(1)} %get-tuple-element.77), channel_id=1, source_target_pairs={{0,16},{2,18},{4,20},{6,22},{8,24},{10,26},{12,28},{14,30},{16,0},... | collective-permute-start | bytes 294920 | tf_op jit(solution)/shard_map/ppermute | solution.py:296
  24.0 0.2 collective-permute-start.15
  24.3 0.8 %collective-permute-done.13.rest_0_ = bf16[3,128,128]{2,1,0:T(8,128)(2,1)S(1)} collective-permute-done((bf16[3,128,128]{2,1,0:T(8,128)(2,1)S(1)}, bf16[3,128,128]{2,1,0:T(8,128)(2,1)S(1)}, u32[]{:S(2)}, u32[]{:S(2)}) %collective-permute-start.13) | collective-permute-done | bytes 98336 | tf_op jit(solution)/shard_map/ppermute | solution.py:296
  25.0 4.3 %collective-permute-done.14.rest_1_ = bf16[3,128,128]{2,1,0:T(8,128)(2,1)S(1)} collective-permute-done((bf16[3,128,128]{2,1,0:T(8,128)(2,1)S(1)}, bf16[3,128,128]{2,1,0:T(8,128)(2,1)S(1)}, u32[]{:S(2)}, u32[]{:S(2)}) %collective-permute-start.14) | collective-permute-done | bytes 98336 | tf_op jit(solution)/shard_map/ppermute | solution.py:296
  29.3 1.2 %collective-permute-done.15.rest_2_ = bf16[3,128,128]{2,1,0:T(8,128)(2,1)S(1)} collective-permute-done((bf16[3,128,128]{2,1,0:T(8,128)(2,1)S(1)}, bf16[3,128,128]{2,1,0:T(8,128)(2,1)S(1)}, u32[]{:S(2)}, u32[]{:S(2)}) %collective-permute-start.15) | collective-permute-done | bytes 98336 | tf_op jit(solution)/shard_map/ppermute | solution.py:296
  30.5 1.0 %update.1 = (f32[3,128,128]{2,1,0:T(8,128)}, f32[3,128,128]{2,1,0:T(8,128)}, f32[3,128,128]{2,1,0:T(8,128)}) custom-call(s32[45]{0:T(128)S(4)} %get-tuple-element.71.place, f32[3,128,128]{2,1,0:T(8,128)S(1)} %get-tuple-element.75.kept, bf16[3,128,128]{2,1,0:T(8,128)(2,1)S(1)} %collective-permute-done.13.rest_0_, ...), custom_call_target="tpu_custom_call" | custom-call | tf_op jit(solution)/shard_map/update/pallas_call | solution.py:378
  (2 shorter events, 0.1 us)
Async XLA Ops:
  0.6 4.7 %collective-permute-start.12 = (bf16[256,4096]{1,0:T(8,128)(2,1)}, bf16[256,4096]{1,0:T(8,128)(2,1)S(1)}, u32[]{:S(2)}, u32[]{:S(2)}) collective-permute-start(bf16[256,4096]{1,0:T(8,128)(2,1)} %features.1), channel_id=1, source_target_pairs={{0,1},{1,0},{2,3},{3,2},{4,5},{5,4},{6,7},{7,6},{8,9},{9,8},{10,11... | collective-permute-start | bytes 6291464 | tf_op jit(solution)/shard_map/ppermute | solution.py:301
  6.0 6.7 %collective-permute-start.1 = (bf16[4,128,128]{2,1,0:T(8,128)(2,1)S(1)}, bf16[4,128,128]{2,1,0:T(8,128)(2,1)S(1)}, u32[]{:S(2)}, u32[]{:S(2)}) collective-permute-start(bf16[4,128,128]{2,1,0:T(8,128)(2,1)S(1)} %get-tuple-element.31), channel_id=1, source_target_pairs={{0,4},{2,6},{4,0},{6,2},{8,12},{10,14},{12,8},{14,10},{16,20},{18,... | collective-permute-start | bytes 393224 | tf_op jit(solution)/shard_map/cond/branch_0_fun/ppermute | solution.py:296
  8.7 5.8 %collective-permute-start = (bf16[4,128,128]{2,1,0:T(8,128)(2,1)S(1)}, bf16[4,128,128]{2,1,0:T(8,128)(2,1)S(1)}, u32[]{:S(2)}, u32[]{:S(2)}) collective-permute-start(bf16[4,128,128]{2,1,0:T(8,128)(2,1)S(1)} %get-tuple-element.29), channel_id=1, source_target_pairs={{0,2},{2,0},{4,6},{6,4},{8,10},{10,8},{12,14},{14,12},{16,18},{18,... | collective-permute-start | bytes 393224 | tf_op jit(solution)/shard_map/cond/branch_0_fun/ppermute | solution.py:296
  12.8 5.2 %collective-permute-start.3 = (bf16[4,128,128]{2,1,0:T(8,128)(2,1)S(1)}, bf16[4,128,128]{2,1,0:T(8,128)(2,1)S(1)}, u32[]{:S(2)}, u32[]{:S(2)}) collective-permute-start(bf16[4,128,128]{2,1,0:T(8,128)(2,1)S(1)} %get-tuple-element.34), channel_id=1, source_target_pairs={{0,2},{2,0},{4,6},{6,4},{8,10},{10,8},{12,14},{14,12},{16,18},{18,... | collective-permute-start | bytes 393224 | tf_op jit(solution)/shard_map/cond/branch_0_fun/ppermute | solution.py:296
  14.6 5.0 %collective-permute-start.2 = (bf16[4,128,128]{2,1,0:T(8,128)(2,1)S(1)}, bf16[4,128,128]{2,1,0:T(8,128)(2,1)S(1)}, u32[]{:S(2)}, u32[]{:S(2)}) collective-permute-start(bf16[4,128,128]{2,1,0:T(8,128)(2,1)S(1)} %get-tuple-element.33), channel_id=1, source_target_pairs={{0,4},{2,6},{4,0},{6,2},{8,12},{10,14},{12,8},{14,10},{16,20},{18,... | collective-permute-start | bytes 393224 | tf_op jit(solution)/shard_map/cond/branch_0_fun/ppermute | solution.py:296
  19.8 5.2 %collective-permute-start.13 = (bf16[3,128,128]{2,1,0:T(8,128)(2,1)S(1)}, bf16[3,128,128]{2,1,0:T(8,128)(2,1)S(1)}, u32[]{:S(2)}, u32[]{:S(2)}) collective-permute-start(bf16[3,128,128]{2,1,0:T(8,128)(2,1)S(1)} %get-tuple-element.76), channel_id=1, source_target_pairs={{0,8},{2,10},{4,12},{6,14},{8,0},{10,2},{12,4},{14,6},{16,24},{18,... | collective-permute-start | bytes 294920 | tf_op jit(solution)/shard_map/ppermute | solution.py:296
  21.4 7.9 %collective-permute-start.14 = (bf16[3,128,128]{2,1,0:T(8,128)(2,1)S(1)}, bf16[3,128,128]{2,1,0:T(8,128)(2,1)S(1)}, u32[]{:S(2)}, u32[]{:S(2)}) collective-permute-start(bf16[3,128,128]{2,1,0:T(8,128)(2,1)S(1)} %get-tuple-element.77), channel_id=1, source_target_pairs={{0,16},{2,18},{4,20},{6,22},{8,24},{10,26},{12,28},{14,30},{16,0},... | collective-permute-start | bytes 294920 | tf_op jit(solution)/shard_map/ppermute | solution.py:296
  24.0 6.5 %collective-permute-start.15 = (bf16[3,128,128]{2,1,0:T(8,128)(2,1)S(1)}, bf16[3,128,128]{2,1,0:T(8,128)(2,1)S(1)}, u32[]{:S(2)}, u32[]{:S(2)}) collective-permute-start(bf16[3,128,128]{2,1,0:T(8,128)(2,1)S(1)} %get-tuple-element.78), channel_id=1, source_target_pairs={{0,24},{2,26},{4,28},{6,30},{8,16},{10,18},{12,20},{14,22},{16,8},... | collective-permute-start | bytes 294920 | tf_op jit(solution)/shard_map/ppermute | solution.py:296

commit v5 on v4

--- a/solution.py
+++ b/solution.py
@@ -26,7 +26,7 @@
     return sorted({min(level, most), min(level + max(listed // 16, 1), most), most})
 
 
-def route(blk, own, place, flag, seen, work, *, capacity, sizes):
+def route(blk, own, place, flag, depth, seen, work, *, capacity, sizes):
     listed = own.shape[0]
     replicas = seen.shape[0]
     me = lax.axis_index("dp")
@@ -112,18 +112,22 @@
 
         @pl.when(q == column)
         def _():
-            place[2 * listed + o // COLUMNS * capacity + s] = jnp.where(in_a, 0, slots) + slot
+            place[2 * listed + o // COLUMNS * capacity + s] = jnp.where(in_a, 0, sizes[-1]) + slot
 
         return carry
 
     lax.fori_loop(0, listed, assign, 0)
     place[place.shape[0] - 1] = seen[me]
+    busiest = jnp.int32(1)
+    for z in range(replicas // COLUMNS):
+        busiest = jnp.maximum(busiest, seen[z * COLUMNS + lax.rem(me, COLUMNS)])
+    depth[0] = busiest - 1
 
 
 def act_kernel(blk_hbm, own_hbm, features, gate, up, cot, *rest, capacity, sizes):
     states, rest = rest[:3], rest[3:]
-    act, rows, place, flag = rest[:4]
-    held, (gbuf, ubuf, cbuf, blk, own, sems, state_sems, seen, work) = rest[4:7], rest[7:]
+    act, rows, place, flag, depth = rest[:5]
+    held, (gbuf, ubuf, cbuf, blk, own, sems, state_sems, seen, work) = rest[5:8], rest[8:]
     listed, _, size = act.shape
     per = features.shape[1] // size
     mine = lax.axis_index("tensor")
@@ -167,7 +171,7 @@
     for copy in state_copies:
         copy.start()
     tables[1].wait()
-    route(blk, own, place, flag, seen, work, capacity=capacity, sizes=sizes)
+    route(blk, own, place, flag, depth, seen, work, capacity=capacity, sizes=sizes)
 
     def compute(k, carry):
         gated = blk[0, k] == 0
@@ -222,35 +226,34 @@
     send[...] = total[...].astype(send.dtype)
 
 
-def plane_kernel(place, sum_a, sum_b, other_a, other_b, *outs, listed, capacity):
+def total_kernel(sum_a, sum_b, other_a, other_b, total):
+    slots = sum_a.shape[0]
+    most = total.shape[0] // 2
+    total[:slots] = sum_a[...] + other_a[...].astype(total.dtype)
+    total[most : most + slots] = sum_b[...] + other_b[...].astype(total.dtype)
+
+
+def plane_kernel(place, total, *outs, listed, capacity):
     kept, sends = outs[0], outs[1:]
-    slots = sum_a.shape[0]
     plane = lax.axis_index("dp") // COLUMNS
 
-    def total(z, s):
-        j = place[2 * listed + z * capacity + s]
-        a = jnp.minimum(j, slots - 1)
-        b = jnp.maximum(j - slots, 0)
-        return jnp.where(
-            j < slots,
-            sum_a[a] + other_a[a].astype(jnp.float32),
-            sum_b[b] + other_b[b].astype(jnp.float32),
-        )
+    def cell(z, s):
+        return total[place[2 * listed + z * capacity + s]]
 
     if len(sends) == 1:
         sends = sends[0]
 
         def lay(j, carry):
-            sends[j] = total(j // capacity, lax.rem(j, capacity)).astype(sends.dtype)
+            sends[j] = cell(j // capacity, lax.rem(j, capacity)).astype(sends.dtype)
             return carry
 
         lax.fori_loop(0, sends.shape[0], lay, 0)
     else:
         for k, send in enumerate(sends):
-            for s in range(capacity):
-                send[s] = total(jnp.bitwise_xor(plane, k + 1), s).astype(send.dtype)
-    for s in range(capacity):
-        kept[s] = total(plane, s)
+            for s in range(send.shape[0]):
+                send[s] = cell(jnp.bitwise_xor(plane, k + 1), s).astype(send.dtype)
+    for s in range(kept.shape[0]):
+        kept[s] = cell(plane, s)
 
 
 def update_kernel(place, kept, *rest, count):
@@ -259,6 +262,11 @@
     outs, (bufs, sems) = outs[:3], outs[3:]
     held = place[place.shape[0] - 1]
     copies = []
+    for s in range(kept.shape[0], weights.shape[0]):
+        for i, (state, out) in enumerate(zip((weights, moment1, moment2), outs)):
+            copy = pltpu.make_async_copy(state.at[s], out.at[s], sems.at[i, s])
+            copy.start()
+            copies.append(copy)
     for s in range(kept.shape[0]):
         valid = s < held
         block_grad = kept[s]
@@ -301,17 +309,18 @@
         lax.ppermute(features, "tensor", [(i, (i + j) % shards) for i in range(shards)])
         for j in range(1, shards)
     ]
-    act, rows, place, flag, *states = pl.pallas_call(
+    act, rows, place, flag, depth, *states = pl.pallas_call(
         functools.partial(act_kernel, capacity=capacity, sizes=sizes),
         out_shape=(
             pltpu.VMEM((listed, tokens, size), bf16),
             pltpu.VMEM((listed, tokens, size), bf16),
             pltpu.SMEM((2 * listed + planes * capacity + 1,), jnp.int32),
             pltpu.SMEM((1,), jnp.int32),
+            pltpu.SMEM((1,), jnp.int32),
         )
         + (in_vmem(capacity, f32),) * 3,
         in_specs=[HBM] * 9,
-        out_specs=(VMEM, VMEM, SMEM, SMEM, VMEM, VMEM, VMEM),
+        out_specs=(VMEM, VMEM, SMEM, SMEM, SMEM, VMEM, VMEM, VMEM),
         scratch_shapes=[pltpu.VMEM((listed, tokens, size), bf16)] * 3
         + [
             pltpu.SMEM((3, listed), jnp.int32),
@@ -353,40 +362,54 @@
         other_a = swap(send_a, 2)
         other_b = swap(send_b, 1)
         return pl.pallas_call(
+            total_kernel,
+            out_shape=in_vmem(2 * sizes[-1], f32),
+            in_specs=[VMEM] * 4,
+            out_specs=VMEM,
+            compiler_params=grant((12 * slots + 8 * sizes[-1]) * block),
+            name="totals",
+        )(sum_a, sum_b, other_a, other_b)
+
+    total = lax.switch(flag[0], [functools.partial(plane_sums, n) for n in sizes])
+
+    def finish(slots):
+        outs = (slots,) * (planes - 1) if direct else (planes * capacity,)
+        kept, *sends = pl.pallas_call(
             functools.partial(plane_kernel, listed=listed, capacity=capacity),
-            out_shape=(in_vmem(capacity, f32),)
-            + ((in_vmem(capacity, bf16),) * (planes - 1) if direct else (in_vmem(planes * capacity, bf16),)),
-            in_specs=[SMEM, VMEM, VMEM, VMEM, VMEM],
-            out_specs=(VMEM,) * (planes if direct else 2),
-            compiler_params=grant((12 * slots + (4 + 2 * planes) * capacity) * block),
+            out_shape=(in_vmem(slots, f32),) + tuple(in_vmem(n, bf16) for n in outs),
+            in_specs=[SMEM, VMEM],
+            out_specs=(VMEM,) * (1 + len(outs)),
+            compiler_params=grant((8 * sizes[-1] + 4 * slots + 2 * sum(outs)) * block),
             name="planes",
-        )(place, sum_a, sum_b, other_a, other_b)
-
-    kept, *sends = lax.switch(flag[0], [functools.partial(plane_sums, n) for n in sizes])
-    if direct:
-        parts = []
-        for k, send in enumerate(sends):
-            parts.append(swap(send, (k + 1) * COLUMNS))
-    else:
-        groups = [[z * COLUMNS + c for z in range(planes)] for c in range(COLUMNS)]
-        incoming = lax.all_to_all(
-            sends[0], "dp", split_axis=0, concat_axis=0, tiled=True, axis_index_groups=groups
-        )
-        away = jnp.arange(planes) != lax.axis_index("dp") // COLUMNS
-        incoming = incoming.astype(f32).reshape(planes, capacity, size, size)
-        parts = [jnp.sum(jnp.where(away[:, None, None, None], incoming, 0.0), axis=0)]
-    return pl.pallas_call(
-        functools.partial(update_kernel, count=len(parts)),
-        out_shape=(jax.ShapeDtypeStruct(weights.shape, f32),) * 3,
-        in_specs=[SMEM] + [VMEM] * (4 + len(parts)),
-        out_specs=(HBM, HBM, HBM),
-        scratch_shapes=[
-            pltpu.VMEM((3,) + weights.shape, f32),
-            pltpu.SemaphoreType.DMA((3, capacity)),
-        ],
-        compiler_params=grant((28 + 4 * len(parts)) * capacity * block),
-        name="update",
-    )(place, kept, *parts, *states)
+        )(place, total)
+        if direct:
+            parts = []
+            for k, send in enumerate(sends):
+                parts.append(swap(send, (k + 1) * COLUMNS))
+        else:
+            groups = [[z * COLUMNS + c for z in range(planes)] for c in range(COLUMNS)]
+            incoming = lax.all_to_all(
+                sends[0], "dp", split_axis=0, concat_axis=0, tiled=True, axis_index_groups=groups
+            )
+            away = jnp.arange(planes) != lax.axis_index("dp") // COLUMNS
+            incoming = incoming.astype(f32).reshape(planes, capacity, size, size)
+            parts = [jnp.sum(jnp.where(away[:, None, None, None], incoming, 0.0), axis=0)]
+        return pl.pallas_call(
+            functools.partial(update_kernel, count=len(parts)),
+            out_shape=(jax.ShapeDtypeStruct(weights.shape, f32),) * 3,
+            in_specs=[SMEM] + [VMEM] * (4 + len(parts)),
+            out_specs=(HBM, HBM, HBM),
+            scratch_shapes=[
+                pltpu.VMEM((3,) + weights.shape, f32),
+                pltpu.SemaphoreType.DMA((3, capacity)),
+            ],
+            compiler_params=grant((28 + 4 * len(parts)) * capacity * block),
+            name="update",
+        )(place, kept, *parts, *states)
+
+    if not direct:
+        return finish(capacity)
+    return lax.switch(depth[0], [functools.partial(finish, n) for n in range(1, capacity + 1)])
 
 
 def solution(mesh):

time: 31.7 us -> 31.2 us (0.984)
  waiting for transfers between devices: 12.3 us -> 11.8 us
    ppermute x7, waiting for transfers between devices: 12.3 us -> 11.8 us  [local(): lax.ppermute(v, 'dp', [(i, i ^ bit) for i in range(replicas)])]
    pallas_call x2 -> x3, Pallas kernels: 1.1 us -> 0.99 us  [the longest x1 0.9 us: finish(): pl.pallas_call(functools.partial(update_kernel, count=len(parts)), out_sh...]
  transfers between devices with their start and end apart: 8 -> 8, of which waited for: 6 -> 6; matrix products, arithmetic and copies ran while one was open for 0% -> 0% of each run, Pallas kernels for 13% -> 14%
where the time goes in v5:
time: 31.2 us; the launch traced here: 31 us
  starting transfers between devices  12.6 us (40%)
  waiting for transfers between devices  11.8 us (38%)
  Pallas kernels  5.85 us (19%)
  between operations  0.67 us (2%)
    ppermute x7, starting transfers between devices, local(): lax.ppermute(v, 'dp', [(i, i ^ bit) for i in range(replicas)])  12 us
    ppermute x7, waiting for transfers between devices, local(): lax.ppermute(v, 'dp', [(i, i ^ bit) for i in range(replicas)])  11.8 us
    pallas_call x1, Pallas kernels, local(): pl.pallas_call(functools.partial(act_kernel, capacity=capacity, sizes=siz...  4.17 us
    pallas_call x1, Pallas kernels, finish(): pl.pallas_call(functools.partial(update_kernel, count=len(parts)), out_sh...  0.9 us
  transfers between devices with their start and end apart: 8, of which 6 were waited for; matrix products, arithmetic and copies ran while one was open for 0% of the time, Pallas kernels for 14%

profile of v5, /device:TPU:0, one launch (start us, length us, event | category | flops | bytes accessed | tf_op | source)
XLA Modules:
  0.0 31.0 jit_solution(1246843365837665141)
XLA Ops:
  0.6 0.6 %collective-permute-start.21 = (bf16[256,4096]{1,0:T(8,128)(2,1)}, bf16[256,4096]{1,0:T(8,128)(2,1)S(1)}, u32[]{:S(2)}, u32[]{:S(2)}) collective-permute-start(bf16[256,4096]{1,0:T(8,128)(2,1)} %features.1), channel_id=1, source_target_pairs={{0,1},{1,0},{2,3},{3,2},{4,5},{5,4},{6,7},{7,6},{8,9},{9,8},{10,11... | collective-permute-start | bytes 6291464 | tf_op jit(solution)/shard_map/ppermute | solution.py:309
  1.2 4.2 %activations.1 = (bf16[16,256,128]{2,1,0:T(8,128)(2,1)S(1)}, bf16[16,256,128]{2,1,0:T(8,128)(2,1)S(1)}, s32[45]{0:T(128)S(4)}, s32[1]{0:T(128)S(4)}, s32[1]{0:T(...) custom-call(s32[3,16]{1,0:T(4,128)} %bitcast.3, s32[16]{0:T(128)} %own_hbm.1, ...), custom_call_target="tpu_custom_call" | custom-call | tf_op jit(solution)/shard_map/activations/pallas_call | solution.py:312
  5.4 0.0 collective-permute-done.21
  5.4 14.3 %conditional.2 = (f32[12,128,128]{2,1,0:T(8,128)S(1)}) conditional(s32[]{:T(128)} %bitcast.2, (s32[45]{0:T(128)S(4)}, bf16[16,256,128]{2,1,0:T(8,128)(2,1)S(1)}, bf16[16,256,128]{2,1,0:T(8,128)(2,1)S(1)}, bf16[256,4096]{1,0:T(8,128)(2,1)S(1)}) %tuple.25, (s32[45]{0:T(128)S(4)}, bf16[16,256,128]{2,1,0:T(8,128)(2,1)S(1)}, ...), branch_computations={%region_0.0_spmd, %region_1.0_spmd, %region_2.0_spmd} | conditional | bytes 11534532 | solution.py:373
  5.4 0.6 %products.3 = (bf16[4,128,128]{2,1,0:T(8,128)(2,1)S(1)}, bf16[4,128,128]{2,1,0:T(8,128)(2,1)S(1)}, f32[16,128,128]{2,1,0:T(8,128)S(1)}) custom-call(s32[45]{0:T(128)S(4)} %get-tuple-element.44.place, bf16[16,256,128]{2,1,0:T(8,128)(2,1)S(1)} %get-tuple-element.54.act, bf16[16,256,128]{2,1,0:T(8,128)(2,1)S(1)} %get-tuple-element.60.rows, ...), custom_call_target="tpu_custom_call" | custom-call | tf_op jit(solution)/shard_map/cond/branch_0_fun/products/pallas_call | solution.py:339
  6.0 2.7 %collective-permute-start.1 = (bf16[4,128,128]{2,1,0:T(8,128)(2,1)S(1)}, bf16[4,128,128]{2,1,0:T(8,128)(2,1)S(1)}, u32[]{:S(2)}, u32[]{:S(2)}) collective-permute-start(bf16[4,128,128]{2,1,0:T(8,128)(2,1)S(1)} %get-tuple-element.65), channel_id=1, source_target_pairs={{0,4},{2,6},{4,0},{6,2},{8,12},{10,14},{12,8},{14,10},{16,20},{18,... | collective-permute-start | bytes 393224 | tf_op jit(solution)/shard_map/cond/branch_0_fun/ppermute | solution.py:304
  8.7 1.5 %collective-permute-start = (bf16[4,128,128]{2,1,0:T(8,128)(2,1)S(1)}, bf16[4,128,128]{2,1,0:T(8,128)(2,1)S(1)}, u32[]{:S(2)}, u32[]{:S(2)}) collective-permute-start(bf16[4,128,128]{2,1,0:T(8,128)(2,1)S(1)} %get-tuple-element.63), channel_id=1, source_target_pairs={{0,2},{2,0},{4,6},{6,4},{8,10},{10,8},{12,14},{14,12},{16,18},{18,... | collective-permute-start | bytes 393224 | tf_op jit(solution)/shard_map/cond/branch_0_fun/ppermute | solution.py:304
  10.2 2.5 %collective-permute-done.1.got = bf16[4,128,128]{2,1,0:T(8,128)(2,1)S(1)} collective-permute-done((bf16[4,128,128]{2,1,0:T(8,128)(2,1)S(1)}, bf16[4,128,128]{2,1,0:T(8,128)(2,1)S(1)}, u32[]{:S(2)}, u32[]{:S(2)}) %collective-permute-start.1) | collective-permute-done | bytes 131104 | tf_op jit(solution)/shard_map/cond/branch_0_fun/ppermute | solution.py:304
  12.8 1.8 %collective-permute-start.3 = (bf16[4,128,128]{2,1,0:T(8,128)(2,1)S(1)}, bf16[4,128,128]{2,1,0:T(8,128)(2,1)S(1)}, u32[]{:S(2)}, u32[]{:S(2)}) collective-permute-start(bf16[4,128,128]{2,1,0:T(8,128)(2,1)S(1)} %get-tuple-element.68), channel_id=1, source_target_pairs={{0,2},{2,0},{4,6},{6,4},{8,10},{10,8},{12,14},{14,12},{16,18},{18,... | collective-permute-start | bytes 393224 | tf_op jit(solution)/shard_map/cond/branch_0_fun/ppermute | solution.py:304
  14.6 0.0 collective-permute-done.got
  14.6 1.6 %collective-permute-start.2 = (bf16[4,128,128]{2,1,0:T(8,128)(2,1)S(1)}, bf16[4,128,128]{2,1,0:T(8,128)(2,1)S(1)}, u32[]{:S(2)}, u32[]{:S(2)}) collective-permute-start(bf16[4,128,128]{2,1,0:T(8,128)(2,1)S(1)} %get-tuple-element.67), channel_id=1, source_target_pairs={{0,4},{2,6},{4,0},{6,2},{8,12},{10,14},{12,8},{14,10},{16,20},{18,... | collective-permute-start | bytes 393224 | tf_op jit(solution)/shard_map/cond/branch_0_fun/ppermute | solution.py:304
  16.2 1.8 %collective-permute-done.3.other_b = bf16[4,128,128]{2,1,0:T(8,128)(2,1)S(1)} collective-permute-done((bf16[4,128,128]{2,1,0:T(8,128)(2,1)S(1)}, bf16[4,128,128]{2,1,0:T(8,128)(2,1)S(1)}, u32[]{:S(2)}, u32[]{:S(2)}) %collective-permute-start.3) | collective-permute-done | bytes 131104 | tf_op jit(solution)/shard_map/cond/branch_0_fun/ppermute | solution.py:304
  18.0 1.6 %collective-permute-done.2.other_a = bf16[4,128,128]{2,1,0:T(8,128)(2,1)S(1)} collective-permute-done((bf16[4,128,128]{2,1,0:T(8,128)(2,1)S(1)}, bf16[4,128,128]{2,1,0:T(8,128)(2,1)S(1)}, u32[]{:S(2)}, u32[]{:S(2)}) %collective-permute-start.2) | collective-permute-done | bytes 131104 | tf_op jit(solution)/shard_map/cond/branch_0_fun/ppermute | solution.py:304
  19.7 11.3 %conditional.3 = ((f32[3,128,128]{2,1,0:T(8,128)}, f32[3,128,128]{2,1,0:T(8,128)}, f32[3,128,128]{2,1,0:T(8,128)})) conditional(s32[]{:T(128)} %bitcast.1, (s32[45]{0:T(128)S(4)}, f32[12,128,128]{2,1,0:T(8,128)S(1)}, f32[3,128,128]{2,1,0:T(8,128)S(1)}, f32[3,128,128]{2,1,0:T(8,128)S(1)}, f32[3,128,128]{2,1,0:T(8,128)S(1)}) %tuple.26, ...), branch_computations={%region_3.0_spmd, %region_4.0_spmd, %region_5.0_spmd} | conditional | bytes 1179776 | solution.py:412
  19.7 0.1 planes.4
  19.8 1.6 %collective-permute-start.15 = (bf16[2,128,128]{2,1,0:T(8,128)(2,1)S(1)}, bf16[2,128,128]{2,1,0:T(8,128)(2,1)S(1)}, u32[]{:S(2)}, u32[]{:S(2)}) collective-permute-start(bf16[2,128,128]{2,1,0:T(8,128)(2,1)S(1)} %get-tuple-element.103), channel_id=1, source_target_pairs={{0,8},{2,10},{4,12},{6,14},{8,0},{10,2},{12,4},{14,6},{16,24},{18,... | collective-permute-start | bytes 196616 | tf_op jit(solution)/shard_map/cond/branch_1_fun/ppermute | solution.py:304
  21.4 2.6 %collective-permute-start.16 = (bf16[2,128,128]{2,1,0:T(8,128)(2,1)S(1)}, bf16[2,128,128]{2,1,0:T(8,128)(2,1)S(1)}, u32[]{:S(2)}, u32[]{:S(2)}) collective-permute-start(bf16[2,128,128]{2,1,0:T(8,128)(2,1)S(1)} %get-tuple-element.104), channel_id=1, source_target_pairs={{0,16},{2,18},{4,20},{6,22},{8,24},{10,26},{12,28},{14,30},{16,0},... | collective-permute-start | bytes 196616 | tf_op jit(solution)/shard_map/cond/branch_1_fun/ppermute | solution.py:304
  24.0 0.2 collective-permute-start.17
  24.3 0.1 collective-permute-done.15.rest_0_
  24.4 3.7 %collective-permute-done.16.rest_1_ = bf16[2,128,128]{2,1,0:T(8,128)(2,1)S(1)} collective-permute-done((bf16[2,128,128]{2,1,0:T(8,128)(2,1)S(1)}, bf16[2,128,128]{2,1,0:T(8,128)(2,1)S(1)}, u32[]{:S(2)}, u32[]{:S(2)}) %collective-permute-start.16) | collective-permute-done | bytes 65568 | tf_op jit(solution)/shard_map/cond/branch_1_fun/ppermute | solution.py:304
  28.0 2.1 %collective-permute-done.17.rest_2_ = bf16[2,128,128]{2,1,0:T(8,128)(2,1)S(1)} collective-permute-done((bf16[2,128,128]{2,1,0:T(8,128)(2,1)S(1)}, bf16[2,128,128]{2,1,0:T(8,128)(2,1)S(1)}, u32[]{:S(2)}, u32[]{:S(2)}) %collective-permute-start.17) | collective-permute-done | bytes 65568 | tf_op jit(solution)/shard_map/cond/branch_1_fun/ppermute | solution.py:304
  30.1 0.9 %update.4 = (f32[3,128,128]{2,1,0:T(8,128)}, f32[3,128,128]{2,1,0:T(8,128)}, f32[3,128,128]{2,1,0:T(8,128)}) custom-call(s32[45]{0:T(128)S(4)} %get-tuple-element.100.place, f32[2,128,128]{2,1,0:T(8,128)S(1)} %get-tuple-element.102.kept, bf16[2,128,128]{2,1,0:T(8,128)(2,1)S(1)} %collective-permute-done.15.rest_0_, ...), custom_call_target="tpu_custom_call" | custom-call | tf_op jit(solution)/shard_map/cond/branch_1_fun/update/pallas_call | solution.py:397
  (3 shorter events, 0.1 us)
Async XLA Ops:
  0.6 4.8 %collective-permute-start.21 = (bf16[256,4096]{1,0:T(8,128)(2,1)}, bf16[256,4096]{1,0:T(8,128)(2,1)S(1)}, u32[]{:S(2)}, u32[]{:S(2)}) collective-permute-start(bf16[256,4096]{1,0:T(8,128)(2,1)} %features.1), channel_id=1, source_target_pairs={{0,1},{1,0},{2,3},{3,2},{4,5},{5,4},{6,7},{7,6},{8,9},{9,8},{10,11... | collective-permute-start | bytes 6291464 | tf_op jit(solution)/shard_map/ppermute | solution.py:309
  6.0 6.7 %collective-permute-start.1 = (bf16[4,128,128]{2,1,0:T(8,128)(2,1)S(1)}, bf16[4,128,128]{2,1,0:T(8,128)(2,1)S(1)}, u32[]{:S(2)}, u32[]{:S(2)}) collective-permute-start(bf16[4,128,128]{2,1,0:T(8,128)(2,1)S(1)} %get-tuple-element.65), channel_id=1, source_target_pairs={{0,4},{2,6},{4,0},{6,2},{8,12},{10,14},{12,8},{14,10},{16,20},{18,... | collective-permute-start | bytes 393224 | tf_op jit(solution)/shard_map/cond/branch_0_fun/ppermute | solution.py:304
  8.7 5.8 %collective-permute-start = (bf16[4,128,128]{2,1,0:T(8,128)(2,1)S(1)}, bf16[4,128,128]{2,1,0:T(8,128)(2,1)S(1)}, u32[]{:S(2)}, u32[]{:S(2)}) collective-permute-start(bf16[4,128,128]{2,1,0:T(8,128)(2,1)S(1)} %get-tuple-element.63), channel_id=1, source_target_pairs={{0,2},{2,0},{4,6},{6,4},{8,10},{10,8},{12,14},{14,12},{16,18},{18,... | collective-permute-start | bytes 393224 | tf_op jit(solution)/shard_map/cond/branch_0_fun/ppermute | solution.py:304
  12.8 5.2 %collective-permute-start.3 = (bf16[4,128,128]{2,1,0:T(8,128)(2,1)S(1)}, bf16[4,128,128]{2,1,0:T(8,128)(2,1)S(1)}, u32[]{:S(2)}, u32[]{:S(2)}) collective-permute-start(bf16[4,128,128]{2,1,0:T(8,128)(2,1)S(1)} %get-tuple-element.68), channel_id=1, source_target_pairs={{0,2},{2,0},{4,6},{6,4},{8,10},{10,8},{12,14},{14,12},{16,18},{18,... | collective-permute-start | bytes 393224 | tf_op jit(solution)/shard_map/cond/branch_0_fun/ppermute | solution.py:304
  14.6 5.0 %collective-permute-start.2 = (bf16[4,128,128]{2,1,0:T(8,128)(2,1)S(1)}, bf16[4,128,128]{2,1,0:T(8,128)(2,1)S(1)}, u32[]{:S(2)}, u32[]{:S(2)}) collective-permute-start(bf16[4,128,128]{2,1,0:T(8,128)(2,1)S(1)} %get-tuple-element.67), channel_id=1, source_target_pairs={{0,4},{2,6},{4,0},{6,2},{8,12},{10,14},{12,8},{14,10},{16,20},{18,... | collective-permute-start | bytes 393224 | tf_op jit(solution)/shard_map/cond/branch_0_fun/ppermute | solution.py:304
  19.8 4.6 %collective-permute-start.15 = (bf16[2,128,128]{2,1,0:T(8,128)(2,1)S(1)}, bf16[2,128,128]{2,1,0:T(8,128)(2,1)S(1)}, u32[]{:S(2)}, u32[]{:S(2)}) collective-permute-start(bf16[2,128,128]{2,1,0:T(8,128)(2,1)S(1)} %get-tuple-element.103), channel_id=1, source_target_pairs={{0,8},{2,10},{4,12},{6,14},{8,0},{10,2},{12,4},{14,6},{16,24},{18,... | collective-permute-start | bytes 196616 | tf_op jit(solution)/shard_map/cond/branch_1_fun/ppermute | solution.py:304
  21.4 6.6 %collective-permute-start.16 = (bf16[2,128,128]{2,1,0:T(8,128)(2,1)S(1)}, bf16[2,128,128]{2,1,0:T(8,128)(2,1)S(1)}, u32[]{:S(2)}, u32[]{:S(2)}) collective-permute-start(bf16[2,128,128]{2,1,0:T(8,128)(2,1)S(1)} %get-tuple-element.104), channel_id=1, source_target_pairs={{0,16},{2,18},{4,20},{6,22},{8,24},{10,26},{12,28},{14,30},{16,0},... | collective-permute-start | bytes 196616 | tf_op jit(solution)/shard_map/cond/branch_1_fun/ppermute | solution.py:304
  24.0 6.1 %collective-permute-start.17 = (bf16[2,128,128]{2,1,0:T(8,128)(2,1)S(1)}, bf16[2,128,128]{2,1,0:T(8,128)(2,1)S(1)}, u32[]{:S(2)}, u32[]{:S(2)}) collective-permute-start(bf16[2,128,128]{2,1,0:T(8,128)(2,1)S(1)} %get-tuple-element.105), channel_id=1, source_target_pairs={{0,24},{2,26},{4,28},{6,30},{8,16},{10,18},{12,20},{14,22},{16,8},... | collective-permute-start | bytes 196616 | tf_op jit(solution)/shard_map/cond/branch_1_fun/ppermute | solution.py:304

commit v6 on v5

--- a/solution.py
+++ b/solution.py
@@ -28,6 +28,8 @@
 
 def route(blk, own, place, flag, depth, seen, work, *, capacity, sizes):
     listed = own.shape[0]
+    most = sizes[-1]
+    cells = 4 * most + listed
     replicas = seen.shape[0]
     me = lax.axis_index("dp")
     column = lax.rem(me, COLUMNS)
@@ -38,7 +40,7 @@
         seen[o] = 0
         return carry
 
-    lax.fori_loop(0, replicas, clear_seen, 0)
+    lax.fori_loop(0, replicas, clear_seen, 0, unroll=8)
     for i in range(6 * COLUMNS):
         work[i] = 0
 
@@ -47,7 +49,7 @@
         work[COUNT + q] = work[COUNT + q] + 1
         return carry
 
-    lax.fori_loop(0, listed, count, 0)
+    lax.fori_loop(0, listed, count, 0, unroll=4)
 
     n = [work[COUNT + q] for q in range(COLUMNS)]
 
@@ -68,20 +70,16 @@
 
         return lax.fori_loop(0, size + 1, attempt, jnp.int32(-1))
 
-    flag[0] = len(sizes) - 1
-    work[LOAD + 1] = sizes[-1]
-    work[LOAD] = search(sizes[-1])
-    for i in reversed(range(len(sizes) - 1)):
+    def settle(i):
         best = search(sizes[i])
-
-        @pl.when(best >= 0)
-        def _():
-            flag[0] = i
-            work[LOAD + 1] = sizes[i]
-            work[LOAD] = best
-
-    slots = work[LOAD + 1]
-    a = shares(slots, work[LOAD])
+        flag[0] = i
+        work[LOAD + 1] = sizes[i]
+        work[LOAD] = best
+        if i + 1 < len(sizes):
+            pl.when(best < 0)(lambda: settle(i + 1))
+
+    settle(0)
+    a = shares(work[LOAD + 1], work[LOAD])
     for q in range(COLUMNS):
         work[TAKE + q] = a[q]
     for q, (at_a, at_b) in enumerate(((0, 0), (0, n[0] - a[0]), (a[0], 0), (a[1], n[2] - a[2]))):
@@ -89,10 +87,16 @@
         work[AT_B + q] = at_b
 
     def clear_place(j, carry):
-        place[2 * listed + j] = 0
-        return carry
-
-    lax.fori_loop(0, replicas // COLUMNS * capacity, clear_place, 0)
+        place[cells + j] = 0
+        return carry
+
+    lax.fori_loop(0, replicas // COLUMNS * capacity, clear_place, 0, unroll=4)
+
+    def clear_slots(j, carry):
+        place[j] = 0
+        return carry
+
+    lax.fori_loop(0, 4 * most, clear_slots, 0, unroll=8)
 
     def assign(k, carry):
         o = own[k]
@@ -105,18 +109,18 @@
         bit = jnp.where(in_a, lax.rem(q, 2), q // 2)
         mine = jnp.where(in_a, my_bit[0], my_bit[1])
         keep = (bit == mine).astype(jnp.int32)
-        place[k] = jnp.where(in_a, 0, 2 * slots) + keep * slots + slot
-        place[listed + k] = blk[1, k]
+        place[jnp.where(in_a, 0, 2 * most) + keep * most + slot] = k
+        place[4 * most + k] = blk[1, k]
         s = seen[o]
         seen[o] = s + 1
 
         @pl.when(q == column)
         def _():
-            place[2 * listed + o // COLUMNS * capacity + s] = jnp.where(in_a, 0, sizes[-1]) + slot
-
-        return carry
-
-    lax.fori_loop(0, listed, assign, 0)
+            place[cells + o // COLUMNS * capacity + s] = jnp.where(in_a, 0, most) + slot
+
+        return carry
+
+    lax.fori_loop(0, listed, assign, 0, unroll=4)
     place[place.shape[0] - 1] = seen[me]
     busiest = jnp.int32(1)
     for z in range(replicas // COLUMNS):
@@ -197,32 +201,32 @@
         copy.wait()
 
 
-def product_kernel(place, act, rows, *rest, shards, slots):
-    others = rest[: shards - 1]
-    send_a, send_b, part = rest[shards - 1 :]
-    listed, _, size = act.shape
+def product_kernel(place, act, rows, *rest, shards, most, bins):
+    others, outs = rest[: shards - 1], rest[shards - 1 :]
+    _, _, size = act.shape
     per = others[0].shape[1] // size
     mine = lax.axis_index("tensor")
 
-    def compute(k, carry):
-        r = place[listed + k]
-        cols = pl.ds(pl.multiple_of(lax.rem(r, per) * size, size), size)
-        source = lax.rem(mine + shards - r // per, shards)
-        lhs = rows[k]
-        for j in range(1, shards):
-            lhs = jnp.where(source == j, others[j - 1][:, cols], lhs)
-        part[place[k]] = lax.dot_general(
-            lhs, act[k], (((0,), (0,)), ((), ())), preferred_element_type=jnp.float32
-        )
-        return carry
-
-    lax.fori_loop(0, listed, compute, 0, unroll=16)
-    send_a[...] = part[:slots].astype(send_a.dtype)
-    send_b[...] = part[2 * slots : 3 * slots].astype(send_b.dtype)
-
-
-def add_kernel(part, got, total, send, *, start):
-    total[...] = part[start : start + total.shape[0]] + got[...].astype(total.dtype)
+    for out, at in zip(outs, bins):
+
+        def compute(j, carry):
+            k = place[at * most + j]
+            r = place[4 * most + k]
+            cols = pl.ds(pl.multiple_of(lax.rem(r, per) * size, size), size)
+            source = lax.rem(mine + shards - r // per, shards)
+            lhs = rows[k]
+            for i in range(1, shards):
+                lhs = jnp.where(source == i, others[i - 1][:, cols], lhs)
+            out[j] = lax.dot_general(
+                lhs, act[k], (((0,), (0,)), ((), ())), preferred_element_type=jnp.float32
+            ).astype(out.dtype)
+            return carry
+
+        lax.fori_loop(0, out.shape[0], compute, 0, unroll=min(out.shape[0], 8))
+
+
+def add_kernel(part, got, total, send):
+    total[...] = part[...] + got[...].astype(total.dtype)
     send[...] = total[...].astype(send.dtype)
 
 
@@ -233,12 +237,12 @@
     total[most : most + slots] = sum_b[...] + other_b[...].astype(total.dtype)
 
 
-def plane_kernel(place, total, *outs, listed, capacity):
+def plane_kernel(place, total, *outs, cells, capacity):
     kept, sends = outs[0], outs[1:]
     plane = lax.axis_index("dp") // COLUMNS
 
     def cell(z, s):
-        return total[place[2 * listed + z * capacity + s]]
+        return total[place[cells + z * capacity + s]]
 
     if len(sends) == 1:
         sends = sends[0]
@@ -314,7 +318,7 @@
         out_shape=(
             pltpu.VMEM((listed, tokens, size), bf16),
             pltpu.VMEM((listed, tokens, size), bf16),
-            pltpu.SMEM((2 * listed + planes * capacity + 1,), jnp.int32),
+            pltpu.SMEM((4 * sizes[-1] + listed + planes * capacity + 1,), jnp.int32),
             pltpu.SMEM((1,), jnp.int32),
             pltpu.SMEM((1,), jnp.int32),
         )
@@ -336,31 +340,36 @@
     direct = planes <= 4 and planes & (planes - 1) == 0
 
     def plane_sums(slots):
-        send_a, send_b, part = pl.pallas_call(
-            functools.partial(product_kernel, shards=shards, slots=slots),
-            out_shape=(in_vmem(slots, bf16), in_vmem(slots, bf16), in_vmem(4 * slots, f32)),
-            in_specs=[SMEM] + [VMEM] * (shards + 1),
-            out_specs=(VMEM, VMEM, VMEM),
-            compiler_params=grant(
-                2 * listed * column * 2 + (shards - 1) * features.size * 2 + 20 * slots * block
-            ),
-            name="products",
-        )(place, act, rows, *others)
-
-        def add(got, start):
+        def products(dtype, *bins):
             return pl.pallas_call(
-                functools.partial(add_kernel, start=start),
+                functools.partial(product_kernel, shards=shards, most=sizes[-1], bins=bins),
+                out_shape=(in_vmem(slots, dtype),) * len(bins),
+                in_specs=[SMEM] + [VMEM] * (shards + 1),
+                out_specs=(VMEM,) * len(bins),
+                compiler_params=grant(
+                    2 * listed * column * 2 + (shards - 1) * features.size * 2 + 8 * slots * block
+                ),
+                name="products",
+            )(place, act, rows, *others)
+
+        def add(part, got):
+            return pl.pallas_call(
+                add_kernel,
                 out_shape=(in_vmem(slots, f32), in_vmem(slots, bf16)),
                 in_specs=[VMEM, VMEM],
                 out_specs=(VMEM, VMEM),
-                compiler_params=grant(24 * slots * block),
+                compiler_params=grant(12 * slots * block),
                 name="sums",
             )(part, got)
 
-        sum_a, send_a = add(swap(send_a, 1), slots)
-        sum_b, send_b = add(swap(send_b, 2), 3 * slots)
+        send_b, send_a = products(bf16, 2, 0)
+        got_b = swap(send_b, 2)
+        got_a = swap(send_a, 1)
+        kept_b, kept_a = products(f32, 3, 1)
+        sum_b, send_b = add(kept_b, got_b)
+        sum_a, send_a = add(kept_a, got_a)
+        other_b = swap(send_b, 1)
         other_a = swap(send_a, 2)
-        other_b = swap(send_b, 1)
         return pl.pallas_call(
             total_kernel,
             out_shape=in_vmem(2 * sizes[-1], f32),
@@ -375,7 +384,7 @@
     def finish(slots):
         outs = (slots,) * (planes - 1) if direct else (planes * capacity,)
         kept, *sends = pl.pallas_call(
-            functools.partial(plane_kernel, listed=listed, capacity=capacity),
+            functools.partial(plane_kernel, cells=4 * sizes[-1] + listed, capacity=capacity),
             out_shape=(in_vmem(slots, f32),) + tuple(in_vmem(n, bf16) for n in outs),
             in_specs=[SMEM, VMEM],
             out_specs=(VMEM,) * (1 + len(outs)),

time: 31.2 us -> 31 us (level)
    ppermute x7, waiting for transfers between devices: 11.8 us -> 11.4 us  [local(): lax.ppermute(v, 'dp', [(i, i ^ bit) for i in range(replicas)])]
    pallas_call x1, Pallas kernels: 4.17 us -> 3.78 us  [local(): pl.pallas_call(functools.partial(act_kernel, capacity=capacity, sizes=siz...]
    pallas_call x4 -> x5, Pallas kernels: 0.73 us -> 0.9 us  [the longest x2 0.77 us: products(): pl.pallas_call(functools.partial(product_kernel, shards=shards, most=size...]
  transfers between devices with their start and end apart: 8 -> 8, of which waited for: 6 -> 7; matrix products, arithmetic and copies ran while one was open for 0% -> 0% of each run, Pallas kernels for 14% -> 14%
where the time goes in v6:
time: 31 us; the launch traced here: 30.8 us
  starting transfers between devices  12.8 us (41%)
  waiting for transfers between devices  11.6 us (37%)
  Pallas kernels  5.62 us (18%)
  between operations  0.66 us (2%)
    ppermute x7, starting transfers between devices, local(): lax.ppermute(v, 'dp', [(i, i ^ bit) for i in range(replicas)])  12.3 us
    ppermute x7, waiting for transfers between devices, local(): lax.ppermute(v, 'dp', [(i, i ^ bit) for i in range(replicas)])  11.4 us
    pallas_call x1, Pallas kernels, local(): pl.pallas_call(functools.partial(act_kernel, capacity=capacity, sizes=siz...  3.78 us
    pallas_call x1, Pallas kernels, finish(): pl.pallas_call(functools.partial(update_kernel, count=len(parts)), out_sh...  0.9 us
    pallas_call x2, Pallas kernels, products(): pl.pallas_call(functools.partial(product_kernel, shards=shards, most=size...  0.77 us
  transfers between devices with their start and end apart: 8, of which 7 were waited for; matrix products, arithmetic and copies ran while one was open for 0% of the time, Pallas kernels for 14%

profile of v6, /device:TPU:0, one launch (start us, length us, event | category | flops | bytes accessed | tf_op | source)
XLA Modules:
  0.0 30.8 jit_solution(3895936220276800344)
XLA Ops:
  0.6 0.6 %collective-permute-start.21 = (bf16[256,4096]{1,0:T(8,128)(2,1)}, bf16[256,4096]{1,0:T(8,128)(2,1)S(1)}, u32[]{:S(2)}, u32[]{:S(2)}) collective-permute-start(bf16[256,4096]{1,0:T(8,128)(2,1)} %features.1), channel_id=1, source_target_pairs={{0,1},{1,0},{2,3},{3,2},{4,5},{5,4},{6,7},{7,6},{8,9},{9,8},{10,11... | collective-permute-start | bytes 6291464 | tf_op jit(solution)/shard_map/ppermute | solution.py:313
  1.2 3.8 %activations.1 = (bf16[16,256,128]{2,1,0:T(8,128)(2,1)S(1)}, bf16[16,256,128]{2,1,0:T(8,128)(2,1)S(1)}, s32[53]{0:T(128)S(4)}, s32[1]{0:T(128)S(4)}, s32[1]{0:T(...) custom-call(s32[3,16]{1,0:T(4,128)} %bitcast.3, s32[16]{0:T(128)} %own_hbm.1, ...), custom_call_target="tpu_custom_call" | custom-call | tf_op jit(solution)/shard_map/activations/pallas_call | solution.py:316
  5.0 0.2 collective-permute-done.21
  5.2 14.3 %conditional.2 = (f32[12,128,128]{2,1,0:T(8,128)S(1)}) conditional(s32[]{:T(128)} %bitcast.2, (s32[53]{0:T(128)S(4)}, bf16[16,256,128]{2,1,0:T(8,128)(2,1)S(1)}, bf16[16,256,128]{2,1,0:T(8,128)(2,1)S(1)}, bf16[256,4096]{1,0:T(8,128)(2,1)S(1)}) %tuple.25, (s32[53]{0:T(128)S(4)}, bf16[16,256,128]{2,1,0:T(8,128)(2,1)S(1)}, ...), branch_computations={%region_0.0_spmd, %region_1.0_spmd, %region_2.0_spmd} | conditional | bytes 3145896 | solution.py:382
  5.2 0.4 %products.7 = (bf16[4,128,128]{2,1,0:T(8,128)(2,1)S(1)}, bf16[4,128,128]{2,1,0:T(8,128)(2,1)S(1)}) custom-call(s32[53]{0:T(128)S(4)} %get-tuple-element.44.place, bf16[16,256,128]{2,1,0:T(8,128)(2,1)S(1)} %get-tuple-element.54.act, bf16[16,256,128]{2,1,0:T(8,128)(2,1)S(1)} %get-tuple-element.60.rows, bf16[256,4096]{1,0:T(8,128)(2,1)S(1)} %get-tuple-element.61.rest_0_), custom_call_target="tpu_custom_call" | custom-call | tf_op jit(solution)/shard_map/cond/branch_0_fun/products/pallas_call | solution.py:344
  5.6 2.9 %collective-permute-start = (bf16[4,128,128]{2,1,0:T(8,128)(2,1)S(1)}, bf16[4,128,128]{2,1,0:T(8,128)(2,1)S(1)}, u32[]{:S(2)}, u32[]{:S(2)}) collective-permute-start(bf16[4,128,128]{2,1,0:T(8,128)(2,1)S(1)} %get-tuple-element.63), channel_id=1, source_target_pairs={{0,2},{2,0},{4,6},{6,4},{8,10},{10,8},{12,14},{14,12},{16,18},{18,... | collective-permute-start | bytes 393224 | tf_op jit(solution)/shard_map/cond/branch_0_fun/ppermute | solution.py:308
  8.5 1.5 %collective-permute-start.1 = (bf16[4,128,128]{2,1,0:T(8,128)(2,1)S(1)}, bf16[4,128,128]{2,1,0:T(8,128)(2,1)S(1)}, u32[]{:S(2)}, u32[]{:S(2)}) collective-permute-start(bf16[4,128,128]{2,1,0:T(8,128)(2,1)S(1)} %get-tuple-element.66), channel_id=1, source_target_pairs={{0,4},{2,6},{4,0},{6,2},{8,12},{10,14},{12,8},{14,10},{16,20},{18,... | collective-permute-start | bytes 393224 | tf_op jit(solution)/shard_map/cond/branch_0_fun/ppermute | solution.py:308
  10.0 0.4 %products.6 = (f32[4,128,128]{2,1,0:T(8,128)S(1)}, f32[4,128,128]{2,1,0:T(8,128)S(1)}) custom-call(s32[53]{0:T(128)S(4)} %get-tuple-element.44.place, bf16[16,256,128]{2,1,0:T(8,128)(2,1)S(1)} %get-tuple-element.54.act, bf16[16,256,128]{2,1,0:T(8,128)(2,1)S(1)} %get-tuple-element.60.rows, bf16[256,4096]{1,0:T(8,128)(2,1)S(1)} %get-tuple-element.61.rest_0_), custom_call_target="tpu_custom_call" | custom-call | tf_op jit(solution)/shard_map/cond/branch_0_fun/products/pallas_call | solution.py:344
  10.4 2.1 %collective-permute-done.got = bf16[4,128,128]{2,1,0:T(8,128)(2,1)S(1)} collective-permute-done((bf16[4,128,128]{2,1,0:T(8,128)(2,1)S(1)}, bf16[4,128,128]{2,1,0:T(8,128)(2,1)S(1)}, u32[]{:S(2)}, u32[]{:S(2)}) %collective-permute-start) | collective-permute-done | bytes 131104 | tf_op jit(solution)/shard_map/cond/branch_0_fun/ppermute | solution.py:308
  12.5 1.8 %collective-permute-start.2 = (bf16[4,128,128]{2,1,0:T(8,128)(2,1)S(1)}, bf16[4,128,128]{2,1,0:T(8,128)(2,1)S(1)}, u32[]{:S(2)}, u32[]{:S(2)}) collective-permute-start(bf16[4,128,128]{2,1,0:T(8,128)(2,1)S(1)} %get-tuple-element.68), channel_id=1, source_target_pairs={{0,4},{2,6},{4,0},{6,2},{8,12},{10,14},{12,8},{14,10},{16,20},{18,... | collective-permute-start | bytes 393224 | tf_op jit(solution)/shard_map/cond/branch_0_fun/ppermute | solution.py:308
  14.4 0.0 collective-permute-done.1.got
  14.4 1.6 %collective-permute-start.3 = (bf16[4,128,128]{2,1,0:T(8,128)(2,1)S(1)}, bf16[4,128,128]{2,1,0:T(8,128)(2,1)S(1)}, u32[]{:S(2)}, u32[]{:S(2)}) collective-permute-start(bf16[4,128,128]{2,1,0:T(8,128)(2,1)S(1)} %get-tuple-element.69), channel_id=1, source_target_pairs={{0,2},{2,0},{4,6},{6,4},{8,10},{10,8},{12,14},{14,12},{16,18},{18,... | collective-permute-start | bytes 393224 | tf_op jit(solution)/shard_map/cond/branch_0_fun/ppermute | solution.py:308
  16.0 1.8 %collective-permute-done.2.other_a = bf16[4,128,128]{2,1,0:T(8,128)(2,1)S(1)} collective-permute-done((bf16[4,128,128]{2,1,0:T(8,128)(2,1)S(1)}, bf16[4,128,128]{2,1,0:T(8,128)(2,1)S(1)}, u32[]{:S(2)}, u32[]{:S(2)}) %collective-permute-start.2) | collective-permute-done | bytes 131104 | tf_op jit(solution)/shard_map/cond/branch_0_fun/ppermute | solution.py:308
  17.8 1.7 %collective-permute-done.3.other_b = bf16[4,128,128]{2,1,0:T(8,128)(2,1)S(1)} collective-permute-done((bf16[4,128,128]{2,1,0:T(8,128)(2,1)S(1)}, bf16[4,128,128]{2,1,0:T(8,128)(2,1)S(1)}, u32[]{:S(2)}, u32[]{:S(2)}) %collective-permute-start.3) | collective-permute-done | bytes 131104 | tf_op jit(solution)/shard_map/cond/branch_0_fun/ppermute | solution.py:308
  19.5 11.3 %conditional.3 = ((f32[3,128,128]{2,1,0:T(8,128)}, f32[3,128,128]{2,1,0:T(8,128)}, f32[3,128,128]{2,1,0:T(8,128)})) conditional(s32[]{:T(128)} %bitcast.1, (s32[53]{0:T(128)S(4)}, f32[12,128,128]{2,1,0:T(8,128)S(1)}, f32[3,128,128]{2,1,0:T(8,128)S(1)}, f32[3,128,128]{2,1,0:T(8,128)S(1)}, f32[3,128,128]{2,1,0:T(8,128)S(1)}) %tuple.26, ...), branch_computations={%region_3.0_spmd, %region_4.0_spmd, %region_5.0_spmd} | conditional | bytes 1179776 | solution.py:421
  19.5 0.1 planes.4
  19.6 1.6 %collective-permute-start.15 = (bf16[2,128,128]{2,1,0:T(8,128)(2,1)S(1)}, bf16[2,128,128]{2,1,0:T(8,128)(2,1)S(1)}, u32[]{:S(2)}, u32[]{:S(2)}) collective-permute-start(bf16[2,128,128]{2,1,0:T(8,128)(2,1)S(1)} %get-tuple-element.106), channel_id=1, source_target_pairs={{0,8},{2,10},{4,12},{6,14},{8,0},{10,2},{12,4},{14,6},{16,24},{18,... | collective-permute-start | bytes 196616 | tf_op jit(solution)/shard_map/cond/branch_1_fun/ppermute | solution.py:308
  21.2 2.6 %collective-permute-start.16 = (bf16[2,128,128]{2,1,0:T(8,128)(2,1)S(1)}, bf16[2,128,128]{2,1,0:T(8,128)(2,1)S(1)}, u32[]{:S(2)}, u32[]{:S(2)}) collective-permute-start(bf16[2,128,128]{2,1,0:T(8,128)(2,1)S(1)} %get-tuple-element.107), channel_id=1, source_target_pairs={{0,16},{2,18},{4,20},{6,22},{8,24},{10,26},{12,28},{14,30},{16,0},... | collective-permute-start | bytes 196616 | tf_op jit(solution)/shard_map/cond/branch_1_fun/ppermute | solution.py:308
  23.8 0.2 collective-permute-start.17
  24.0 0.1 collective-permute-done.15.rest_0_
  24.1 3.7 %collective-permute-done.16.rest_1_ = bf16[2,128,128]{2,1,0:T(8,128)(2,1)S(1)} collective-permute-done((bf16[2,128,128]{2,1,0:T(8,128)(2,1)S(1)}, bf16[2,128,128]{2,1,0:T(8,128)(2,1)S(1)}, u32[]{:S(2)}, u32[]{:S(2)}) %collective-permute-start.16) | collective-permute-done | bytes 65568 | tf_op jit(solution)/shard_map/cond/branch_1_fun/ppermute | solution.py:308
  27.8 2.1 %collective-permute-done.17.rest_2_ = bf16[2,128,128]{2,1,0:T(8,128)(2,1)S(1)} collective-permute-done((bf16[2,128,128]{2,1,0:T(8,128)(2,1)S(1)}, bf16[2,128,128]{2,1,0:T(8,128)(2,1)S(1)}, u32[]{:S(2)}, u32[]{:S(2)}) %collective-permute-start.17) | collective-permute-done | bytes 65568 | tf_op jit(solution)/shard_map/cond/branch_1_fun/ppermute | solution.py:308
  29.9 0.9 %update.4 = (f32[3,128,128]{2,1,0:T(8,128)}, f32[3,128,128]{2,1,0:T(8,128)}, f32[3,128,128]{2,1,0:T(8,128)}) custom-call(s32[53]{0:T(128)S(4)} %get-tuple-element.103.place, f32[2,128,128]{2,1,0:T(8,128)S(1)} %get-tuple-element.105.kept, bf16[2,128,128]{2,1,0:T(8,128)(2,1)S(1)} %collective-permute-done.15.rest_0_, ...), custom_call_target="tpu_custom_call" | custom-call | tf_op jit(solution)/shard_map/cond/branch_1_fun/update/pallas_call | solution.py:406
  (3 shorter events, 0.1 us)
Async XLA Ops:
  0.6 4.6 %collective-permute-start.21 = (bf16[256,4096]{1,0:T(8,128)(2,1)}, bf16[256,4096]{1,0:T(8,128)(2,1)S(1)}, u32[]{:S(2)}, u32[]{:S(2)}) collective-permute-start(bf16[256,4096]{1,0:T(8,128)(2,1)} %features.1), channel_id=1, source_target_pairs={{0,1},{1,0},{2,3},{3,2},{4,5},{5,4},{6,7},{7,6},{8,9},{9,8},{10,11... | collective-permute-start | bytes 6291464 | tf_op jit(solution)/shard_map/ppermute | solution.py:313
  5.6 6.9 %collective-permute-start = (bf16[4,128,128]{2,1,0:T(8,128)(2,1)S(1)}, bf16[4,128,128]{2,1,0:T(8,128)(2,1)S(1)}, u32[]{:S(2)}, u32[]{:S(2)}) collective-permute-start(bf16[4,128,128]{2,1,0:T(8,128)(2,1)S(1)} %get-tuple-element.63), channel_id=1, source_target_pairs={{0,2},{2,0},{4,6},{6,4},{8,10},{10,8},{12,14},{14,12},{16,18},{18,... | collective-permute-start | bytes 393224 | tf_op jit(solution)/shard_map/cond/branch_0_fun/ppermute | solution.py:308
  8.5 5.9 %collective-permute-start.1 = (bf16[4,128,128]{2,1,0:T(8,128)(2,1)S(1)}, bf16[4,128,128]{2,1,0:T(8,128)(2,1)S(1)}, u32[]{:S(2)}, u32[]{:S(2)}) collective-permute-start(bf16[4,128,128]{2,1,0:T(8,128)(2,1)S(1)} %get-tuple-element.66), channel_id=1, source_target_pairs={{0,4},{2,6},{4,0},{6,2},{8,12},{10,14},{12,8},{14,10},{16,20},{18,... | collective-permute-start | bytes 393224 | tf_op jit(solution)/shard_map/cond/branch_0_fun/ppermute | solution.py:308
  12.5 5.2 %collective-permute-start.2 = (bf16[4,128,128]{2,1,0:T(8,128)(2,1)S(1)}, bf16[4,128,128]{2,1,0:T(8,128)(2,1)S(1)}, u32[]{:S(2)}, u32[]{:S(2)}) collective-permute-start(bf16[4,128,128]{2,1,0:T(8,128)(2,1)S(1)} %get-tuple-element.68), channel_id=1, source_target_pairs={{0,4},{2,6},{4,0},{6,2},{8,12},{10,14},{12,8},{14,10},{16,20},{18,... | collective-permute-start | bytes 393224 | tf_op jit(solution)/shard_map/cond/branch_0_fun/ppermute | solution.py:308
  14.4 5.0 %collective-permute-start.3 = (bf16[4,128,128]{2,1,0:T(8,128)(2,1)S(1)}, bf16[4,128,128]{2,1,0:T(8,128)(2,1)S(1)}, u32[]{:S(2)}, u32[]{:S(2)}) collective-permute-start(bf16[4,128,128]{2,1,0:T(8,128)(2,1)S(1)} %get-tuple-element.69), channel_id=1, source_target_pairs={{0,2},{2,0},{4,6},{6,4},{8,10},{10,8},{12,14},{14,12},{16,18},{18,... | collective-permute-start | bytes 393224 | tf_op jit(solution)/shard_map/cond/branch_0_fun/ppermute | solution.py:308
  19.6 4.5 %collective-permute-start.15 = (bf16[2,128,128]{2,1,0:T(8,128)(2,1)S(1)}, bf16[2,128,128]{2,1,0:T(8,128)(2,1)S(1)}, u32[]{:S(2)}, u32[]{:S(2)}) collective-permute-start(bf16[2,128,128]{2,1,0:T(8,128)(2,1)S(1)} %get-tuple-element.106), channel_id=1, source_target_pairs={{0,8},{2,10},{4,12},{6,14},{8,0},{10,2},{12,4},{14,6},{16,24},{18,... | collective-permute-start | bytes 196616 | tf_op jit(solution)/shard_map/cond/branch_1_fun/ppermute | solution.py:308
  21.2 6.6 %collective-permute-start.16 = (bf16[2,128,128]{2,1,0:T(8,128)(2,1)S(1)}, bf16[2,128,128]{2,1,0:T(8,128)(2,1)S(1)}, u32[]{:S(2)}, u32[]{:S(2)}) collective-permute-start(bf16[2,128,128]{2,1,0:T(8,128)(2,1)S(1)} %get-tuple-element.107), channel_id=1, source_target_pairs={{0,16},{2,18},{4,20},{6,22},{8,24},{10,26},{12,28},{14,30},{16,0},... | collective-permute-start | bytes 196616 | tf_op jit(solution)/shard_map/cond/branch_1_fun/ppermute | solution.py:308
  23.8 6.1 %collective-permute-start.17 = (bf16[2,128,128]{2,1,0:T(8,128)(2,1)S(1)}, bf16[2,128,128]{2,1,0:T(8,128)(2,1)S(1)}, u32[]{:S(2)}, u32[]{:S(2)}) collective-permute-start(bf16[2,128,128]{2,1,0:T(8,128)(2,1)S(1)} %get-tuple-element.108), channel_id=1, source_target_pairs={{0,24},{2,26},{4,28},{6,30},{8,16},{10,18},{12,20},{14,22},{16,8},... | collective-permute-start | bytes 196616 | tf_op jit(solution)/shard_map/cond/branch_1_fun/ppermute | solution.py:308

commit v7 on v6

--- a/solution.py
+++ b/solution.py
@@ -23,13 +23,17 @@
 def bin_sizes(listed, replicas, capacity):
     crowd = min(listed, capacity * replicas // COLUMNS)
     level, most = -(-listed // COLUMNS), max(-(-listed // 3), -(-crowd // 2))
-    return sorted({min(level, most), min(level + max(listed // 16, 1), most), most})
+    step = max(listed // 16, 1)
+    whole = [(n, n) for n in sorted({min(level, most), min(level + step, most), most})]
+    small = (whole[0][0], whole[0][0] - step)
+    return [small] * (0 < 2 * small[1] <= most) + whole
 
 
 def route(blk, own, place, flag, depth, seen, work, *, capacity, sizes):
     listed = own.shape[0]
-    most = sizes[-1]
+    most = sizes[-1][0]
     cells = 4 * most + listed
+    starts = place.shape[0] - 5
     replicas = seen.shape[0]
     me = lax.axis_index("dp")
     column = lax.rem(me, COLUMNS)
@@ -59,21 +63,23 @@
         a3 = jnp.minimum(n[3], size - a1)
         return a0, a1, a2, a3
 
-    def search(size):
+    def search(size, part):
         low = jnp.maximum(n[0] - size, 0)
         high = jnp.minimum(n[0], size)
 
         def attempt(i, best):
             a = shares(size, low + i)
             ok = (low + i <= high) & (a[1] <= size) & (n[2] - a[2] + n[3] - a[3] <= size)
+            for q in range(COLUMNS):
+                ok = ok & (jnp.maximum(a[q], n[q] - a[q]) <= part)
             return jnp.where(ok, low + i, best)
 
         return lax.fori_loop(0, size + 1, attempt, jnp.int32(-1))
 
     def settle(i):
-        best = search(sizes[i])
+        best = search(*sizes[i])
         flag[0] = i
-        work[LOAD + 1] = sizes[i]
+        work[LOAD + 1] = sizes[i][0]
         work[LOAD] = best
         if i + 1 < len(sizes):
             pl.when(best < 0)(lambda: settle(i + 1))
@@ -85,6 +91,14 @@
     for q, (at_a, at_b) in enumerate(((0, 0), (0, n[0] - a[0]), (a[0], 0), (a[1], n[2] - a[2]))):
         work[AT_A + q] = at_a
         work[AT_B + q] = at_b
+
+    lo, hi = my_bit
+    first_a = jnp.where(lo == 0, a[0], a[1])
+    first_b = jnp.where(hi == 0, n[0] - a[0], n[2] - a[2])
+    place[starts] = jnp.where(hi == 0, first_a, 0)
+    place[starts + 1] = jnp.where(hi == 0, 0, first_a)
+    place[starts + 2] = jnp.where(lo == 0, first_b, 0)
+    place[starts + 3] = jnp.where(lo == 0, 0, first_b)
 
     def clear_place(j, carry):
         place[cells + j] = 0
@@ -225,16 +239,28 @@
         lax.fori_loop(0, out.shape[0], compute, 0, unroll=min(out.shape[0], 8))
 
 
-def add_kernel(part, got, total, send):
+def add_kernel(place, part, got, total, send, *, bin):
+    slots = total.shape[0]
     total[...] = part[...] + got[...].astype(total.dtype)
-    send[...] = total[...].astype(send.dtype)
-
-
-def total_kernel(sum_a, sum_b, other_a, other_b, total):
+    if send.shape[0] == slots:
+        send[...] = total[...].astype(send.dtype)
+    else:
+        start = place[place.shape[0] - 5 + 2 * bin]
+        for j in range(send.shape[0]):
+            send[j] = total[jnp.minimum(start + j, slots - 1)].astype(send.dtype)
+
+
+def total_kernel(place, sum_a, sum_b, other_a, other_b, total):
     slots = sum_a.shape[0]
-    most = total.shape[0] // 2
-    total[:slots] = sum_a[...] + other_a[...].astype(total.dtype)
-    total[most : most + slots] = sum_b[...] + other_b[...].astype(total.dtype)
+    for bin, (own, other) in enumerate(((sum_a, other_a), (sum_b, other_b))):
+        at = bin * (total.shape[0] // 2)
+        if other.shape[0] == slots:
+            total[at : at + slots] = own[...] + other[...].astype(total.dtype)
+        else:
+            start = place[place.shape[0] - 4 + 2 * bin]
+            for j in range(other.shape[0]):
+                kept = own[jnp.minimum(start + j, slots - 1)]
+                total[at + start + j] = kept + other[j].astype(total.dtype)
 
 
 def plane_kernel(place, total, *outs, cells, capacity):
@@ -318,7 +344,7 @@
         out_shape=(
             pltpu.VMEM((listed, tokens, size), bf16),
             pltpu.VMEM((listed, tokens, size), bf16),
-            pltpu.SMEM((4 * sizes[-1] + listed + planes * capacity + 1,), jnp.int32),
+            pltpu.SMEM((4 * sizes[-1][0] + listed + planes * capacity + 5,), jnp.int32),
             pltpu.SMEM((1,), jnp.int32),
             pltpu.SMEM((1,), jnp.int32),
         )
@@ -339,10 +365,10 @@
     )(*map(stay, (blocks.T, owner, features, gate_pre, up_pre, grad_hidden, weights, moment1, moment2)))
     direct = planes <= 4 and planes & (planes - 1) == 0
 
-    def plane_sums(slots):
+    def plane_sums(slots, some):
         def products(dtype, *bins):
             return pl.pallas_call(
-                functools.partial(product_kernel, shards=shards, most=sizes[-1], bins=bins),
+                functools.partial(product_kernel, shards=shards, most=sizes[-1][0], bins=bins),
                 out_shape=(in_vmem(slots, dtype),) * len(bins),
                 in_specs=[SMEM] + [VMEM] * (shards + 1),
                 out_specs=(VMEM,) * len(bins),
@@ -352,43 +378,43 @@
                 name="products",
             )(place, act, rows, *others)
 
-        def add(part, got):
+        def add(part, got, bin):
             return pl.pallas_call(
-                add_kernel,
-                out_shape=(in_vmem(slots, f32), in_vmem(slots, bf16)),
-                in_specs=[VMEM, VMEM],
+                functools.partial(add_kernel, bin=bin),
+                out_shape=(in_vmem(slots, f32), in_vmem(some, bf16)),
+                in_specs=[SMEM, VMEM, VMEM],
                 out_specs=(VMEM, VMEM),
                 compiler_params=grant(12 * slots * block),
                 name="sums",
-            )(part, got)
+            )(place, part, got)
 
         send_b, send_a = products(bf16, 2, 0)
         got_b = swap(send_b, 2)
         got_a = swap(send_a, 1)
         kept_b, kept_a = products(f32, 3, 1)
-        sum_b, send_b = add(kept_b, got_b)
-        sum_a, send_a = add(kept_a, got_a)
+        sum_b, send_b = add(kept_b, got_b, 1)
+        sum_a, send_a = add(kept_a, got_a, 0)
         other_b = swap(send_b, 1)
         other_a = swap(send_a, 2)
         return pl.pallas_call(
             total_kernel,
-            out_shape=in_vmem(2 * sizes[-1], f32),
-            in_specs=[VMEM] * 4,
+            out_shape=in_vmem(2 * sizes[-1][0], f32),
+            in_specs=[SMEM] + [VMEM] * 4,
             out_specs=VMEM,
-            compiler_params=grant((12 * slots + 8 * sizes[-1]) * block),
+            compiler_params=grant((12 * slots + 8 * sizes[-1][0]) * block),
             name="totals",
-        )(sum_a, sum_b, other_a, other_b)
-
-    total = lax.switch(flag[0], [functools.partial(plane_sums, n) for n in sizes])
+        )(place, sum_a, sum_b, other_a, other_b)
+
+    total = lax.switch(flag[0], [functools.partial(plane_sums, *n) for n in sizes])
 
     def finish(slots):
         outs = (slots,) * (planes - 1) if direct else (planes * capacity,)
         kept, *sends = pl.pallas_call(
-            functools.partial(plane_kernel, cells=4 * sizes[-1] + listed, capacity=capacity),
+            functools.partial(plane_kernel, cells=4 * sizes[-1][0] + listed, capacity=capacity),
             out_shape=(in_vmem(slots, f32),) + tuple(in_vmem(n, bf16) for n in outs),
             in_specs=[SMEM, VMEM],
             out_specs=(VMEM,) * (1 + len(outs)),
-            compiler_params=grant((8 * sizes[-1] + 4 * slots + 2 * sum(outs)) * block),
+            compiler_params=grant((8 * sizes[-1][0] + 4 * slots + 2 * sum(outs)) * block),
             name="planes",
         )(place, total)
         if direct:

time: 31 us -> 30.6 us (0.987)
  waiting for transfers between devices: 11.6 us -> 11.2 us
    ppermute x7, waiting for transfers between devices: 11.4 us -> 11.1 us  [local(): lax.ppermute(v, 'dp', [(i, i ^ bit) for i in range(replicas)])]
where the time goes in v7:
time: 30.6 us; the launch traced here: 30.5 us
  starting transfers between devices  12.8 us (42%)
  waiting for transfers between devices  11.2 us (37%)
  Pallas kernels  5.66 us (18%)
  between operations  0.66 us (2%)
    ppermute x7, starting transfers between devices, local(): lax.ppermute(v, 'dp', [(i, i ^ bit) for i in range(replicas)])  12.3 us
    ppermute x7, waiting for transfers between devices, local(): lax.ppermute(v, 'dp', [(i, i ^ bit) for i in range(replicas)])  11.1 us
    pallas_call x1, Pallas kernels, local(): pl.pallas_call(functools.partial(act_kernel, capacity=capacity, sizes=siz...  3.82 us
    pallas_call x1, Pallas kernels, finish(): pl.pallas_call(functools.partial(update_kernel, count=len(parts)), out_sh...  0.9 us
    pallas_call x2, Pallas kernels, products(): pl.pallas_call(functools.partial(product_kernel, shards=shards, most=size...  0.77 us
  transfers between devices with their start and end apart: 8, of which 7 were waited for; matrix products, arithmetic and copies ran while one was open for 0% of the time, Pallas kernels for 14%

profile of v7, /device:TPU:0, one launch (start us, length us, event | category | flops | bytes accessed | tf_op | source)
XLA Modules:
  0.0 30.5 jit_solution(9996647799582583839)
XLA Ops:
  0.6 0.6 %collective-permute-start.25 = (bf16[256,4096]{1,0:T(8,128)(2,1)}, bf16[256,4096]{1,0:T(8,128)(2,1)S(1)}, u32[]{:S(2)}, u32[]{:S(2)}) collective-permute-start(bf16[256,4096]{1,0:T(8,128)(2,1)} %features.1), channel_id=1, source_target_pairs={{0,1},{1,0},{2,3},{3,2},{4,5},{5,4},{6,7},{7,6},{8,9},{9,8},{10,11... | collective-permute-start | bytes 6291464 | tf_op jit(solution)/shard_map/ppermute | solution.py:339
  1.2 3.8 %activations.1 = (bf16[16,256,128]{2,1,0:T(8,128)(2,1)S(1)}, bf16[16,256,128]{2,1,0:T(8,128)(2,1)S(1)}, s32[57]{0:T(128)S(4)}, s32[1]{0:T(128)S(4)}, s32[1]{0:T(...) custom-call(s32[3,16]{1,0:T(4,128)} %bitcast.3, s32[16]{0:T(128)} %own_hbm.1, ...), custom_call_target="tpu_custom_call" | custom-call | tf_op jit(solution)/shard_map/activations/pallas_call | solution.py:342
  5.0 0.2 collective-permute-done.25
  5.2 14.0 %conditional.2 = (f32[12,128,128]{2,1,0:T(8,128)S(1)}) conditional(s32[]{:T(128)} %bitcast.2, (s32[57]{0:T(128)S(4)}, bf16[16,256,128]{2,1,0:T(8,128)(2,1)S(1)}, bf16[16,256,128]{2,1,0:T(8,128)(2,1)S(1)}, bf16[256,4096]{1,0:T(8,128)(2,1)S(1)}) %tuple.28, (s32[57]{0:T(128)S(4)}, bf16[16,256,128]{2,1,0:T(8,128)(2,1)S(1)}, ...), branch_computations={%region_0.0_spmd, %region_1.0_spmd, %region_2.0_spmd, %region_3.0_... | conditional | bytes 3145896 | solution.py:408
  5.2 0.4 %products.9 = (bf16[4,128,128]{2,1,0:T(8,128)(2,1)S(1)}, bf16[4,128,128]{2,1,0:T(8,128)(2,1)S(1)}) custom-call(s32[57]{0:T(128)S(4)} %get-tuple-element.62.place, bf16[16,256,128]{2,1,0:T(8,128)(2,1)S(1)} %get-tuple-element.63.act, bf16[16,256,128]{2,1,0:T(8,128)(2,1)S(1)} %get-tuple-element.64.rows, bf16[256,4096]{1,0:T(8,128)(2,1)S(1)} %get-tuple-element.70.rest_0_), custom_call_target="tpu_custom_call" | custom-call | tf_op jit(solution)/shard_map/cond/branch_0_fun/products/pallas_call | solution.py:370
  5.6 2.9 %collective-permute-start = (bf16[4,128,128]{2,1,0:T(8,128)(2,1)S(1)}, bf16[4,128,128]{2,1,0:T(8,128)(2,1)S(1)}, u32[]{:S(2)}, u32[]{:S(2)}) collective-permute-start(bf16[4,128,128]{2,1,0:T(8,128)(2,1)S(1)} %get-tuple-element.72), channel_id=1, source_target_pairs={{0,2},{2,0},{4,6},{6,4},{8,10},{10,8},{12,14},{14,12},{16,18},{18,... | collective-permute-start | bytes 393224 | tf_op jit(solution)/shard_map/cond/branch_0_fun/ppermute | solution.py:334
  8.5 1.5 %collective-permute-start.1 = (bf16[4,128,128]{2,1,0:T(8,128)(2,1)S(1)}, bf16[4,128,128]{2,1,0:T(8,128)(2,1)S(1)}, u32[]{:S(2)}, u32[]{:S(2)}) collective-permute-start(bf16[4,128,128]{2,1,0:T(8,128)(2,1)S(1)} %get-tuple-element.75), channel_id=1, source_target_pairs={{0,4},{2,6},{4,0},{6,2},{8,12},{10,14},{12,8},{14,10},{16,20},{18,... | collective-permute-start | bytes 393224 | tf_op jit(solution)/shard_map/cond/branch_0_fun/ppermute | solution.py:334
  10.0 0.4 %products.8 = (f32[4,128,128]{2,1,0:T(8,128)S(1)}, f32[4,128,128]{2,1,0:T(8,128)S(1)}) custom-call(s32[57]{0:T(128)S(4)} %get-tuple-element.62.place, bf16[16,256,128]{2,1,0:T(8,128)(2,1)S(1)} %get-tuple-element.63.act, bf16[16,256,128]{2,1,0:T(8,128)(2,1)S(1)} %get-tuple-element.64.rows, bf16[256,4096]{1,0:T(8,128)(2,1)S(1)} %get-tuple-element.70.rest_0_), custom_call_target="tpu_custom_call" | custom-call | tf_op jit(solution)/shard_map/cond/branch_0_fun/products/pallas_call | solution.py:370
  10.4 2.1 %collective-permute-done.got = bf16[4,128,128]{2,1,0:T(8,128)(2,1)S(1)} collective-permute-done((bf16[4,128,128]{2,1,0:T(8,128)(2,1)S(1)}, bf16[4,128,128]{2,1,0:T(8,128)(2,1)S(1)}, u32[]{:S(2)}, u32[]{:S(2)}) %collective-permute-start) | collective-permute-done | bytes 131104 | tf_op jit(solution)/shard_map/cond/branch_0_fun/ppermute | solution.py:334
  12.6 1.8 %collective-permute-start.2 = (bf16[3,128,128]{2,1,0:T(8,128)(2,1)S(1)}, bf16[3,128,128]{2,1,0:T(8,128)(2,1)S(1)}, u32[]{:S(2)}, u32[]{:S(2)}) collective-permute-start(bf16[3,128,128]{2,1,0:T(8,128)(2,1)S(1)} %get-tuple-element.77), channel_id=1, source_target_pairs={{0,4},{2,6},{4,0},{6,2},{8,12},{10,14},{12,8},{14,10},{16,20},{18,... | collective-permute-start | bytes 294920 | tf_op jit(solution)/shard_map/cond/branch_0_fun/ppermute | solution.py:334
  14.4 0.0 collective-permute-done.1.got
  14.4 1.6 %collective-permute-start.3 = (bf16[3,128,128]{2,1,0:T(8,128)(2,1)S(1)}, bf16[3,128,128]{2,1,0:T(8,128)(2,1)S(1)}, u32[]{:S(2)}, u32[]{:S(2)}) collective-permute-start(bf16[3,128,128]{2,1,0:T(8,128)(2,1)S(1)} %get-tuple-element.78), channel_id=1, source_target_pairs={{0,2},{2,0},{4,6},{6,4},{8,10},{10,8},{12,14},{14,12},{16,18},{18,... | collective-permute-start | bytes 294920 | tf_op jit(solution)/shard_map/cond/branch_0_fun/ppermute | solution.py:334
  16.0 1.5 %collective-permute-done.2.other_a = bf16[3,128,128]{2,1,0:T(8,128)(2,1)S(1)} collective-permute-done((bf16[3,128,128]{2,1,0:T(8,128)(2,1)S(1)}, bf16[3,128,128]{2,1,0:T(8,128)(2,1)S(1)}, u32[]{:S(2)}, u32[]{:S(2)}) %collective-permute-start.2) | collective-permute-done | bytes 98336 | tf_op jit(solution)/shard_map/cond/branch_0_fun/ppermute | solution.py:334
  17.4 1.7 %collective-permute-done.3.other_b = bf16[3,128,128]{2,1,0:T(8,128)(2,1)S(1)} collective-permute-done((bf16[3,128,128]{2,1,0:T(8,128)(2,1)S(1)}, bf16[3,128,128]{2,1,0:T(8,128)(2,1)S(1)}, u32[]{:S(2)}, u32[]{:S(2)}) %collective-permute-start.3) | collective-permute-done | bytes 98336 | tf_op jit(solution)/shard_map/cond/branch_0_fun/ppermute | solution.py:334
  19.2 11.3 %conditional.3 = ((f32[3,128,128]{2,1,0:T(8,128)}, f32[3,128,128]{2,1,0:T(8,128)}, f32[3,128,128]{2,1,0:T(8,128)})) conditional(s32[]{:T(128)} %bitcast.1, (s32[57]{0:T(128)S(4)}, f32[12,128,128]{2,1,0:T(8,128)S(1)}, f32[3,128,128]{2,1,0:T(8,128)S(1)}, f32[3,128,128]{2,1,0:T(8,128)S(1)}, f32[3,128,128]{2,1,0:T(8,128)S(1)}) %tuple.29, ...), branch_computations={%region_4.0_spmd, %region_5.0_spmd, %region_6.0_spmd} | conditional | bytes 1179776 | solution.py:447
  19.2 0.1 planes.4
  19.3 1.6 %collective-permute-start.19 = (bf16[2,128,128]{2,1,0:T(8,128)(2,1)S(1)}, bf16[2,128,128]{2,1,0:T(8,128)(2,1)S(1)}, u32[]{:S(2)}, u32[]{:S(2)}) collective-permute-start(bf16[2,128,128]{2,1,0:T(8,128)(2,1)S(1)} %get-tuple-element.127), channel_id=1, source_target_pairs={{0,8},{2,10},{4,12},{6,14},{8,0},{10,2},{12,4},{14,6},{16,24},{18,... | collective-permute-start | bytes 196616 | tf_op jit(solution)/shard_map/cond/branch_1_fun/ppermute | solution.py:334
  20.9 2.6 %collective-permute-start.20 = (bf16[2,128,128]{2,1,0:T(8,128)(2,1)S(1)}, bf16[2,128,128]{2,1,0:T(8,128)(2,1)S(1)}, u32[]{:S(2)}, u32[]{:S(2)}) collective-permute-start(bf16[2,128,128]{2,1,0:T(8,128)(2,1)S(1)} %get-tuple-element.128), channel_id=1, source_target_pairs={{0,16},{2,18},{4,20},{6,22},{8,24},{10,26},{12,28},{14,30},{16,0},... | collective-permute-start | bytes 196616 | tf_op jit(solution)/shard_map/cond/branch_1_fun/ppermute | solution.py:334
  23.5 0.2 collective-permute-start.21
  23.7 0.2 collective-permute-done.19.rest_0_
  23.9 3.5 %collective-permute-done.20.rest_1_ = bf16[2,128,128]{2,1,0:T(8,128)(2,1)S(1)} collective-permute-done((bf16[2,128,128]{2,1,0:T(8,128)(2,1)S(1)}, bf16[2,128,128]{2,1,0:T(8,128)(2,1)S(1)}, u32[]{:S(2)}, u32[]{:S(2)}) %collective-permute-start.20) | collective-permute-done | bytes 65568 | tf_op jit(solution)/shard_map/cond/branch_1_fun/ppermute | solution.py:334
  27.5 2.1 %collective-permute-done.21.rest_2_ = bf16[2,128,128]{2,1,0:T(8,128)(2,1)S(1)} collective-permute-done((bf16[2,128,128]{2,1,0:T(8,128)(2,1)S(1)}, bf16[2,128,128]{2,1,0:T(8,128)(2,1)S(1)}, u32[]{:S(2)}, u32[]{:S(2)}) %collective-permute-start.21) | collective-permute-done | bytes 65568 | tf_op jit(solution)/shard_map/cond/branch_1_fun/ppermute | solution.py:334
  29.6 0.9 %update.4 = (f32[3,128,128]{2,1,0:T(8,128)}, f32[3,128,128]{2,1,0:T(8,128)}, f32[3,128,128]{2,1,0:T(8,128)}) custom-call(s32[57]{0:T(128)S(4)} %get-tuple-element.124.place, f32[2,128,128]{2,1,0:T(8,128)S(1)} %get-tuple-element.126.kept, bf16[2,128,128]{2,1,0:T(8,128)(2,1)S(1)} %collective-permute-done.19.rest_0_, ...), custom_call_target="tpu_custom_call" | custom-call | tf_op jit(solution)/shard_map/cond/branch_1_fun/update/pallas_call | solution.py:432
  (3 shorter events, 0.1 us)
Async XLA Ops:
  0.6 4.6 %collective-permute-start.25 = (bf16[256,4096]{1,0:T(8,128)(2,1)}, bf16[256,4096]{1,0:T(8,128)(2,1)S(1)}, u32[]{:S(2)}, u32[]{:S(2)}) collective-permute-start(bf16[256,4096]{1,0:T(8,128)(2,1)} %features.1), channel_id=1, source_target_pairs={{0,1},{1,0},{2,3},{3,2},{4,5},{5,4},{6,7},{7,6},{8,9},{9,8},{10,11... | collective-permute-start | bytes 6291464 | tf_op jit(solution)/shard_map/ppermute | solution.py:339
  5.6 6.9 %collective-permute-start = (bf16[4,128,128]{2,1,0:T(8,128)(2,1)S(1)}, bf16[4,128,128]{2,1,0:T(8,128)(2,1)S(1)}, u32[]{:S(2)}, u32[]{:S(2)}) collective-permute-start(bf16[4,128,128]{2,1,0:T(8,128)(2,1)S(1)} %get-tuple-element.72), channel_id=1, source_target_pairs={{0,2},{2,0},{4,6},{6,4},{8,10},{10,8},{12,14},{14,12},{16,18},{18,... | collective-permute-start | bytes 393224 | tf_op jit(solution)/shard_map/cond/branch_0_fun/ppermute | solution.py:334
  8.5 5.9 %collective-permute-start.1 = (bf16[4,128,128]{2,1,0:T(8,128)(2,1)S(1)}, bf16[4,128,128]{2,1,0:T(8,128)(2,1)S(1)}, u32[]{:S(2)}, u32[]{:S(2)}) collective-permute-start(bf16[4,128,128]{2,1,0:T(8,128)(2,1)S(1)} %get-tuple-element.75), channel_id=1, source_target_pairs={{0,4},{2,6},{4,0},{6,2},{8,12},{10,14},{12,8},{14,10},{16,20},{18,... | collective-permute-start | bytes 393224 | tf_op jit(solution)/shard_map/cond/branch_0_fun/ppermute | solution.py:334
  12.6 4.9 %collective-permute-start.2 = (bf16[3,128,128]{2,1,0:T(8,128)(2,1)S(1)}, bf16[3,128,128]{2,1,0:T(8,128)(2,1)S(1)}, u32[]{:S(2)}, u32[]{:S(2)}) collective-permute-start(bf16[3,128,128]{2,1,0:T(8,128)(2,1)S(1)} %get-tuple-element.77), channel_id=1, source_target_pairs={{0,4},{2,6},{4,0},{6,2},{8,12},{10,14},{12,8},{14,10},{16,20},{18,... | collective-permute-start | bytes 294920 | tf_op jit(solution)/shard_map/cond/branch_0_fun/ppermute | solution.py:334
  14.4 4.7 %collective-permute-start.3 = (bf16[3,128,128]{2,1,0:T(8,128)(2,1)S(1)}, bf16[3,128,128]{2,1,0:T(8,128)(2,1)S(1)}, u32[]{:S(2)}, u32[]{:S(2)}) collective-permute-start(bf16[3,128,128]{2,1,0:T(8,128)(2,1)S(1)} %get-tuple-element.78), channel_id=1, source_target_pairs={{0,2},{2,0},{4,6},{6,4},{8,10},{10,8},{12,14},{14,12},{16,18},{18,... | collective-permute-start | bytes 294920 | tf_op jit(solution)/shard_map/cond/branch_0_fun/ppermute | solution.py:334
  19.3 4.7 %collective-permute-start.19 = (bf16[2,128,128]{2,1,0:T(8,128)(2,1)S(1)}, bf16[2,128,128]{2,1,0:T(8,128)(2,1)S(1)}, u32[]{:S(2)}, u32[]{:S(2)}) collective-permute-start(bf16[2,128,128]{2,1,0:T(8,128)(2,1)S(1)} %get-tuple-element.127), channel_id=1, source_target_pairs={{0,8},{2,10},{4,12},{6,14},{8,0},{10,2},{12,4},{14,6},{16,24},{18,... | collective-permute-start | bytes 196616 | tf_op jit(solution)/shard_map/cond/branch_1_fun/ppermute | solution.py:334
  20.9 6.6 %collective-permute-start.20 = (bf16[2,128,128]{2,1,0:T(8,128)(2,1)S(1)}, bf16[2,128,128]{2,1,0:T(8,128)(2,1)S(1)}, u32[]{:S(2)}, u32[]{:S(2)}) collective-permute-start(bf16[2,128,128]{2,1,0:T(8,128)(2,1)S(1)} %get-tuple-element.128), channel_id=1, source_target_pairs={{0,16},{2,18},{4,20},{6,22},{8,24},{10,26},{12,28},{14,30},{16,0},... | collective-permute-start | bytes 196616 | tf_op jit(solution)/shard_map/cond/branch_1_fun/ppermute | solution.py:334
  23.5 6.1 %collective-permute-start.21 = (bf16[2,128,128]{2,1,0:T(8,128)(2,1)S(1)}, bf16[2,128,128]{2,1,0:T(8,128)(2,1)S(1)}, u32[]{:S(2)}, u32[]{:S(2)}) collective-permute-start(bf16[2,128,128]{2,1,0:T(8,128)(2,1)S(1)} %get-tuple-element.129), channel_id=1, source_target_pairs={{0,24},{2,26},{4,28},{6,30},{8,16},{10,18},{12,20},{14,22},{16,8},... | collective-permute-start | bytes 196616 | tf_op jit(solution)/shard_map/cond/branch_1_fun/ppermute | solution.py:334
